TPU v7x, 32 devices: a whole 2x2x4 slice. The times are simulated.
32 devices in a mesh: grp: 2 (over x), seq: 8 (over z, y), ch: 2 (over core).
Axes of the slice: x: 2, y: 2, z: 4, core: 2. Of those that a mesh axis runs over, the one named last changes fastest.
Arguments:
- tokens: bfloat16 [16, 1024, 2048], P(('grp', 'seq'), None, 'ch'), parts along dimension 0, may hold values from -6 to 6
- short_weight: float32 [3, 2048], P(None, 'ch'), may hold values from -3 to 3
- inner_factor: bfloat16 [1024, 1024], P('seq'), may hold values from -0.1875 to 0.1875
- outer_factor: float32 [8, 8], replicated, may hold values from -2 to 2
- twiddle: float32 [8, 1024], P(None, 'seq'), may hold values from 0.5 to 1.5
- kernel: bfloat16 [8, 1024, 2048], P(None, 'seq', 'ch'), may hold values from -6 to 6
- cotangent: bfloat16 [16, 1024, 2048], P(('grp', 'seq'), None, 'ch'), parts along dimension 0, may hold values from -6 to 6
Outputs:
- mixer_out: bfloat16 [16, 1024, 2048], P(('grp', 'seq'), None, 'ch'), parts along dimension 0
- token_grad: bfloat16 [16, 1024, 2048], P(('grp', 'seq'), None, 'ch'), parts along dimension 0
- kernel_grad: bfloat16 [16, 1024, 2048], P('grp', 'seq', 'ch'), parts along dimension 0
There are 2 independent parts, one for each index of `grp`. A program takes and returns all parts, laid end to end along the dimension named above; an argument that names none is the same for every part. Nothing has to cross between parts.
All inputs are finite; a program needn't handle non-finite values.
Results may differ from a plain program's by a relative error of at most 0.0064.
Values may be sent and summed in bfloat16 or wider, within the bound.
No kernel may reach another device: no remote copies, remote signals or barrier semaphores. Data moves between devices by JAX's collectives and lax.ppermute only.
A program may use at most 128 MiB of HBM per device.

v0:
```python
import functools

import jax
import jax.numpy as jnp
from jax import lax
from jax.experimental import pallas as pl
from jax.experimental.pallas import tpu as pltpu
from jax.sharding import PartitionSpec as P

BF16, F32 = jnp.bfloat16, jnp.float32
VMEM_LIMIT = 48 * 1024 * 1024


def hop(block, distance):
    peers = lax.axis_size("seq")
    return lax.ppermute(block, "seq", [(i, (i + distance) % peers) for i in range(peers)])


def shifted(block, distance):
    devices = range(lax.axis_size("seq"))
    return lax.ppermute(block, "seq", [(i - distance, i) for i in devices if i - distance in devices])


def swap_cores(block):
    return lax.ppermute(block, "ch", [(0, 1), (1, 0)])


def call(body, name, grid, in_specs, out_specs, out_shape, flops, moved, scalars=0, transcendentals=0):
    return pl.pallas_call(
        body,
        name=name,
        grid_spec=pltpu.PrefetchScalarGridSpec(
            num_scalar_prefetch=scalars, grid=grid, in_specs=in_specs, out_specs=out_specs
        ),
        out_shape=out_shape,
        compiler_params=pltpu.CompilerParams(vmem_limit_bytes=VMEM_LIMIT),
        cost_estimate=pl.CostEstimate(flops=flops, bytes_accessed=moved, transcendentals=transcendentals),
    )


def whole(shape):
    return pl.BlockSpec(shape, lambda c, *_: (0,) * len(shape))


def tile(rows, width):
    return pl.BlockSpec((rows, width), lambda c, *_: (0, c))


def struct(shape, dtype):
    return jax.ShapeDtypeStruct(shape, dtype)


def matmul(left, right):
    return jnp.dot(left, right, preferred_element_type=F32)


def gate_body(tokens, halo, weight, cot, gated, gate, scaled):
    x = tokens[...].astype(F32)
    row = lax.broadcasted_iota(jnp.int32, x.shape, 0)
    edge = halo[...].astype(F32)
    one_back = jnp.where(row == 0, edge[1:2], pltpu.roll(x, 1, 0))
    two_back = jnp.where(row == 0, edge[0:1], jnp.where(row == 1, edge[1:2], pltpu.roll(x, 2, 0)))
    taps = weight[...]
    conv = taps[0:1] * x + taps[1:2] * one_back + taps[2:3] * two_back
    sig = jax.nn.sigmoid(conv)
    value = conv * sig
    slope = sig * (1.0 + conv * (1.0 - sig))
    wide = cot[...].astype(F32)
    gated[...] = (wide * value).astype(BF16)
    gate[...] = value
    scaled[...] = wide * slope


def gate_call(tokens, halo, weight, cot):
    length, channels = tokens.shape
    width = min(channels, 128)
    return call(
        gate_body,
        "gate",
        (channels // width,),
        [tile(length, width), tile(2, width), tile(3, width), tile(length, width)],
        [tile(length, width)] * 3,
        [struct((length, channels), BF16), struct((length, channels), F32), struct((length, channels), F32)],
        20 * length * channels,
        14 * length * channels,
        transcendentals=2 * length * channels,
    )(tokens, halo, weight, cot)


def spread_first_body(peers, core, own, *refs):
    mine, other = refs[: peers - 1], refs[peers - 1 : 2 * peers - 2]
    values, joined, pieces = refs[2 * peers - 2], refs[2 * peers - 1], refs[2 * peers :]
    share = own.shape[0]
    half = share // 2

    @pl.when(pl.program_id(0) == 0)
    def _():
        joined[0:share] = own[...]

        @pl.when(core[0] == 0)
        def _():
            for k in range(1, peers):
                joined[k * share : k * share + half] = mine[k - 1][...]
                joined[k * share + half : (k + 1) * share] = other[k - 1][...]

        @pl.when(core[0] != 0)
        def _():
            for k in range(1, peers):
                joined[k * share : k * share + half] = other[k - 1][...]
                joined[k * share + half : (k + 1) * share] = mine[k - 1][...]

    spread_pieces(joined, values, pieces)


def spread_pieces(joined, values, pieces):
    share = pieces[0].shape[0]
    product = matmul(joined[...], values[...]).astype(BF16)
    for k, piece in enumerate(pieces):
        piece[...] = product[k * share : (k + 1) * share]


def spread_body(joined, values, *pieces):
    spread_pieces(joined, values, pieces)


def spread_first_call(core, own, mine, other, values):
    share, block = own.shape
    channels = values.shape[1]
    peers = len(mine) + 1
    width = min(channels, 256)
    halves = [whole((share // 2, block))] * (2 * peers - 2)
    out = call(
        functools.partial(spread_first_body, peers),
        "spread_first",
        (channels // width,),
        [whole((share, block))] + halves + [tile(block, width)],
        [whole((peers * share, block))] + [tile(share, width)] * peers,
        [struct((peers * share, block), BF16)] + [struct((share, channels), BF16)] * peers,
        2 * block * block * channels,
        4 * block * channels + 4 * block * block,
        scalars=1,
    )(core, own, *mine, *other, values)
    return out[0], list(out[1:])


def spread_call(joined, values, peers):
    block, channels = values.shape
    share = block // peers
    width = min(channels, 256)
    return list(
        call(
            spread_body,
            "spread",
            (channels // width,),
            [whole((block, block)), tile(block, width)],
            [tile(share, width)] * peers,
            [struct((share, channels), BF16)] * peers,
            2 * block * block * channels,
            4 * block * channels + 2 * block * block,
        )(joined, values)
    )


def turn_body(joined, turned):
    turned[...] = joined[...].T


def turn_call(joined):
    block = joined.shape[0]
    width = min(block, 256)
    return call(
        turn_body,
        "turn",
        (block // width,),
        [tile(block, width)],
        pl.BlockSpec((width, block), lambda c: (c, 0)),
        struct((block, block), BF16),
        block * block,
        4 * block * block,
    )(joined)


def two_part(values):
    high = values.astype(BF16)
    return high, (values - high.astype(F32)).astype(BF16)


def middle_body(peers, span, with_grad, place, high, low, high_t, low_t, kern, *refs):
    pieces, refs = refs[:peers], refs[peers:]
    if with_grad:
        first, refs = refs[:peers], refs[peers:]
        grad, refs = refs[0], refs[1:]
    outs = refs[:peers]
    columns = pieces[0].shape[0]
    rows = [lax.rem(place[0] + r, peers) for r in range(peers)]
    for g in range(columns // span):
        part = slice(g * span, (g + 1) * span)
        stacked = jnp.concatenate([piece[part] for piece in pieces], axis=0)
        mid = matmul(high[g], stacked) + matmul(low[g], stacked)
        if with_grad:
            stacked = jnp.concatenate([piece[part] for piece in first], axis=0)
            product = ((matmul(high[g], stacked) + matmul(low[g], stacked)) * mid).astype(BF16)
            for r in range(peers):
                grad[rows[r], part] = product[r * span : (r + 1) * span]
        filters = jnp.concatenate([kern[rows[r], part] for r in range(peers)], axis=0)
        upper, lower = two_part(filters.astype(F32) * mid)
        result = matmul(high_t[g], upper) + matmul(low_t[g], upper) + matmul(high_t[g], lower)
        result = result.astype(BF16)
        for r in range(peers):
            outs[r][part] = result[r * span : (r + 1) * span]


def middle_call(place, factors, kern, pieces, first=None):
    peers, columns, channels = kern.shape
    groups, side, _ = factors[0].shape
    width = min(channels, 256)
    cube = pl.BlockSpec((peers, columns, width), lambda c, *_: (0, 0, c))
    with_grad = first is not None
    n_in = peers * (2 if with_grad else 1)
    out = call(
        functools.partial(middle_body, peers, side // peers, with_grad),
        "middle_grad" if with_grad else "middle",
        (channels // width,),
        [whole((groups, side, side))] * 4 + [cube] + [tile(columns, width)] * n_in,
        ([cube] if with_grad else []) + [tile(columns, width)] * peers,
        ([struct(kern.shape, BF16)] if with_grad else []) + [struct((columns, channels), BF16)] * peers,
        (14 if with_grad else 10) * groups * side * side * channels,
        (10 if with_grad else 6) * peers * columns * channels + 8 * groups * side * side,
        scalars=1,
    )(place, *factors, kern, *pieces, *(first or []))
    return (out[0], list(out[1:])) if with_grad else list(out)


def middle_factors(outer, twiddle, place):
    peers, columns = twiddle.shape
    span = min(columns, max(16, 256 // peers))
    groups, side = columns // span, peers * span
    outer_here = lax.dynamic_slice(jnp.tile(outer, (2, 2)), (place, place), (peers, peers))
    twiddle_here = lax.dynamic_slice(jnp.tile(twiddle, (2, 1)), (place, 0), (peers, columns))
    wide = jnp.repeat(jnp.repeat(outer_here, span, axis=0), span, axis=1)
    spot = jnp.arange(side) % span
    wide = jnp.where(spot[:, None] == spot[None, :], wide, 0.0)
    scale = twiddle_here.reshape(peers, groups, span).transpose(1, 0, 2).reshape(groups, 1, side)
    factor = wide[None] * scale
    high = lax.reduce_precision(factor, 8, 7)
    low = factor - high
    high, low = high.astype(BF16), low.astype(BF16)
    return high, low, high.transpose(0, 2, 1), low.transpose(0, 2, 1)


def join_rows(pieces):
    return jnp.concatenate([piece[...] for piece in pieces], axis=0)


def forward_body(peers, turned, weight, gate, scaled, *refs):
    pieces, (mixed, back, head) = refs[:peers], refs[peers:]
    conv = matmul(turned[...], join_rows(pieces))
    mixed[...] = (gate[...] * conv).astype(BF16)
    grad = scaled[...] * conv
    head[...] = grad[0:2]
    length = grad.shape[0]
    row = lax.broadcasted_iota(jnp.int32, grad.shape, 0)
    taps = weight[...]
    one_on = jnp.where(row < length - 1, pltpu.roll(grad, length - 1, 0), 0.0)
    two_on = jnp.where(row < length - 2, pltpu.roll(grad, length - 2, 0), 0.0)
    back[...] = taps[0:1] * grad + taps[1:2] * one_on + taps[2:3] * two_on


def forward_call(turned, weight, gate, scaled, pieces):
    length, channels = gate.shape
    peers, share = len(pieces), pieces[0].shape[0]
    width = min(channels, 256)
    return call(
        functools.partial(forward_body, peers),
        "forward_rows",
        (channels // width,),
        [whole(turned.shape), tile(3, width), tile(length, width), tile(length, width)]
        + [tile(share, width)] * peers,
        [tile(length, width), tile(length, width), tile(2, width)],
        [struct((length, channels), BF16), struct((length, channels), F32), struct((2, channels), F32)],
        2 * length * length * channels,
        16 * length * channels + 2 * length * length,
    )(turned, weight, gate, scaled, *pieces)


def backward_body(peers, turned, weight, back, tail, *refs):
    pieces, grad = refs[:peers], refs[peers]
    total = matmul(turned[...], join_rows(pieces)) + back[...]
    taps, edge = weight[...], tail[...]
    length = total.shape[0]
    grad[...] = total.astype(BF16)
    last = total[length - 16 :]
    row = lax.broadcasted_iota(jnp.int32, last.shape, 0)
    extra = jnp.where(row == 15, taps[1:2] * edge[0:1] + taps[2:3] * edge[1:2], 0.0)
    extra = jnp.where(row == 14, taps[2:3] * edge[0:1], extra)
    grad[length - 16 :] = (last + extra).astype(BF16)


def backward_call(turned, weight, back, tail, pieces):
    length, channels = back.shape
    peers, share = len(pieces), pieces[0].shape[0]
    width = min(channels, 256)
    return call(
        functools.partial(backward_body, peers),
        "backward_rows",
        (channels // width,),
        [whole(turned.shape), tile(3, width), tile(length, width), tile(2, width)]
        + [tile(share, width)] * peers,
        tile(length, width),
        struct((length, channels), BF16),
        2 * length * length * channels,
        8 * length * channels + 2 * length * length,
    )(turned, weight, back, tail, *pieces)


def to_middle(pieces):
    return [piece if r == 0 else hop(piece, -r) for r, piece in enumerate(pieces)]


def to_rows(pieces):
    return [piece if r == 0 else hop(piece, r) for r, piece in enumerate(pieces)]


def on_device(tokens, short_weight, inner_factor, outer_factor, twiddle, kernel, cotangent):
    peers = lax.axis_size("seq")
    place, core = lax.axis_index("seq"), lax.axis_index("ch")
    row_count, block, channels = tokens.shape
    assert row_count == 1 and lax.axis_size("ch") == 2
    flat, cot = tokens.reshape(block, channels), cotangent.reshape(block, channels)
    share = inner_factor.shape[0]
    place_ref, core_ref = place.reshape(1).astype(jnp.int32), core.reshape(1).astype(jnp.int32)

    half = lax.dynamic_slice(inner_factor, (core * (share // 2), 0), (share // 2, block))
    mine = [hop(half, k) for k in range(1, peers)]
    other = [swap_cores(piece) for piece in mine]

    preceding = shifted(flat[-2:], 1)
    gated, gate, scaled = gate_call(flat, preceding, short_weight, cot)
    factors = middle_factors(outer_factor, twiddle, place)

    joined, spread = spread_first_call(core_ref, inner_factor, mine, other, flat)
    spread = to_middle(spread)
    spread_cot = to_middle(spread_call(joined, gated, peers))
    turned = turn_call(joined)

    rows_fwd = to_rows(middle_call(place_ref, factors, kernel, spread))
    kernel_grad, rows_bwd = middle_call(place_ref, factors, kernel, spread_cot, spread)
    rows_bwd = to_rows(rows_bwd)

    mixer_out, back, head = forward_call(turned, short_weight, gate, scaled, rows_fwd)
    following = shifted(head, -1)
    token_grad = backward_call(turned, short_weight, back, following, rows_bwd)
    return mixer_out.reshape(tokens.shape), token_grad.reshape(tokens.shape), kernel_grad


def solution(mesh):
    in_specs = (
        P(("grp", "seq"), None, "ch"),
        P(None, "ch"),
        P("seq", None),
        P(),
        P(None, "seq"),
        P(None, "seq", "ch"),
        P(("grp", "seq"), None, "ch"),
    )
    out_specs = (
        P(("grp", "seq"), None, "ch"),
        P(("grp", "seq"), None, "ch"),
        P("grp", "seq", "ch"),
    )
    return jax.shard_map(
        on_device, mesh=mesh, in_specs=in_specs, out_specs=out_specs, check_vma=False
    )
```

profile of v0, /device:TPU:14, one launch (start us, length us, event | category | flops | bytes accessed | tf_op | source)
XLA Modules:
  0.0 277.3 jit_solution(803175752708293080)
XLA Ops:
  23.7 4.7 %collective-permute-done.1.refs_1_ = bf16[64,1024]{1,0:T(8,128)(2,1)S(1)} collective-permute-done((bf16[64,1024]{1,0:T(8,128)(2,1)S(1)}, bf16[64,1024]{1,0:T(8,128)(2,1)S(1)}, u32[]{:S(2)}, u32[]{:S(2)}) %collective-permute-start.1) | collective-permute-done | bytes 131104 | tf_op jit(solution)/shard_map/ppermute | solution.py:16
  32.8 9.0 %gate.1 = (bf16[1024,1024]{1,0:T(8,128)(2,1)S(1)}, f32[1024,1024]{1,0:T(8,128)}, f32[1024,1024]{1,0:T(8,128)}) custom-call(bf16[1024,1024]{1,0:T(8,128)(2,1)S(1)} %bitcast.19, bf16[2,1024]{1,0:T(2,128)(2,1)S(1)} %collective-permute-done.14.halo, f32[3,1024]{1,0:T(4,128)S(1)} %copy-done.7, bf16[1024,1024]{1,0:T(8,128)(2,1)} %bitcast.21), custom_call_target="tpu_custom_call" | custom-call | flops 20971520 | bytes 14680064 | tf_op jit(solution)/shard_map/gate/pallas_call | solution.py:77
  43.1 5.4 %spread_first.1 = (bf16[1024,1024]{1,0:T(8,128)(2,1)}, bf16[128,1024]{1,0:T(8,128)(2,1)S(1)}, bf16[128,1024]{1,0:T(8,128)(2,1)S(1)}, bf16[128,1024]{1,0:T(8,128)...) custom-call(s32[1]{0:T(128)} %bitcast.core, ...), custom_call_target="tpu_custom_call" | custom-call | flops 2147483648 | bytes 8388608 | tf_op jit(solution)/shard_map/spread_first/pallas_call | solution.py:132
  50.8 5.2 %spread.1 = (bf16[128,1024]{1,0:T(8,128)(2,1)S(1)}, bf16[128,1024]{1,0:T(8,128)(2,1)}, bf16[128,1024]{1,0:T(8,128)(2,1)}, bf16[128,1024]{1,0:T(8,128)(2,1)S(1)},...) custom-call(bf16[1024,1024]{1,0:T(8,128)(2,1)S(1)} %copy-done.2, ...), custom_call_target="tpu_custom_call" | custom-call | flops 2147483648 | bytes 6291456 | tf_op jit(solution)/shard_map/spread/pallas_call | solution.py:151
  69.7 4.9 %collective-permute-start.36 = (bf16[128,1024]{1,0:T(8,128)(2,1)}, bf16[128,1024]{1,0:T(8,128)(2,1)}, u32[]{:S(2)}, u32[]{:S(2)}) collective-permute-start(bf16[128,1024]{1,0:T(8,128)(2,1)} %get-tuple-element.73), channel_id=1, source_target_pairs={{0,2},{2,4},{4,6},{6,8},{8,10},{10,12},{12,14},{14,0},{1,3},{3,5},... | collective-permute-start | bytes 786440 | tf_op jit(solution)/shard_map/ppermute | solution.py:16
  74.6 5.2 %collective-permute-done.32.refs_3_ = bf16[128,1024]{1,0:T(8,128)(2,1)S(1)} collective-permute-done((bf16[128,1024]{1,0:T(8,128)(2,1)S(1)}, bf16[128,1024]{1,0:T(8,128)(2,1)S(1)}, u32[]{:S(2)}, u32[]{:S(2)}) %collective-permute-start.32) | collective-permute-done | bytes 262176 | tf_op jit(solution)/shard_map/ppermute | solution.py:16
  79.8 9.0 %collective-permute-start.15 = (bf16[128,1024]{1,0:T(8,128)(2,1)S(1)}, bf16[128,1024]{1,0:T(8,128)(2,1)S(1)}, u32[]{:S(2)}, u32[]{:S(2)}) collective-permute-start(bf16[128,1024]{1,0:T(8,128)(2,1)S(1)} %get-tuple-element.47), channel_id=1, source_target_pairs={{0,14},{2,0},{4,2},{6,4},{8,6},{10,8},{12,10},{14,12},{1,15},{3,1}... | collective-permute-start | bytes 786440 | tf_op jit(solution)/shard_map/ppermute | solution.py:16
  91.3 10.9 %collective-permute-start.16 = (bf16[128,1024]{1,0:T(8,128)(2,1)S(1)}, bf16[128,1024]{1,0:T(8,128)(2,1)}, u32[]{:S(2)}, u32[]{:S(2)}) collective-permute-start(bf16[128,1024]{1,0:T(8,128)(2,1)S(1)} %get-tuple-element.48), channel_id=1, source_target_pairs={{0,12},{2,14},{4,0},{6,2},{8,4},{10,6},{12,8},{14,10},{1,13},{3,15... | collective-permute-start | bytes 786440 | tf_op jit(solution)/shard_map/ppermute | solution.py:16
  102.4 5.7 %collective-permute-start.17 = (bf16[128,1024]{1,0:T(8,128)(2,1)S(1)}, bf16[128,1024]{1,0:T(8,128)(2,1)S(1)}, u32[]{:S(2)}, u32[]{:S(2)}) collective-permute-start(bf16[128,1024]{1,0:T(8,128)(2,1)S(1)} %get-tuple-element.49), channel_id=1, source_target_pairs={{0,10},{2,12},{4,14},{6,0},{8,2},{10,4},{12,6},{14,8},{1,11},{3,13... | collective-permute-start | bytes 786440 | tf_op jit(solution)/shard_map/ppermute | solution.py:16
  108.1 5.6 %collective-permute-done.35.refs_6_ = bf16[128,1024]{1,0:T(8,128)(2,1)} collective-permute-done((bf16[128,1024]{1,0:T(8,128)(2,1)}, bf16[128,1024]{1,0:T(8,128)(2,1)}, u32[]{:S(2)}, u32[]{:S(2)}) %collective-permute-start.35) | collective-permute-done | bytes 262176 | tf_op jit(solution)/shard_map/ppermute | solution.py:16
  113.7 11.3 %collective-permute-done.36.refs_7_ = bf16[128,1024]{1,0:T(8,128)(2,1)} collective-permute-done((bf16[128,1024]{1,0:T(8,128)(2,1)}, bf16[128,1024]{1,0:T(8,128)(2,1)}, u32[]{:S(2)}, u32[]{:S(2)}) %collective-permute-start.36) | collective-permute-done | bytes 262176 | tf_op jit(solution)/shard_map/ppermute | solution.py:16
  131.0 5.0 %collective-permute-done.18.refs_4_.refs_12_ = bf16[128,1024]{1,0:T(8,128)(2,1)S(1)} collective-permute-done((bf16[128,1024]{1,0:T(8,128)(2,1)S(1)}, bf16[128,1024]{1,0:T(8,128)(2,1)S(1)}, u32[]{:S(2)}, u32[]{:S(2)}) %collective-permute-start.18) | collective-permute-done | bytes 262176 | tf_op jit(solution)/shard_map/ppermute | solution.py:16
  136.1 5.8 %collective-permute-done.19.refs_5_.refs_13_ = bf16[128,1024]{1,0:T(8,128)(2,1)S(1)} collective-permute-done((bf16[128,1024]{1,0:T(8,128)(2,1)S(1)}, bf16[128,1024]{1,0:T(8,128)(2,1)S(1)}, u32[]{:S(2)}, u32[]{:S(2)}) %collective-permute-start.19) | collective-permute-done | bytes 262176 | tf_op jit(solution)/shard_map/ppermute | solution.py:16
  141.8 5.6 %collective-permute-done.20.refs_6_.refs_14_ = bf16[128,1024]{1,0:T(8,128)(2,1)S(1)} collective-permute-done((bf16[128,1024]{1,0:T(8,128)(2,1)S(1)}, bf16[128,1024]{1,0:T(8,128)(2,1)S(1)}, u32[]{:S(2)}, u32[]{:S(2)}) %collective-permute-start.20) | collective-permute-done | bytes 262176 | tf_op jit(solution)/shard_map/ppermute | solution.py:16
  147.5 5.6 %collective-permute-done.21.refs_7_.refs_15_ = bf16[128,1024]{1,0:T(8,128)(2,1)S(1)} collective-permute-done((bf16[128,1024]{1,0:T(8,128)(2,1)S(1)}, bf16[128,1024]{1,0:T(8,128)(2,1)S(1)}, u32[]{:S(2)}, u32[]{:S(2)}) %collective-permute-start.21) | collective-permute-done | bytes 262176 | tf_op jit(solution)/shard_map/ppermute | solution.py:16
  153.7 9.0 %middle_grad.1 = (bf16[8,128,1024]{2,1,0:T(8,128)(2,1)}, bf16[128,1024]{1,0:T(8,128)(2,1)S(1)}, bf16[128,1024]{1,0:T(8,128)(2,1)S(1)}, bf16[128,1024]{1,0:T(8,12...) custom-call(s32[1]{0:T(128)} %bitcast.4.place, ...), custom_call_target="tpu_custom_call" | custom-call | flops 3758096384 | bytes 12582912 | tf_op jit(solution)/shard_map/middle_grad/pallas_call | solution.py:220
  167.2 7.5 %middle.1 = (bf16[128,1024]{1,0:T(8,128)(2,1)S(1)}, bf16[128,1024]{1,0:T(8,128)(2,1)S(1)}, bf16[128,1024]{1,0:T(8,128)(2,1)S(1)}, bf16[128,1024]{1,0:T(8,128)(2,...) custom-call(s32[1]{0:T(128)} %bitcast.4.place, ...), custom_call_target="tpu_custom_call" | custom-call | flops 2684354560 | bytes 8388608 | tf_op jit(solution)/shard_map/middle/pallas_call | solution.py:220
  174.9 5.6 %collective-permute-start.24 = (bf16[128,1024]{1,0:T(8,128)(2,1)S(1)}, bf16[128,1024]{1,0:T(8,128)(2,1)S(1)}, u32[]{:S(2)}, u32[]{:S(2)}) collective-permute-start(bf16[128,1024]{1,0:T(8,128)(2,1)S(1)} %get-tuple-element.57), channel_id=1, source_target_pairs={{0,6},{2,8},{4,10},{6,12},{8,14},{10,0},{12,2},{14,4},{1,7},{3,9},... | collective-permute-start | bytes 786440 | tf_op jit(solution)/shard_map/ppermute | solution.py:16
  184.3 27.8 %collective-permute-done.23.refs_2_ = bf16[128,1024]{1,0:T(8,128)(2,1)S(1)} collective-permute-done((bf16[128,1024]{1,0:T(8,128)(2,1)S(1)}, bf16[128,1024]{1,0:T(8,128)(2,1)S(1)}, u32[]{:S(2)}, u32[]{:S(2)}) %collective-permute-start.23) | collective-permute-done | bytes 262176 | tf_op jit(solution)/shard_map/ppermute | solution.py:16
  212.1 16.8 %collective-permute-done.24.refs_3_ = bf16[128,1024]{1,0:T(8,128)(2,1)S(1)} collective-permute-done((bf16[128,1024]{1,0:T(8,128)(2,1)S(1)}, bf16[128,1024]{1,0:T(8,128)(2,1)S(1)}, u32[]{:S(2)}, u32[]{:S(2)}) %collective-permute-start.24) | collective-permute-done | bytes 262176 | tf_op jit(solution)/shard_map/ppermute | solution.py:16
  233.2 7.0 %collective-permute-done.25.refs_4_ = bf16[128,1024]{1,0:T(8,128)(2,1)S(1)} collective-permute-done((bf16[128,1024]{1,0:T(8,128)(2,1)S(1)}, bf16[128,1024]{1,0:T(8,128)(2,1)S(1)}, u32[]{:S(2)}, u32[]{:S(2)}) %collective-permute-start.25) | collective-permute-done | bytes 262176 | tf_op jit(solution)/shard_map/ppermute | solution.py:16
  246.3 8.1 %forward_rows.1 = (bf16[1024,1024]{1,0:T(8,128)(2,1)}, f32[1024,1024]{1,0:T(8,128)}, f32[2,1024]{1,0:T(2,128)S(1)}) custom-call(bf16[1024,1024]{1,0:T(8,128)(2,1)S(1)} %turn.1.turned, f32[3,1024]{1,0:T(4,128)S(1)} %copy-done.8, f32[1024,1024]{1,0:T(8,128)} %get-tuple-element.44.gate, f32[1024,1024]{1,0:T(8,128)} %get-tuple-element.45.scaled, ...), custom_call_target="tpu_custom_call" | custom-call | flops 2147483648 | bytes 18874368 | tf_op jit(solution)/shard_map/forward_rows/pallas_call | solution.py:273
  257.8 13.6 %collective-permute-done.43.refs_7_ = bf16[128,1024]{1,0:T(8,128)(2,1)S(1)} collective-permute-done((bf16[128,1024]{1,0:T(8,128)(2,1)S(1)}, bf16[128,1024]{1,0:T(8,128)(2,1)S(1)}, u32[]{:S(2)}, u32[]{:S(2)}) %collective-permute-start.43) | collective-permute-done | bytes 262176 | tf_op jit(solution)/shard_map/ppermute | solution.py:16
  271.5 5.8 %backward_rows.1 = bf16[1024,1024]{1,0:T(8,128)(2,1)} custom-call(bf16[1024,1024]{1,0:T(8,128)(2,1)S(1)} %turn.1.turned, f32[3,1024]{1,0:T(4,128)S(1)} %copy-done.8, f32[1024,1024]{1,0:T(8,128)} %get-tuple-element.63.back, f32[2,1024]{1,0:T(2,128)S(1)} %collective-permute-done.29.tail, bf16[128,1024]{1,0:T(8,128)(2,1)S(1)} %get-tuple-element.74.refs_0_, ...), custom_call_target="tpu_custom_call" | custom-call | flops 2147483648 | bytes 10485760 | tf_op jit(solution)/shard_map/backward_rows/pallas_call | solution.py:303
  (127 shorter events, 76.3 us)
Async XLA Ops:
  1.6 17.2 %collective-permute-start.3 = (bf16[64,1024]{1,0:T(8,128)(2,1)S(1)}, bf16[64,1024]{1,0:T(8,128)(2,1)S(1)}, u32[]{:S(2)}, u32[]{:S(2)}) collective-permute-start(bf16[64,1024]{1,0:T(8,128)(2,1)S(1)} %constant_dynamic-slice_fusion.1), channel_id=1, source_target_pairs={{0,8},{2,10},{4,12},{6,14},{8,0},{10,2},{12,4},{14,6},{1,9},{3,11}... | collective-permute-start | bytes 393224 | tf_op jit(solution)/shard_map/ppermute | solution.py:16
  23.7 19.4 %collective-permute-start.12 = (bf16[64,1024]{1,0:T(8,128)(2,1)S(1)}, bf16[64,1024]{1,0:T(8,128)(2,1)S(1)}, u32[]{:S(2)}, u32[]{:S(2)}) collective-permute-start(bf16[64,1024]{1,0:T(8,128)(2,1)S(1)} %collective-permute-done.5.refs_5_), channel_id=1, source_target_pairs={{0,1},{1,0},{2,3},{3,2},{4,5},{5,4},{6,7},{7,6},{8,9},{9,8},{10,11... | collective-permute-start | bytes 393224 | tf_op jit(solution)/shard_map/ppermute | solution.py:25
  59.0 20.7 %collective-permute-start.32 = (bf16[128,1024]{1,0:T(8,128)(2,1)S(1)}, bf16[128,1024]{1,0:T(8,128)(2,1)S(1)}, u32[]{:S(2)}, u32[]{:S(2)}) collective-permute-start(bf16[128,1024]{1,0:T(8,128)(2,1)S(1)} %get-tuple-element.69), channel_id=1, source_target_pairs={{0,10},{2,12},{4,14},{6,0},{8,2},{10,4},{12,6},{14,8},{1,11},{3,13... | collective-permute-start | bytes 786440 | tf_op jit(solution)/shard_map/ppermute | solution.py:16
  62.5 28.8 %collective-permute-start.33 = (bf16[128,1024]{1,0:T(8,128)(2,1)}, bf16[128,1024]{1,0:T(8,128)(2,1)S(1)}, u32[]{:S(2)}, u32[]{:S(2)}) collective-permute-start(bf16[128,1024]{1,0:T(8,128)(2,1)} %get-tuple-element.70), channel_id=1, source_target_pairs={{0,8},{2,10},{4,12},{6,14},{8,0},{10,2},{12,4},{14,6},{1,9},{3,11}... | collective-permute-start | bytes 786440 | tf_op jit(solution)/shard_map/ppermute | solution.py:16
  63.9 38.5 %collective-permute-start.34 = (bf16[128,1024]{1,0:T(8,128)(2,1)}, bf16[128,1024]{1,0:T(8,128)(2,1)S(1)}, u32[]{:S(2)}, u32[]{:S(2)}) collective-permute-start(bf16[128,1024]{1,0:T(8,128)(2,1)} %get-tuple-element.71), channel_id=1, source_target_pairs={{0,6},{2,8},{4,10},{6,12},{8,14},{10,0},{12,2},{14,4},{1,7},{3,9},... | collective-permute-start | bytes 786440 | tf_op jit(solution)/shard_map/ppermute | solution.py:16
  67.0 46.7 %collective-permute-start.35 = (bf16[128,1024]{1,0:T(8,128)(2,1)}, bf16[128,1024]{1,0:T(8,128)(2,1)}, u32[]{:S(2)}, u32[]{:S(2)}) collective-permute-start(bf16[128,1024]{1,0:T(8,128)(2,1)} %get-tuple-element.72), channel_id=1, source_target_pairs={{0,4},{2,6},{4,8},{6,10},{8,12},{10,14},{12,0},{14,2},{1,5},{3,7},... | collective-permute-start | bytes 786440 | tf_op jit(solution)/shard_map/ppermute | solution.py:16
  69.7 55.3 %collective-permute-start.36 = (bf16[128,1024]{1,0:T(8,128)(2,1)}, bf16[128,1024]{1,0:T(8,128)(2,1)}, u32[]{:S(2)}, u32[]{:S(2)}) collective-permute-start(bf16[128,1024]{1,0:T(8,128)(2,1)} %get-tuple-element.73), channel_id=1, source_target_pairs={{0,2},{2,4},{4,6},{6,8},{8,10},{10,12},{12,14},{14,0},{1,3},{3,5},... | collective-permute-start | bytes 786440 | tf_op jit(solution)/shard_map/ppermute | solution.py:16
  79.8 45.5 %collective-permute-start.15 = (bf16[128,1024]{1,0:T(8,128)(2,1)S(1)}, bf16[128,1024]{1,0:T(8,128)(2,1)S(1)}, u32[]{:S(2)}, u32[]{:S(2)}) collective-permute-start(bf16[128,1024]{1,0:T(8,128)(2,1)S(1)} %get-tuple-element.47), channel_id=1, source_target_pairs={{0,14},{2,0},{4,2},{6,4},{8,6},{10,8},{12,10},{14,12},{1,15},{3,1}... | collective-permute-start | bytes 786440 | tf_op jit(solution)/shard_map/ppermute | solution.py:16
  91.3 36.5 %collective-permute-start.16 = (bf16[128,1024]{1,0:T(8,128)(2,1)S(1)}, bf16[128,1024]{1,0:T(8,128)(2,1)}, u32[]{:S(2)}, u32[]{:S(2)}) collective-permute-start(bf16[128,1024]{1,0:T(8,128)(2,1)S(1)} %get-tuple-element.48), channel_id=1, source_target_pairs={{0,12},{2,14},{4,0},{6,2},{8,4},{10,6},{12,8},{14,10},{1,13},{3,15... | collective-permute-start | bytes 786440 | tf_op jit(solution)/shard_map/ppermute | solution.py:16
  102.4 28.7 %collective-permute-start.17 = (bf16[128,1024]{1,0:T(8,128)(2,1)S(1)}, bf16[128,1024]{1,0:T(8,128)(2,1)S(1)}, u32[]{:S(2)}, u32[]{:S(2)}) collective-permute-start(bf16[128,1024]{1,0:T(8,128)(2,1)S(1)} %get-tuple-element.49), channel_id=1, source_target_pairs={{0,10},{2,12},{4,14},{6,0},{8,2},{10,4},{12,6},{14,8},{1,11},{3,13... | collective-permute-start | bytes 786440 | tf_op jit(solution)/shard_map/ppermute | solution.py:16
  113.7 22.3 %collective-permute-start.18 = (bf16[128,1024]{1,0:T(8,128)(2,1)S(1)}, bf16[128,1024]{1,0:T(8,128)(2,1)S(1)}, u32[]{:S(2)}, u32[]{:S(2)}) collective-permute-start(bf16[128,1024]{1,0:T(8,128)(2,1)S(1)} %get-tuple-element.50), channel_id=1, source_target_pairs={{0,8},{2,10},{4,12},{6,14},{8,0},{10,2},{12,4},{14,6},{1,9},{3,11}... | collective-permute-start | bytes 786440 | tf_op jit(solution)/shard_map/ppermute | solution.py:16
  125.3 22.2 %collective-permute-start.20 = (bf16[128,1024]{1,0:T(8,128)(2,1)S(1)}, bf16[128,1024]{1,0:T(8,128)(2,1)S(1)}, u32[]{:S(2)}, u32[]{:S(2)}) collective-permute-start(bf16[128,1024]{1,0:T(8,128)(2,1)S(1)} %get-tuple-element.52), channel_id=1, source_target_pairs={{0,4},{2,6},{4,8},{6,10},{8,12},{10,14},{12,0},{14,2},{1,5},{3,7},... | collective-permute-start | bytes 786440 | tf_op jit(solution)/shard_map/ppermute | solution.py:16
  127.8 25.2 %collective-permute-start.21 = (bf16[128,1024]{1,0:T(8,128)(2,1)S(1)}, bf16[128,1024]{1,0:T(8,128)(2,1)S(1)}, u32[]{:S(2)}, u32[]{:S(2)}) collective-permute-start(bf16[128,1024]{1,0:T(8,128)(2,1)S(1)} %get-tuple-element.53), channel_id=1, source_target_pairs={{0,2},{2,4},{4,6},{6,8},{8,10},{10,12},{12,14},{14,0},{1,3},{3,5},... | collective-permute-start | bytes 786440 | tf_op jit(solution)/shard_map/ppermute | solution.py:16
  162.7 17.7 %collective-permute-start.37 = (bf16[128,1024]{1,0:T(8,128)(2,1)S(1)}, bf16[128,1024]{1,0:T(8,128)(2,1)S(1)}, u32[]{:S(2)}, u32[]{:S(2)}) collective-permute-start(bf16[128,1024]{1,0:T(8,128)(2,1)S(1)} %get-tuple-element.75), channel_id=1, source_target_pairs={{0,2},{2,4},{4,6},{6,8},{8,10},{10,12},{12,14},{14,0},{1,3},{3,5},... | collective-permute-start | bytes 786440 | tf_op jit(solution)/shard_map/ppermute | solution.py:16
  174.8 37.3 %collective-permute-start.23 = (bf16[128,1024]{1,0:T(8,128)(2,1)S(1)}, bf16[128,1024]{1,0:T(8,128)(2,1)S(1)}, u32[]{:S(2)}, u32[]{:S(2)}) collective-permute-start(bf16[128,1024]{1,0:T(8,128)(2,1)S(1)} %get-tuple-element.56), channel_id=1, source_target_pairs={{0,4},{2,6},{4,8},{6,10},{8,12},{10,14},{12,0},{14,2},{1,5},{3,7},... | collective-permute-start | bytes 786440 | tf_op jit(solution)/shard_map/ppermute | solution.py:16
  174.9 54.1 %collective-permute-start.24 = (bf16[128,1024]{1,0:T(8,128)(2,1)S(1)}, bf16[128,1024]{1,0:T(8,128)(2,1)S(1)}, u32[]{:S(2)}, u32[]{:S(2)}) collective-permute-start(bf16[128,1024]{1,0:T(8,128)(2,1)S(1)} %get-tuple-element.57), channel_id=1, source_target_pairs={{0,6},{2,8},{4,10},{6,12},{8,14},{10,0},{12,2},{14,4},{1,7},{3,9},... | collective-permute-start | bytes 786440 | tf_op jit(solution)/shard_map/ppermute | solution.py:16
  180.5 59.7 %collective-permute-start.25 = (bf16[128,1024]{1,0:T(8,128)(2,1)S(1)}, bf16[128,1024]{1,0:T(8,128)(2,1)S(1)}, u32[]{:S(2)}, u32[]{:S(2)}) collective-permute-start(bf16[128,1024]{1,0:T(8,128)(2,1)S(1)} %get-tuple-element.58), channel_id=1, source_target_pairs={{0,8},{2,10},{4,12},{6,14},{8,0},{10,2},{12,4},{14,6},{1,9},{3,11}... | collective-permute-start | bytes 786440 | tf_op jit(solution)/shard_map/ppermute | solution.py:16
  180.5 63.1 %collective-permute-start.26 = (bf16[128,1024]{1,0:T(8,128)(2,1)S(1)}, bf16[128,1024]{1,0:T(8,128)(2,1)S(1)}, u32[]{:S(2)}, u32[]{:S(2)}) collective-permute-start(bf16[128,1024]{1,0:T(8,128)(2,1)S(1)} %get-tuple-element.59), channel_id=1, source_target_pairs={{0,10},{2,12},{4,14},{6,0},{8,2},{10,4},{12,6},{14,8},{1,11},{3,13... | collective-permute-start | bytes 786440 | tf_op jit(solution)/shard_map/ppermute | solution.py:16
  184.0 59.6 %collective-permute-start.27 = (bf16[128,1024]{1,0:T(8,128)(2,1)S(1)}, bf16[128,1024]{1,0:T(8,128)(2,1)S(1)}, u32[]{:S(2)}, u32[]{:S(2)}) collective-permute-start(bf16[128,1024]{1,0:T(8,128)(2,1)S(1)} %get-tuple-element.60), channel_id=1, source_target_pairs={{0,12},{2,14},{4,0},{6,2},{8,4},{10,6},{12,8},{14,10},{1,13},{3,15... | collective-permute-start | bytes 786440 | tf_op jit(solution)/shard_map/ppermute | solution.py:16
  212.1 31.6 %collective-permute-start.28 = (bf16[128,1024]{1,0:T(8,128)(2,1)S(1)}, bf16[128,1024]{1,0:T(8,128)(2,1)S(1)}, u32[]{:S(2)}, u32[]{:S(2)}) collective-permute-start(bf16[128,1024]{1,0:T(8,128)(2,1)S(1)} %get-tuple-element.61), channel_id=1, source_target_pairs={{0,14},{2,0},{4,2},{6,4},{8,6},{10,8},{12,10},{14,12},{1,15},{3,1}... | collective-permute-start | bytes 786440 | tf_op jit(solution)/shard_map/ppermute | solution.py:16
  229.0 25.4 %collective-permute-start.39 = (bf16[128,1024]{1,0:T(8,128)(2,1)S(1)}, bf16[128,1024]{1,0:T(8,128)(2,1)S(1)}, u32[]{:S(2)}, u32[]{:S(2)}) collective-permute-start(bf16[128,1024]{1,0:T(8,128)(2,1)S(1)} %get-tuple-element.77), channel_id=1, source_target_pairs={{0,6},{2,8},{4,10},{6,12},{8,14},{10,0},{12,2},{14,4},{1,7},{3,9},... | collective-permute-start | bytes 786440 | tf_op jit(solution)/shard_map/ppermute | solution.py:16
  240.2 17.5 %collective-permute-start.40 = (bf16[128,1024]{1,0:T(8,128)(2,1)S(1)}, bf16[128,1024]{1,0:T(8,128)(2,1)S(1)}, u32[]{:S(2)}, u32[]{:S(2)}) collective-permute-start(bf16[128,1024]{1,0:T(8,128)(2,1)S(1)} %get-tuple-element.78), channel_id=1, source_target_pairs={{0,8},{2,10},{4,12},{6,14},{8,0},{10,2},{12,4},{14,6},{1,9},{3,11}... | collective-permute-start | bytes 786440 | tf_op jit(solution)/shard_map/ppermute | solution.py:16
  243.7 27.7 %collective-permute-start.43 = (bf16[128,1024]{1,0:T(8,128)(2,1)S(1)}, bf16[128,1024]{1,0:T(8,128)(2,1)S(1)}, u32[]{:S(2)}, u32[]{:S(2)}) collective-permute-start(bf16[128,1024]{1,0:T(8,128)(2,1)S(1)} %get-tuple-element.81), channel_id=1, source_target_pairs={{0,14},{2,0},{4,2},{6,4},{8,6},{10,8},{12,10},{14,12},{1,15},{3,1}... | collective-permute-start | bytes 786440 | tf_op jit(solution)/shard_map/ppermute | solution.py:16
  254.4 17.1 %collective-permute-start.29 = (f32[2,1024]{1,0:T(2,128)S(1)}, f32[2,1024]{1,0:T(2,128)S(1)}, u32[]{:S(2)}, u32[]{:S(2)}) collective-permute-start(f32[2,1024]{1,0:T(2,128)S(1)} %get-tuple-element.64), channel_id=1, source_target_pairs={{2,0},{4,2},{6,4},{8,6},{10,8},{12,10},{14,12},{3,1},{5,3},{7,5},{... | collective-permute-start | bytes 24584 | tf_op jit(solution)/shard_map/ppermute | solution.py:21
  (39 other events, 601.6 us)
where the time goes:
time: 278 us; the launch traced here: 277 us
  waiting for transfers between devices  126 us (45%)
  starting transfers between devices  85.2 us (31%)
  Pallas kernels  51.2 us (18%)
  local copies, waits for them, and re-layouts  11.5 us (4%)
    ppermute x35, waiting for transfers between devices, hop(): lax.ppermute(block, 'seq', [(i, (i + distance) % peers) for i in range(pe...  122 us
    ppermute x35, starting transfers between devices, hop(): lax.ppermute(block, 'seq', [(i, (i + distance) % peers) for i in range(pe...  76.5 us
    pallas_call x2, Pallas kernels, middle_call(): call(functools.partial(middle_body, peers, side // peers, with_grad), 'mi...  16.5 us
    pallas_call x1, Pallas kernels, gate_call(): call(gate_body, 'gate', (channels // width,), [tile(length, width), tile(...  8.99 us
    unnamed x39, local copies, waits for them, and re-layouts  8.52 us
    pallas_call x1, Pallas kernels, forward_call(): call(functools.partial(forward_body, peers), 'forward_rows', (channels //...  8.11 us
    ppermute x2, starting transfers between devices, shifted(): lax.ppermute(block, 'seq', [(i - distance, i) for i in devices if i - dis...  7.68 us
    pallas_call x1, Pallas kernels, backward_call(): call(functools.partial(backward_body, peers), 'backward_rows', (channels...  5.83 us
  transfers between devices with their start and end apart: 44, of which 19 were waited for; matrix products, arithmetic and copies ran while one was open for 2% of the time, Pallas kernels for 9%

commit v1 on v0

v1 whole, which is shorter than its diff:
```python
import functools

import jax
import jax.numpy as jnp
from jax import lax
from jax.experimental import pallas as pl
from jax.experimental.pallas import tpu as pltpu
from jax.sharding import PartitionSpec as P

BF16, F32 = jnp.bfloat16, jnp.float32
VMEM_LIMIT = 48 * 1024 * 1024


def exchange(block, mask):
    return lax.ppermute(block, "seq", [(i, i ^ mask) for i in range(lax.axis_size("seq"))])


def shifted(block, distance):
    devices = range(lax.axis_size("seq"))
    return lax.ppermute(block, "seq", [(i - distance, i) for i in devices if i - distance in devices])


def swap_cores(block):
    return lax.ppermute(block, "ch", [(0, 1), (1, 0)])


def call(body, name, grid, in_specs, out_specs, out_shape, flops, moved, scalars=0, transcendentals=0):
    return pl.pallas_call(
        body,
        name=name,
        grid_spec=pltpu.PrefetchScalarGridSpec(
            num_scalar_prefetch=scalars, grid=grid, in_specs=in_specs, out_specs=out_specs
        ),
        out_shape=out_shape,
        compiler_params=pltpu.CompilerParams(vmem_limit_bytes=VMEM_LIMIT),
        cost_estimate=pl.CostEstimate(flops=flops, bytes_accessed=moved, transcendentals=transcendentals),
    )


def whole(shape):
    return pl.BlockSpec(shape, lambda c, *_: (0,) * len(shape))


def tile(rows, width):
    return pl.BlockSpec((rows, width), lambda c, *_: (0, c))


def struct(shape, dtype):
    return jax.ShapeDtypeStruct(shape, dtype)


def matmul(left, right):
    return jnp.dot(left, right, preferred_element_type=F32)


def gate_values(tokens, halo, weight):
    x = tokens[...].astype(F32)
    row = lax.broadcasted_iota(jnp.int32, x.shape, 0)
    edge, taps = halo[...].astype(F32), weight[...]
    one_back = jnp.where(row == 0, edge[1:2], pltpu.roll(x, 1, 0))
    two_back = jnp.where(row == 0, edge[0:1], jnp.where(row == 1, edge[1:2], pltpu.roll(x, 2, 0)))
    conv = taps[0:1] * x + taps[1:2] * one_back + taps[2:3] * two_back
    return conv, jax.nn.sigmoid(conv)


def spread_peer_body(core, mine, other, values, piece, rows):
    half = mine.shape[0]
    ours, theirs = matmul(mine[...], values[...]).astype(BF16), matmul(other[...], values[...]).astype(BF16)

    @pl.when(core[0] == 0)
    def _():
        piece[0:half], piece[half:] = ours, theirs
        rows[0:half], rows[half:] = mine[...], other[...]

    @pl.when(core[0] != 0)
    def _():
        piece[0:half], piece[half:] = theirs, ours
        rows[0:half], rows[half:] = other[...], mine[...]


def spread_peer_call(core, mine, other, values):
    half, block = mine.shape
    channels = values.shape[1]
    width = min(channels, 512)
    return call(
        spread_peer_body,
        "spread_peer",
        (channels // width,),
        [whole((half, block))] * 2 + [tile(block, width)],
        [tile(2 * half, width), whole((2 * half, block))],
        [struct((2 * half, channels), BF16), struct((2 * half, block), BF16)],
        4 * half * block * channels,
        2 * block * channels + 8 * half * block,
        scalars=1,
    )(core, mine, other, values)


def spread_own_body(row, values, piece):
    piece[...] = matmul(row[...], values[...]).astype(BF16)


def spread_own_call(row, values):
    share, block = row.shape
    channels = values.shape[1]
    width = min(channels, 512)
    return call(
        spread_own_body,
        "spread_own",
        (channels // width,),
        [whole((share, block)), tile(block, width)],
        tile(share, width),
        struct((share, channels), BF16),
        2 * share * block * channels,
        2 * block * channels + 2 * share * (block + channels),
    )(row, values)


def spread_gated_body(peers, tokens, halo, weight, cot, *refs):
    rows, pieces = refs[:peers], refs[peers:]
    conv, sig = gate_values(tokens, halo, weight)
    gated = (cot[...].astype(F32) * (conv * sig)).astype(BF16)
    for row, piece in zip(rows, pieces):
        piece[...] = matmul(row[...], gated).astype(BF16)


def spread_gated_call(tokens, halo, weight, cot, rows):
    block, channels = tokens.shape
    peers, share = len(rows), rows[0].shape[0]
    width = min(channels, 128)
    out = call(
        functools.partial(spread_gated_body, peers),
        "spread_gated",
        (channels // width,),
        [tile(block, width), tile(2, width), tile(3, width), tile(block, width)]
        + [whole((share, block))] * peers,
        [tile(share, width)] * peers,
        [struct((share, channels), BF16)] * peers,
        2 * peers * share * block * channels,
        4 * block * channels + 2 * peers * share * (block + channels),
        transcendentals=2 * block * channels,
    )(tokens, halo, weight, cot, *rows)
    return list(out)


def turn_body(peers, *refs):
    refs[peers][...] = join_rows(refs[:peers]).T


def turn_call(rows):
    share, block = rows[0].shape
    width = min(block, 256)
    return call(
        functools.partial(turn_body, len(rows)),
        "turn",
        (block // width,),
        [tile(share, width)] * len(rows),
        pl.BlockSpec((width, block), lambda c: (c, 0)),
        struct((block, block), BF16),
        block * block,
        4 * block * block,
    )(*rows)


def two_part(values):
    high = values.astype(BF16)
    return high, (values - high.astype(F32)).astype(BF16)


def middle_body(peers, span, with_grad, place, high, low, high_t, low_t, kern, *refs):
    pieces, refs = refs[:peers], refs[peers:]
    if with_grad:
        first, refs = refs[:peers], refs[peers:]
        grad, refs = refs[0], refs[1:]
    outs = refs[:peers]
    columns = pieces[0].shape[0]
    rows = [lax.bitwise_xor(place[0], r) for r in range(peers)]
    for g in range(columns // span):
        part = slice(g * span, (g + 1) * span)
        stacked = jnp.concatenate([piece[part] for piece in pieces], axis=0)
        mid = matmul(high[g], stacked) + matmul(low[g], stacked)
        if with_grad:
            stacked = jnp.concatenate([piece[part] for piece in first], axis=0)
            product = ((matmul(high[g], stacked) + matmul(low[g], stacked)) * mid).astype(BF16)
            for r in range(peers):
                grad[rows[r], part] = product[r * span : (r + 1) * span]
        filters = jnp.concatenate([kern[rows[r], part] for r in range(peers)], axis=0)
        upper, lower = two_part(filters.astype(F32) * mid)
        result = matmul(high_t[g], upper) + matmul(low_t[g], upper) + matmul(high_t[g], lower)
        result = result.astype(BF16)
        for r in range(peers):
            outs[r][part] = result[r * span : (r + 1) * span]


def middle_call(place, factors, kern, pieces, first=None):
    peers, columns, channels = kern.shape
    groups, side, _ = factors[0].shape
    width = min(channels, 256)
    cube = pl.BlockSpec((peers, columns, width), lambda c, *_: (0, 0, c))
    with_grad = first is not None
    n_in = peers * (2 if with_grad else 1)
    out = call(
        functools.partial(middle_body, peers, side // peers, with_grad),
        "middle_grad" if with_grad else "middle",
        (channels // width,),
        [whole((groups, side, side))] * 4 + [cube] + [tile(columns, width)] * n_in,
        ([cube] if with_grad else []) + [tile(columns, width)] * peers,
        ([struct(kern.shape, BF16)] if with_grad else []) + [struct((columns, channels), BF16)] * peers,
        (14 if with_grad else 10) * groups * side * side * channels,
        (10 if with_grad else 6) * peers * columns * channels + 8 * groups * side * side,
        scalars=1,
    )(place, *factors, kern, *pieces, *(first or []))
    return (out[0], list(out[1:])) if with_grad else list(out)


def middle_factors(outer, twiddle, place):
    peers, columns = twiddle.shape
    span = min(columns, max(16, 256 // peers))
    groups, side = columns // span, peers * span
    order = lax.bitwise_xor(jnp.arange(peers), place)
    pick = (order[:, None] == jnp.arange(peers)[None, :]).astype(F32)
    exact = functools.partial(jnp.dot, precision=lax.Precision.HIGHEST, preferred_element_type=F32)
    outer_here, twiddle_here = exact(exact(pick, outer), pick.T), exact(pick, twiddle)
    wide = jnp.repeat(jnp.repeat(outer_here, span, axis=0), span, axis=1)
    spot = jnp.arange(side) % span
    wide = jnp.where(spot[:, None] == spot[None, :], wide, 0.0)
    scale = twiddle_here.reshape(peers, groups, span).transpose(1, 0, 2).reshape(groups, 1, side)
    factor = wide[None] * scale
    high = lax.reduce_precision(factor, 8, 7)
    low = factor - high
    high, low = high.astype(BF16), low.astype(BF16)
    return high, low, high.transpose(0, 2, 1), low.transpose(0, 2, 1)


def join_rows(pieces):
    return jnp.concatenate([piece[...] for piece in pieces], axis=0)


def forward_body(peers, turned, weight, tokens, halo, cot, *refs):
    pieces, (mixed, back, head) = refs[:peers], refs[peers:]
    conv_out = matmul(turned[...], join_rows(pieces))
    conv, sig = gate_values(tokens, halo, weight)
    mixed[...] = (conv * sig * conv_out).astype(BF16)
    slope = sig * (1.0 + conv * (1.0 - sig))
    grad = cot[...].astype(F32) * conv_out * slope
    head[...] = grad[0:2]
    length = grad.shape[0]
    row = lax.broadcasted_iota(jnp.int32, grad.shape, 0)
    taps = weight[...]
    one_on = jnp.where(row < length - 1, pltpu.roll(grad, length - 1, 0), 0.0)
    two_on = jnp.where(row < length - 2, pltpu.roll(grad, length - 2, 0), 0.0)
    back[...] = taps[0:1] * grad + taps[1:2] * one_on + taps[2:3] * two_on


def forward_call(turned, weight, tokens, halo, cot, pieces):
    length, channels = tokens.shape
    peers, share = len(pieces), pieces[0].shape[0]
    width = min(channels, 128)
    return call(
        functools.partial(forward_body, peers),
        "forward_rows",
        (channels // width,),
        [whole(turned.shape), tile(3, width), tile(length, width), tile(2, width), tile(length, width)]
        + [tile(share, width)] * peers,
        [tile(length, width), tile(length, width), tile(2, width)],
        [struct((length, channels), BF16), struct((length, channels), F32), struct((2, channels), F32)],
        2 * length * length * channels,
        12 * length * channels + 2 * length * length,
        transcendentals=2 * length * channels,
    )(turned, weight, tokens, halo, cot, *pieces)


def partial_body(peers, turned, back, *refs):
    pieces, total = refs[:peers], refs[peers]
    total[...] = matmul(turned[...], join_rows(pieces)) + back[...]


def partial_call(turned, back, pieces):
    length, channels = back.shape
    peers, share = len(pieces), pieces[0].shape[0]
    width = min(channels, 256)
    depth = peers * share
    return call(
        functools.partial(partial_body, peers),
        "backward_part",
        (channels // width,),
        [pl.BlockSpec((length, depth), lambda c: (0, 0)), tile(length, width)]
        + [tile(share, width)] * peers,
        tile(length, width),
        struct((length, channels), F32),
        2 * length * depth * channels,
        8 * length * channels + 2 * length * depth + 2 * depth * channels,
    )(turned, back, *pieces)


def backward_body(peers, turned, weight, back, tail, *refs):
    pieces, grad = refs[:peers], refs[peers]
    total = matmul(turned[...], join_rows(pieces)) + back[...]
    taps, edge = weight[...], tail[...]
    length = total.shape[0]
    grad[...] = total.astype(BF16)
    last = total[length - 16 :]
    row = lax.broadcasted_iota(jnp.int32, last.shape, 0)
    extra = jnp.where(row == 15, taps[1:2] * edge[0:1] + taps[2:3] * edge[1:2], 0.0)
    extra = jnp.where(row == 14, taps[2:3] * edge[0:1], extra)
    grad[length - 16 :] = (last + extra).astype(BF16)


def backward_call(turned, weight, back, tail, pieces):
    length, channels = back.shape
    peers, share = len(pieces), pieces[0].shape[0]
    width = min(channels, 256)
    depth = peers * share
    last = turned.shape[1] // depth - 1
    return call(
        functools.partial(backward_body, peers),
        "backward_rows",
        (channels // width,),
        [pl.BlockSpec((length, depth), lambda c: (0, last)), tile(3, width), tile(length, width), tile(2, width)]
        + [tile(share, width)] * peers,
        tile(length, width),
        struct((length, channels), BF16),
        2 * length * depth * channels,
        6 * length * channels + 2 * length * depth + 2 * depth * channels,
    )(turned, weight, back, tail, *pieces)


def after(value, *others):
    return lax.optimization_barrier((value, *others))[0]


class Wire:
    DEPTH = 5

    def __init__(self):
        self.ended = []

    def exchange(self, block, mask):
        if len(self.ended) >= self.DEPTH:
            block = after(block, self.ended[-self.DEPTH])
        self.ended.append(exchange(block, mask))
        return self.ended[-1]


def on_device(tokens, short_weight, inner_factor, outer_factor, twiddle, kernel, cotangent):
    peers = lax.axis_size("seq")
    place, core = lax.axis_index("seq"), lax.axis_index("ch")
    row_count, block, channels = tokens.shape
    assert row_count == 1 and lax.axis_size("ch") == 2
    flat, cot = tokens.reshape(block, channels), cotangent.reshape(block, channels)
    share = inner_factor.shape[0]
    place_ref, core_ref = place.reshape(1).astype(jnp.int32), core.reshape(1).astype(jnp.int32)
    assert peers & (peers - 1) == 0
    far = peers // 2
    others = [far] + [m for pair in zip(range(1, far), range(far + 1, peers)) for m in pair]
    arrival = [0] + others
    wire = Wire()

    half = lax.dynamic_slice(inner_factor, (core * (share // 2), 0), (share // 2, block))
    mine = {far: wire.exchange(half, far)}
    for m in range(1, far):
        mine[m] = wire.exchange(half, m)
    preceding = shifted(flat[-2:], 1)
    for m in range(1, far):
        mine[far + m] = wire.exchange(mine[far], m)

    rows, spread, pieces = {0: inner_factor}, {}, []
    for m in others:
        piece, rows[m] = spread_peer_call(core_ref, mine[m], swap_cores(mine[m]), flat)
        pieces.append(piece)
        spread[m] = wire.exchange(piece, m)
    held = after(flat, pieces[-1])
    spread[0] = spread_own_call(inner_factor, held)

    factors = middle_factors(outer_factor, twiddle, place)
    in_order = [rows[m] for m in range(peers)]
    spread_cot = spread_gated_call(held, preceding, short_weight, cot, in_order)
    spread_cot = {m: wire.exchange(spread_cot[m], m) for m in others} | {0: spread_cot[0]}
    turned = turn_call([rows[m] for m in arrival])

    spread = [spread[m] for m in range(peers)]
    mid = middle_call(place_ref, factors, kernel, spread)
    rows_fwd = {m: wire.exchange(mid[m], m) for m in others} | {0: mid[0]}
    spread_cot[0] = after(spread_cot[0], mid[0])
    kernel_grad, mid = middle_call(place_ref, factors, kernel, [spread_cot[m] for m in range(peers)], spread)
    rows_bwd = {m: wire.exchange(mid[m], m) for m in others} | {0: mid[0]}

    mixer_out, back, head = forward_call(
        turned, short_weight, flat, preceding, cot, [rows_fwd[m] for m in arrival]
    )
    following = shifted(head, -1)
    late = max(1, peers // 4)
    back = partial_call(turned, back, [rows_bwd[m] for m in arrival[:-late]])
    token_grad = backward_call(turned, short_weight, back, following, [rows_bwd[m] for m in arrival[-late:]])
    return mixer_out.reshape(tokens.shape), token_grad.reshape(tokens.shape), kernel_grad


def solution(mesh):
    in_specs = (
        P(("grp", "seq"), None, "ch"),
        P(None, "ch"),
        P("seq", None),
        P(),
        P(None, "seq"),
        P(None, "seq", "ch"),
        P(("grp", "seq"), None, "ch"),
    )
    out_specs = (
        P(("grp", "seq"), None, "ch"),
        P(("grp", "seq"), None, "ch"),
        P("grp", "seq", "ch"),
    )
    return jax.shard_map(
        on_device, mesh=mesh, in_specs=in_specs, out_specs=out_specs, check_vma=False
    )
```

time: 278 us -> 221 us (0.79)
  waiting for transfers between devices: 126 us -> 85.3 us
  starting transfers between devices: 85.2 us -> 68.5 us
  local copies, waits for them, and re-layouts: 11.5 us -> 4.06 us
  Pallas kernels: 51.2 us -> 58 us
    ppermute x35, waiting for transfers between devices: 122 us -> 84.8 us  [exchange(): lax.ppermute(block, 'seq', [(i, i ^ mask) for i in range(lax.axis_size('s...]
    ppermute x35, starting transfers between devices: 76.5 us -> 60.2 us  [exchange(): lax.ppermute(block, 'seq', [(i, i ^ mask) for i in range(lax.axis_size('s...]
    unnamed x39 -> x20, local copies, waits for them, and re-layouts: 8.52 us -> 1.98 us
    pallas_call x4 -> x11, Pallas kernels: 20.8 us -> 25.9 us  [the longest x1 9.41 us: spread_gated_call(): call(functools.partial(spread_gated_body, peers), 'spread_gated', (channe...]
    ppermute x2, waiting for transfers between devices: 4.02 us -> 0.01 us  [shifted(): lax.ppermute(block, 'seq', [(i - distance, i) for i in devices if i - dis...]
    pallas_call x1, Pallas kernels: 8.11 us -> 10.9 us  [forward_call(): call(functools.partial(forward_body, peers), 'forward_rows', (channels //...]
  transfers between devices with their start and end apart: 44 -> 44, of which waited for: 19 -> 15; matrix products, arithmetic and copies ran while one was open for 2% -> 2% of each run, Pallas kernels for 9% -> 24%
where the time goes in v1:
time: 221 us; the launch traced here: 219 us
  waiting for transfers between devices  85.3 us (39%)
  starting transfers between devices  68.5 us (31%)
  Pallas kernels  58 us (26%)
  local copies, waits for them, and re-layouts  4.06 us (2%)
    ppermute x35, waiting for transfers between devices, exchange(): lax.ppermute(block, 'seq', [(i, i ^ mask) for i in range(lax.axis_size('s...  84.8 us
    ppermute x35, starting transfers between devices, exchange(): lax.ppermute(block, 'seq', [(i, i ^ mask) for i in range(lax.axis_size('s...  60.2 us
    pallas_call x2, Pallas kernels, middle_call(): call(functools.partial(middle_body, peers, side // peers, with_grad), 'mi...  16.4 us
    pallas_call x1, Pallas kernels, forward_call(): call(functools.partial(forward_body, peers), 'forward_rows', (channels //...  10.9 us
    pallas_call x1, Pallas kernels, spread_gated_call(): call(functools.partial(spread_gated_body, peers), 'spread_gated', (channe...  9.41 us
    pallas_call x7, Pallas kernels, spread_peer_call(): call(spread_peer_body, 'spread_peer', (channels // width,), [whole((half,...  8.7 us
    ppermute x2, starting transfers between devices, shifted(): lax.ppermute(block, 'seq', [(i - distance, i) for i in devices if i - dis...  7.32 us
    pallas_call x1, Pallas kernels, partial_call(): call(functools.partial(partial_body, peers), 'backward_part', (channels /...  5.83 us
  transfers between devices with their start and end apart: 44, of which 15 were waited for; matrix products, arithmetic and copies ran while one was open for 2% of the time, Pallas kernels for 24%

profile of v1, /device:TPU:14, one launch (start us, length us, event | category | flops | bytes accessed | tf_op | source)
XLA Modules:
  0.0 219.1 jit_solution(12917027414445784442)
XLA Ops:
  36.3 4.2 %collective-permute-start.14 = (bf16[2,1024]{1,0:T(2,128)(2,1)S(1)}, bf16[2,1024]{1,0:T(2,128)(2,1)S(1)}, u32[]{:S(2)}, u32[]{:S(2)}) collective-permute-start(bf16[2,1024]{1,0:T(2,128)(2,1)S(1)} %slice_bitcast_fusion), channel_id=1, source_target_pairs={{0,2},{2,4},{4,6},{6,8},{8,10},{10,12},{12,14},{1,3},{3,5},{5,7},{... | collective-permute-start | bytes 12296 | tf_op jit(solution)/shard_map/ppermute | solution.py:20
  46.9 9.4 %spread_gated.1 = (bf16[128,1024]{1,0:T(8,128)(2,1)S(1)}, bf16[128,1024]{1,0:T(8,128)(2,1)S(1)}, bf16[128,1024]{1,0:T(8,128)(2,1)S(1)}, bf16[128,1024]{1,0:T(8,1...) custom-call(bf16[1024,1024]{1,0:T(8,128)(2,1)} %bitcast.17, ...), custom_call_target="tpu_custom_call" | custom-call | flops 2147483648 | bytes 8388608 | tf_op jit(solution)/shard_map/spread_gated/pallas_call | solution.py:130
  56.5 4.3 %collective-permute-start.18 = (bf16[128,1024]{1,0:T(8,128)(2,1)S(1)}, bf16[128,1024]{1,0:T(8,128)(2,1)S(1)}, u32[]{:S(2)}, u32[]{:S(2)}) collective-permute-start(bf16[128,1024]{1,0:T(8,128)(2,1)S(1)} %get-tuple-element.95), channel_id=1, source_target_pairs={{0,6},{2,4},{4,2},{6,0},{8,14},{10,12},{12,10},{14,8},{1,7},{3,5},... | collective-permute-start | bytes 786440 | tf_op jit(solution)/shard_map/ppermute | solution.py:15
  63.2 9.2 %collective-permute-done.20.refs_6_.refs_14_ = bf16[128,1024]{1,0:T(8,128)(2,1)S(1)} collective-permute-done((bf16[128,1024]{1,0:T(8,128)(2,1)S(1)}, bf16[128,1024]{1,0:T(8,128)(2,1)S(1)}, u32[]{:S(2)}, u32[]{:S(2)}) %collective-permute-start.20) | collective-permute-done | bytes 262176 | tf_op jit(solution)/shard_map/ppermute | solution.py:15
  72.4 4.0 %collective-permute-start.22 = (bf16[128,1024]{1,0:T(8,128)(2,1)S(1)}, bf16[128,1024]{1,0:T(8,128)(2,1)S(1)}, u32[]{:S(2)}, u32[]{:S(2)}) collective-permute-start(bf16[128,1024]{1,0:T(8,128)(2,1)S(1)} %get-tuple-element.104), channel_id=1, source_target_pairs={{0,10},{2,8},{4,14},{6,12},{8,2},{10,0},{12,6},{14,4},{1,11},{3,9}... | collective-permute-start | bytes 786440 | tf_op jit(solution)/shard_map/ppermute | solution.py:15
  77.2 14.6 %collective-permute-done.21.refs_7_.refs_15_ = bf16[128,1024]{1,0:T(8,128)(2,1)S(1)} collective-permute-done((bf16[128,1024]{1,0:T(8,128)(2,1)S(1)}, bf16[128,1024]{1,0:T(8,128)(2,1)S(1)}, u32[]{:S(2)}, u32[]{:S(2)}) %collective-permute-start.21) | collective-permute-done | bytes 262176 | tf_op jit(solution)/shard_map/ppermute | solution.py:15
  92.2 7.5 %middle.1 = (bf16[128,1024]{1,0:T(8,128)(2,1)S(1)}, bf16[128,1024]{1,0:T(8,128)(2,1)S(1)}, bf16[128,1024]{1,0:T(8,128)(2,1)S(1)}, bf16[128,1024]{1,0:T(8,128)(2,...) custom-call(s32[1]{0:T(128)} %bitcast.4.place, ...), custom_call_target="tpu_custom_call" | custom-call | flops 2684354560 | bytes 8388608 | tf_op jit(solution)/shard_map/middle/pallas_call | solution.py:201
  99.8 5.0 %collective-permute-done.28.refs_4_ = bf16[128,1024]{1,0:T(8,128)(2,1)S(1)} collective-permute-done((bf16[128,1024]{1,0:T(8,128)(2,1)S(1)}, bf16[128,1024]{1,0:T(8,128)(2,1)S(1)}, u32[]{:S(2)}, u32[]{:S(2)}) %collective-permute-start.28) | collective-permute-done | bytes 262176 | tf_op jit(solution)/shard_map/ppermute | solution.py:15
  104.8 3.8 %collective-permute-start.29 = (bf16[128,1024]{1,0:T(8,128)(2,1)S(1)}, bf16[128,1024]{1,0:T(8,128)(2,1)S(1)}, u32[]{:S(2)}, u32[]{:S(2)}) collective-permute-start(bf16[128,1024]{1,0:T(8,128)(2,1)S(1)} %get-tuple-element.118), channel_id=1, source_target_pairs={{0,6},{2,4},{4,2},{6,0},{8,14},{10,12},{12,10},{14,8},{1,7},{3,5},... | collective-permute-start | bytes 786440 | tf_op jit(solution)/shard_map/ppermute | solution.py:15
  110.5 3.2 %collective-permute-start.23 = (bf16[128,1024]{1,0:T(8,128)(2,1)S(1)}, bf16[128,1024]{1,0:T(8,128)(2,1)S(1)}, u32[]{:S(2)}, u32[]{:S(2)}) collective-permute-start(bf16[128,1024]{1,0:T(8,128)(2,1)S(1)} %get-tuple-element.105), channel_id=1, source_target_pairs={{0,8},{2,10},{4,12},{6,14},{8,0},{10,2},{12,4},{14,6},{1,9},{3,11}... | collective-permute-start | bytes 786440 | tf_op jit(solution)/shard_map/ppermute | solution.py:15
  115.3 20.0 %collective-permute-done.26.refs_6_ = bf16[128,1024]{1,0:T(8,128)(2,1)S(1)} collective-permute-done((bf16[128,1024]{1,0:T(8,128)(2,1)S(1)}, bf16[128,1024]{1,0:T(8,128)(2,1)S(1)}, u32[]{:S(2)}, u32[]{:S(2)}) %collective-permute-start.26) | collective-permute-done | bytes 262176 | tf_op jit(solution)/shard_map/ppermute | solution.py:15
  135.9 4.0 %collective-permute-start.30 = (bf16[128,1024]{1,0:T(8,128)(2,1)S(1)}, bf16[128,1024]{1,0:T(8,128)(2,1)S(1)}, u32[]{:S(2)}, u32[]{:S(2)}) collective-permute-start(bf16[128,1024]{1,0:T(8,128)(2,1)S(1)} %get-tuple-element.119), channel_id=1, source_target_pairs={{0,4},{2,6},{4,0},{6,2},{8,12},{10,14},{12,8},{14,10},{1,5},{3,7},... | collective-permute-start | bytes 786440 | tf_op jit(solution)/shard_map/ppermute | solution.py:15
  142.7 6.4 %collective-permute-start.34 = (bf16[128,1024]{1,0:T(8,128)(2,1)S(1)}, bf16[128,1024]{1,0:T(8,128)(2,1)S(1)}, u32[]{:S(2)}, u32[]{:S(2)}) collective-permute-start(bf16[128,1024]{1,0:T(8,128)(2,1)S(1)} %get-tuple-element.127), channel_id=1, source_target_pairs={{0,6},{2,4},{4,2},{6,0},{8,14},{10,12},{12,10},{14,8},{1,7},{3,5},... | collective-permute-start | bytes 786440 | tf_op jit(solution)/shard_map/ppermute | solution.py:15
  149.1 8.9 %middle_grad.1 = (bf16[8,128,1024]{2,1,0:T(8,128)(2,1)}, bf16[128,1024]{1,0:T(8,128)(2,1)S(1)}, bf16[128,1024]{1,0:T(8,128)(2,1)S(1)}, bf16[128,1024]{1,0:T(8,12...) custom-call(s32[1]{0:T(128)} %bitcast.4.place, ...), custom_call_target="tpu_custom_call" | custom-call | flops 3758096384 | bytes 12582912 | tf_op jit(solution)/shard_map/middle_grad/pallas_call | solution.py:201
  158.0 3.6 %collective-permute-done.27.refs_3_ = bf16[128,1024]{1,0:T(8,128)(2,1)S(1)} collective-permute-done((bf16[128,1024]{1,0:T(8,128)(2,1)S(1)}, bf16[128,1024]{1,0:T(8,128)(2,1)S(1)}, u32[]{:S(2)}, u32[]{:S(2)}) %collective-permute-start.27) | collective-permute-done | bytes 262176 | tf_op jit(solution)/shard_map/ppermute | solution.py:15
  161.5 4.0 %collective-permute-start.36 = (bf16[128,1024]{1,0:T(8,128)(2,1)S(1)}, bf16[128,1024]{1,0:T(8,128)(2,1)S(1)}, u32[]{:S(2)}, u32[]{:S(2)}) collective-permute-start(bf16[128,1024]{1,0:T(8,128)(2,1)S(1)} %get-tuple-element.136), channel_id=1, source_target_pairs={{0,8},{2,10},{4,12},{6,14},{8,0},{10,2},{12,4},{14,6},{1,9},{3,11}... | collective-permute-start | bytes 786440 | tf_op jit(solution)/shard_map/ppermute | solution.py:15
  167.0 3.4 %collective-permute-start.39 = (bf16[128,1024]{1,0:T(8,128)(2,1)S(1)}, bf16[128,1024]{1,0:T(8,128)(2,1)S(1)}, u32[]{:S(2)}, u32[]{:S(2)}) collective-permute-start(bf16[128,1024]{1,0:T(8,128)(2,1)S(1)} %get-tuple-element.142), channel_id=1, source_target_pairs={{0,4},{2,6},{4,0},{6,2},{8,12},{10,14},{12,8},{14,10},{1,5},{3,7},... | collective-permute-start | bytes 786440 | tf_op jit(solution)/shard_map/ppermute | solution.py:15
  170.4 11.0 %collective-permute-done.35.refs_7_ = bf16[128,1024]{1,0:T(8,128)(2,1)S(1)} collective-permute-done((bf16[128,1024]{1,0:T(8,128)(2,1)S(1)}, bf16[128,1024]{1,0:T(8,128)(2,1)S(1)}, u32[]{:S(2)}, u32[]{:S(2)}) %collective-permute-start.35) | collective-permute-done | bytes 262176 | tf_op jit(solution)/shard_map/ppermute | solution.py:15
  182.7 7.0 %collective-permute-done.36.refs_1_ = bf16[128,1024]{1,0:T(8,128)(2,1)S(1)} collective-permute-done((bf16[128,1024]{1,0:T(8,128)(2,1)S(1)}, bf16[128,1024]{1,0:T(8,128)(2,1)S(1)}, u32[]{:S(2)}, u32[]{:S(2)}) %collective-permute-start.36) | collective-permute-done | bytes 262176 | tf_op jit(solution)/shard_map/ppermute | solution.py:15
  189.7 4.5 %collective-permute-start.42 = (bf16[128,1024]{1,0:T(8,128)(2,1)S(1)}, bf16[128,1024]{1,0:T(8,128)(2,1)S(1)}, u32[]{:S(2)}, u32[]{:S(2)}) collective-permute-start(bf16[128,1024]{1,0:T(8,128)(2,1)S(1)} %get-tuple-element.147), channel_id=1, source_target_pairs={{0,6},{2,4},{4,2},{6,0},{8,14},{10,12},{12,10},{14,8},{1,7},{3,5},... | collective-permute-start | bytes 786440 | tf_op jit(solution)/shard_map/ppermute | solution.py:15
  194.5 10.9 %forward_rows.1 = (bf16[1024,1024]{1,0:T(8,128)(2,1)}, f32[1024,1024]{1,0:T(8,128)}, f32[2,1024]{1,0:T(2,128)S(1)}) custom-call(bf16[1024,1024]{1,0:T(8,128)(2,1)S(1)} %turn.1.turned, f32[3,1024]{1,0:T(4,128)S(1)} %copy-done.8, bf16[1024,1024]{1,0:T(8,128)(2,1)} %bitcast.18, bf16[2,1024]{1,0:T(2,128)(2,1)S(1)} %collective-permute-done.14.halo, ...), custom_call_target="tpu_custom_call" | custom-call | flops 2147483648 | bytes 14680064 | tf_op jit(solution)/shard_map/forward_rows/pallas_call | solution.py:258
  205.5 3.1 %collective-permute-start.41 = (f32[2,1024]{1,0:T(2,128)S(1)}, f32[2,1024]{1,0:T(2,128)S(1)}, u32[]{:S(2)}, u32[]{:S(2)}) collective-permute-start(f32[2,1024]{1,0:T(2,128)S(1)} %get-tuple-element.145), channel_id=1, source_target_pairs={{2,0},{4,2},{6,4},{8,6},{10,8},{12,10},{14,12},{3,1},{5,3},{7,5},{... | collective-permute-start | bytes 24584 | tf_op jit(solution)/shard_map/ppermute | solution.py:20
  208.6 5.8 %backward_part.1.back = f32[1024,1024]{1,0:T(8,128)} custom-call(bf16[1024,1024]{1,0:T(8,128)(2,1)S(1)} %turn.1.turned, f32[1024,1024]{1,0:T(8,128)} %get-tuple-element.131.back, bf16[128,1024]{1,0:T(8,128)(2,1)S(1)} %get-tuple-element.134.refs_0_, bf16[128,1024]{1,0:T(8,128)(2,1)S(1)} %collective-permute-done.36.refs_1_, ...), custom_call_target="tpu_custom_call" | custom-call | flops 1610612736 | bytes 11534336 | tf_op jit(solution)/shard_map/backward_part/pallas_call | solution.py:282
  214.4 4.7 %backward_rows.1 = bf16[1024,1024]{1,0:T(8,128)(2,1)} custom-call(bf16[1024,1024]{1,0:T(8,128)(2,1)S(1)} %turn.1.turned, f32[3,1024]{1,0:T(4,128)S(1)} %copy-done.8, f32[1024,1024]{1,0:T(8,128)} %backward_part.1.back, f32[2,1024]{1,0:T(2,128)S(1)} %collective-permute-done.41.tail, bf16[128,1024]{1,0:T(8,128)(2,1)S(1)} %collective-permute-done.42.refs_0_, ...), custom_call_target="tpu_custom_call" | custom-call | flops 536870912 | bytes 7340032 | tf_op jit(solution)/shard_map/backward_rows/pallas_call | solution.py:314
  (114 shorter events, 55.7 us)
Async XLA Ops:
  29.3 27.1 %collective-permute-start.17 = (bf16[128,1024]{1,0:T(8,128)(2,1)S(1)}, bf16[128,1024]{1,0:T(8,128)(2,1)S(1)}, u32[]{:S(2)}, u32[]{:S(2)}) collective-permute-start(bf16[128,1024]{1,0:T(8,128)(2,1)S(1)} %get-tuple-element.94), channel_id=1, source_target_pairs={{0,8},{2,10},{4,12},{6,14},{8,0},{10,2},{12,4},{14,6},{1,9},{3,11}... | collective-permute-start | bytes 786440 | tf_op jit(solution)/shard_map/ppermute | solution.py:15
  34.8 26.0 %collective-permute-start.16 = (bf16[128,1024]{1,0:T(8,128)(2,1)S(1)}, bf16[128,1024]{1,0:T(8,128)(2,1)S(1)}, u32[]{:S(2)}, u32[]{:S(2)}) collective-permute-start(bf16[128,1024]{1,0:T(8,128)(2,1)S(1)} %get-tuple-element.91), channel_id=1, source_target_pairs={{0,4},{2,6},{4,0},{6,2},{8,12},{10,14},{12,8},{14,10},{1,5},{3,7},... | collective-permute-start | bytes 786440 | tf_op jit(solution)/shard_map/ppermute | solution.py:15
  41.8 30.6 %collective-permute-start.19 = (bf16[128,1024]{1,0:T(8,128)(2,1)S(1)}, bf16[128,1024]{1,0:T(8,128)(2,1)S(1)}, u32[]{:S(2)}, u32[]{:S(2)}) collective-permute-start(bf16[128,1024]{1,0:T(8,128)(2,1)S(1)} %get-tuple-element.97), channel_id=1, source_target_pairs={{0,10},{2,8},{4,14},{6,12},{8,2},{10,0},{12,6},{14,4},{1,11},{3,9}... | collective-permute-start | bytes 786440 | tf_op jit(solution)/shard_map/ppermute | solution.py:15
  44.1 28.3 %collective-permute-start.20 = (bf16[128,1024]{1,0:T(8,128)(2,1)S(1)}, bf16[128,1024]{1,0:T(8,128)(2,1)S(1)}, u32[]{:S(2)}, u32[]{:S(2)}) collective-permute-start(bf16[128,1024]{1,0:T(8,128)(2,1)S(1)} %get-tuple-element.99), channel_id=1, source_target_pairs={{0,12},{2,14},{4,8},{6,10},{8,4},{10,6},{12,0},{14,2},{1,13},{3,15... | collective-permute-start | bytes 786440 | tf_op jit(solution)/shard_map/ppermute | solution.py:15
  56.4 35.4 %collective-permute-start.21 = (bf16[128,1024]{1,0:T(8,128)(2,1)S(1)}, bf16[128,1024]{1,0:T(8,128)(2,1)S(1)}, u32[]{:S(2)}, u32[]{:S(2)}) collective-permute-start(bf16[128,1024]{1,0:T(8,128)(2,1)S(1)} %get-tuple-element.100), channel_id=1, source_target_pairs={{0,14},{2,12},{4,10},{6,8},{8,6},{10,4},{12,2},{14,0},{1,15},{3,13... | collective-permute-start | bytes 786440 | tf_op jit(solution)/shard_map/ppermute | solution.py:15
  60.8 31.0 %collective-permute-start.31 = (bf16[128,1024]{1,0:T(8,128)(2,1)S(1)}, bf16[128,1024]{1,0:T(8,128)(2,1)S(1)}, u32[]{:S(2)}, u32[]{:S(2)}) collective-permute-start(bf16[128,1024]{1,0:T(8,128)(2,1)S(1)} %get-tuple-element.123), channel_id=1, source_target_pairs={{0,2},{2,0},{4,6},{6,4},{8,10},{10,8},{12,14},{14,12},{1,3},{3,1},... | collective-permute-start | bytes 786440 | tf_op jit(solution)/shard_map/ppermute | solution.py:15
  72.4 32.4 %collective-permute-start.28 = (bf16[128,1024]{1,0:T(8,128)(2,1)S(1)}, bf16[128,1024]{1,0:T(8,128)(2,1)S(1)}, u32[]{:S(2)}, u32[]{:S(2)}) collective-permute-start(bf16[128,1024]{1,0:T(8,128)(2,1)S(1)} %get-tuple-element.117), channel_id=1, source_target_pairs={{0,8},{2,10},{4,12},{6,14},{8,0},{10,2},{12,4},{14,6},{1,9},{3,11}... | collective-permute-start | bytes 786440 | tf_op jit(solution)/shard_map/ppermute | solution.py:15
  72.4 38.1 %collective-permute-start.22 = (bf16[128,1024]{1,0:T(8,128)(2,1)S(1)}, bf16[128,1024]{1,0:T(8,128)(2,1)S(1)}, u32[]{:S(2)}, u32[]{:S(2)}) collective-permute-start(bf16[128,1024]{1,0:T(8,128)(2,1)S(1)} %get-tuple-element.104), channel_id=1, source_target_pairs={{0,10},{2,8},{4,14},{6,12},{8,2},{10,0},{12,6},{14,4},{1,11},{3,9}... | collective-permute-start | bytes 786440 | tf_op jit(solution)/shard_map/ppermute | solution.py:15
  76.4 37.3 %collective-permute-start.24 = (bf16[128,1024]{1,0:T(8,128)(2,1)S(1)}, bf16[128,1024]{1,0:T(8,128)(2,1)S(1)}, u32[]{:S(2)}, u32[]{:S(2)}) collective-permute-start(bf16[128,1024]{1,0:T(8,128)(2,1)S(1)} %get-tuple-element.108), channel_id=1, source_target_pairs={{0,4},{2,6},{4,0},{6,2},{8,12},{10,14},{12,8},{14,10},{1,5},{3,7},... | collective-permute-start | bytes 786440 | tf_op jit(solution)/shard_map/ppermute | solution.py:15
  91.8 43.5 %collective-permute-start.32 = (bf16[128,1024]{1,0:T(8,128)(2,1)S(1)}, bf16[128,1024]{1,0:T(8,128)(2,1)S(1)}, u32[]{:S(2)}, u32[]{:S(2)}) collective-permute-start(bf16[128,1024]{1,0:T(8,128)(2,1)S(1)} %get-tuple-element.124), channel_id=1, source_target_pairs={{0,14},{2,12},{4,10},{6,8},{8,6},{10,4},{12,2},{14,0},{1,15},{3,13... | collective-permute-start | bytes 786440 | tf_op jit(solution)/shard_map/ppermute | solution.py:15
  91.8 43.5 %collective-permute-start.26 = (bf16[128,1024]{1,0:T(8,128)(2,1)S(1)}, bf16[128,1024]{1,0:T(8,128)(2,1)S(1)}, u32[]{:S(2)}, u32[]{:S(2)}) collective-permute-start(bf16[128,1024]{1,0:T(8,128)(2,1)S(1)} %get-tuple-element.112), channel_id=1, source_target_pairs={{0,12},{2,14},{4,8},{6,10},{8,4},{10,6},{12,0},{14,2},{1,13},{3,15... | collective-permute-start | bytes 786440 | tf_op jit(solution)/shard_map/ppermute | solution.py:15
  104.8 31.1 %collective-permute-start.29 = (bf16[128,1024]{1,0:T(8,128)(2,1)S(1)}, bf16[128,1024]{1,0:T(8,128)(2,1)S(1)}, u32[]{:S(2)}, u32[]{:S(2)}) collective-permute-start(bf16[128,1024]{1,0:T(8,128)(2,1)S(1)} %get-tuple-element.118), channel_id=1, source_target_pairs={{0,6},{2,4},{4,2},{6,0},{8,14},{10,12},{12,10},{14,8},{1,7},{3,5},... | collective-permute-start | bytes 786440 | tf_op jit(solution)/shard_map/ppermute | solution.py:15
  110.5 32.3 %collective-permute-start.23 = (bf16[128,1024]{1,0:T(8,128)(2,1)S(1)}, bf16[128,1024]{1,0:T(8,128)(2,1)S(1)}, u32[]{:S(2)}, u32[]{:S(2)}) collective-permute-start(bf16[128,1024]{1,0:T(8,128)(2,1)S(1)} %get-tuple-element.105), channel_id=1, source_target_pairs={{0,8},{2,10},{4,12},{6,14},{8,0},{10,2},{12,4},{14,6},{1,9},{3,11}... | collective-permute-start | bytes 786440 | tf_op jit(solution)/shard_map/ppermute | solution.py:15
  113.7 35.4 %collective-permute-start.25 = (bf16[128,1024]{1,0:T(8,128)(2,1)S(1)}, bf16[128,1024]{1,0:T(8,128)(2,1)S(1)}, u32[]{:S(2)}, u32[]{:S(2)}) collective-permute-start(bf16[128,1024]{1,0:T(8,128)(2,1)S(1)} %get-tuple-element.109), channel_id=1, source_target_pairs={{0,2},{2,0},{4,6},{6,4},{8,10},{10,8},{12,14},{14,12},{1,3},{3,1},... | collective-permute-start | bytes 786440 | tf_op jit(solution)/shard_map/ppermute | solution.py:15
  135.3 31.1 %collective-permute-start.33 = (bf16[128,1024]{1,0:T(8,128)(2,1)S(1)}, bf16[128,1024]{1,0:T(8,128)(2,1)S(1)}, u32[]{:S(2)}, u32[]{:S(2)}) collective-permute-start(bf16[128,1024]{1,0:T(8,128)(2,1)S(1)} %get-tuple-element.125), channel_id=1, source_target_pairs={{0,12},{2,14},{4,8},{6,10},{8,4},{10,6},{12,0},{14,2},{1,13},{3,15... | collective-permute-start | bytes 786440 | tf_op jit(solution)/shard_map/ppermute | solution.py:15
  135.9 25.6 %collective-permute-start.27 = (bf16[128,1024]{1,0:T(8,128)(2,1)S(1)}, bf16[128,1024]{1,0:T(8,128)(2,1)S(1)}, u32[]{:S(2)}, u32[]{:S(2)}) collective-permute-start(bf16[128,1024]{1,0:T(8,128)(2,1)S(1)} %get-tuple-element.113), channel_id=1, source_target_pairs={{0,10},{2,8},{4,14},{6,12},{8,2},{10,0},{12,6},{14,4},{1,11},{3,9}... | collective-permute-start | bytes 786440 | tf_op jit(solution)/shard_map/ppermute | solution.py:15
  135.9 29.7 %collective-permute-start.30 = (bf16[128,1024]{1,0:T(8,128)(2,1)S(1)}, bf16[128,1024]{1,0:T(8,128)(2,1)S(1)}, u32[]{:S(2)}, u32[]{:S(2)}) collective-permute-start(bf16[128,1024]{1,0:T(8,128)(2,1)S(1)} %get-tuple-element.119), channel_id=1, source_target_pairs={{0,4},{2,6},{4,0},{6,2},{8,12},{10,14},{12,8},{14,10},{1,5},{3,7},... | collective-permute-start | bytes 786440 | tf_op jit(solution)/shard_map/ppermute | solution.py:15
  149.1 32.3 %collective-permute-start.35 = (bf16[128,1024]{1,0:T(8,128)(2,1)S(1)}, bf16[128,1024]{1,0:T(8,128)(2,1)S(1)}, u32[]{:S(2)}, u32[]{:S(2)}) collective-permute-start(bf16[128,1024]{1,0:T(8,128)(2,1)S(1)} %get-tuple-element.129), channel_id=1, source_target_pairs={{0,14},{2,12},{4,10},{6,8},{8,6},{10,4},{12,2},{14,0},{1,15},{3,13... | collective-permute-start | bytes 786440 | tf_op jit(solution)/shard_map/ppermute | solution.py:15
  161.5 28.1 %collective-permute-start.36 = (bf16[128,1024]{1,0:T(8,128)(2,1)S(1)}, bf16[128,1024]{1,0:T(8,128)(2,1)S(1)}, u32[]{:S(2)}, u32[]{:S(2)}) collective-permute-start(bf16[128,1024]{1,0:T(8,128)(2,1)S(1)} %get-tuple-element.136), channel_id=1, source_target_pairs={{0,8},{2,10},{4,12},{6,14},{8,0},{10,2},{12,4},{14,6},{1,9},{3,11}... | collective-permute-start | bytes 786440 | tf_op jit(solution)/shard_map/ppermute | solution.py:15
  165.6 28.6 %collective-permute-start.37 = (bf16[128,1024]{1,0:T(8,128)(2,1)S(1)}, bf16[128,1024]{1,0:T(8,128)(2,1)S(1)}, u32[]{:S(2)}, u32[]{:S(2)}) collective-permute-start(bf16[128,1024]{1,0:T(8,128)(2,1)S(1)} %get-tuple-element.138), channel_id=1, source_target_pairs={{0,2},{2,0},{4,6},{6,4},{8,10},{10,8},{12,14},{14,12},{1,3},{3,1},... | collective-permute-start | bytes 786440 | tf_op jit(solution)/shard_map/ppermute | solution.py:15
  166.4 39.1 %collective-permute-start.38 = (bf16[128,1024]{1,0:T(8,128)(2,1)S(1)}, bf16[128,1024]{1,0:T(8,128)(2,1)S(1)}, u32[]{:S(2)}, u32[]{:S(2)}) collective-permute-start(bf16[128,1024]{1,0:T(8,128)(2,1)S(1)} %get-tuple-element.140), channel_id=1, source_target_pairs={{0,10},{2,8},{4,14},{6,12},{8,2},{10,0},{12,6},{14,4},{1,11},{3,9}... | collective-permute-start | bytes 786440 | tf_op jit(solution)/shard_map/ppermute | solution.py:15
  167.0 41.5 %collective-permute-start.39 = (bf16[128,1024]{1,0:T(8,128)(2,1)S(1)}, bf16[128,1024]{1,0:T(8,128)(2,1)S(1)}, u32[]{:S(2)}, u32[]{:S(2)}) collective-permute-start(bf16[128,1024]{1,0:T(8,128)(2,1)S(1)} %get-tuple-element.142), channel_id=1, source_target_pairs={{0,4},{2,6},{4,0},{6,2},{8,12},{10,14},{12,8},{14,10},{1,5},{3,7},... | collective-permute-start | bytes 786440 | tf_op jit(solution)/shard_map/ppermute | solution.py:15
  181.4 27.1 %collective-permute-start.40 = (bf16[128,1024]{1,0:T(8,128)(2,1)S(1)}, bf16[128,1024]{1,0:T(8,128)(2,1)S(1)}, u32[]{:S(2)}, u32[]{:S(2)}) collective-permute-start(bf16[128,1024]{1,0:T(8,128)(2,1)S(1)} %get-tuple-element.144), channel_id=1, source_target_pairs={{0,12},{2,14},{4,8},{6,10},{8,4},{10,6},{12,0},{14,2},{1,13},{3,15... | collective-permute-start | bytes 786440 | tf_op jit(solution)/shard_map/ppermute | solution.py:15
  189.7 24.7 %collective-permute-start.42 = (bf16[128,1024]{1,0:T(8,128)(2,1)S(1)}, bf16[128,1024]{1,0:T(8,128)(2,1)S(1)}, u32[]{:S(2)}, u32[]{:S(2)}) collective-permute-start(bf16[128,1024]{1,0:T(8,128)(2,1)S(1)} %get-tuple-element.147), channel_id=1, source_target_pairs={{0,6},{2,4},{4,2},{6,0},{8,14},{10,12},{12,10},{14,8},{1,7},{3,5},... | collective-permute-start | bytes 786440 | tf_op jit(solution)/shard_map/ppermute | solution.py:15
  (30 other events, 417.9 us)

commit v2 on v1

--- a/solution.py
+++ b/solution.py
@@ -8,7 +8,8 @@
 from jax.sharding import PartitionSpec as P
 
 BF16, F32 = jnp.bfloat16, jnp.float32
-VMEM_LIMIT = 48 * 1024 * 1024
+MIB = 1024 * 1024
+VMEM_LIMIT = 48 * MIB
 
 
 def exchange(block, mask):
@@ -269,58 +270,75 @@
     )(turned, weight, tokens, halo, cot, *pieces)
 
 
-def partial_body(peers, turned, back, *refs):
+def in_vmem(count):
+    return [pl.BlockSpec(memory_space=pltpu.VMEM)] * count
+
+
+def partial_body(peers, width, turned, back, *refs):
     pieces, total = refs[:peers], refs[peers]
-    total[...] = matmul(turned[...], join_rows(pieces)) + back[...]
+    depth = peers * pieces[0].shape[0]
+    for c in range(total.shape[1] // width):
+        part = slice(c * width, (c + 1) * width)
+        stacked = jnp.concatenate([piece[:, part] for piece in pieces], axis=0)
+        total[:, part] = matmul(turned[:, :depth], stacked) + back[:, part]
 
 
 def partial_call(turned, back, pieces):
     length, channels = back.shape
-    peers, share = len(pieces), pieces[0].shape[0]
-    width = min(channels, 256)
-    depth = peers * share
-    return call(
-        functools.partial(partial_body, peers),
-        "backward_part",
-        (channels // width,),
-        [pl.BlockSpec((length, depth), lambda c: (0, 0)), tile(length, width)]
-        + [tile(share, width)] * peers,
-        tile(length, width),
-        struct((length, channels), F32),
-        2 * length * depth * channels,
-        8 * length * channels + 2 * length * depth + 2 * depth * channels,
+    depth = len(pieces) * pieces[0].shape[0]
+    return pl.pallas_call(
+        functools.partial(partial_body, len(pieces), min(channels, 256)),
+        name="backward_part",
+        in_specs=in_vmem(2 + len(pieces)),
+        out_specs=in_vmem(1)[0],
+        out_shape=struct((length, channels), F32),
+        compiler_params=pltpu.CompilerParams(vmem_limit_bytes=8 * MIB),
+        cost_estimate=pl.CostEstimate(
+            flops=2 * length * depth * channels, bytes_accessed=8 * length * channels, transcendentals=0
+        ),
     )(turned, back, *pieces)
 
 
-def backward_body(peers, turned, weight, back, tail, *refs):
-    pieces, grad = refs[:peers], refs[peers]
-    total = matmul(turned[...], join_rows(pieces)) + back[...]
-    taps, edge = weight[...], tail[...]
-    length = total.shape[0]
-    grad[...] = total.astype(BF16)
-    last = total[length - 16 :]
-    row = lax.broadcasted_iota(jnp.int32, last.shape, 0)
-    extra = jnp.where(row == 15, taps[1:2] * edge[0:1] + taps[2:3] * edge[1:2], 0.0)
-    extra = jnp.where(row == 14, taps[2:3] * edge[0:1], extra)
-    grad[length - 16 :] = (last + extra).astype(BF16)
+def backward_body(peers, width, turned, weight, back, tail, *refs):
+    pieces, out, made, sems = refs[:peers], refs[peers], refs[peers + 1], refs[peers + 2]
+    length, channels = made.shape
+    depth = peers * pieces[0].shape[0]
+    copies = []
+    for c in range(channels // width):
+        part = slice(c * width, (c + 1) * width)
+        stacked = jnp.concatenate([piece[:, part] for piece in pieces], axis=0)
+        total = matmul(turned[:, turned.shape[1] - depth :], stacked) + back[:, part]
+        taps, edge = weight[:, part], tail[:, part]
+        made[: length - 16, part] = total[: length - 16].astype(BF16)
+        last = total[length - 16 :]
+        row = lax.broadcasted_iota(jnp.int32, last.shape, 0)
+        extra = jnp.where(row == 15, taps[1:2] * edge[0:1] + taps[2:3] * edge[1:2], 0.0)
+        extra = jnp.where(row == 14, taps[2:3] * edge[0:1], extra)
+        made[length - 16 :, part] = (last + extra).astype(BF16)
+        copies.append(pltpu.make_async_copy(made.at[:, part], out.at[:, part], sems.at[c]))
+        copies[-1].start()
+    for copy in copies:
+        copy.wait()
 
 
 def backward_call(turned, weight, back, tail, pieces):
     length, channels = back.shape
-    peers, share = len(pieces), pieces[0].shape[0]
+    peers, depth = len(pieces), len(pieces) * pieces[0].shape[0]
     width = min(channels, 256)
-    depth = peers * share
-    last = turned.shape[1] // depth - 1
-    return call(
-        functools.partial(backward_body, peers),
-        "backward_rows",
-        (channels // width,),
-        [pl.BlockSpec((length, depth), lambda c: (0, last)), tile(3, width), tile(length, width), tile(2, width)]
-        + [tile(share, width)] * peers,
-        tile(length, width),
-        struct((length, channels), BF16),
-        2 * length * depth * channels,
-        6 * length * channels + 2 * length * depth + 2 * depth * channels,
+    return pl.pallas_call(
+        functools.partial(backward_body, peers, width),
+        name="backward_rows",
+        in_specs=in_vmem(4 + peers),
+        out_specs=pl.BlockSpec(memory_space=pl.ANY),
+        out_shape=struct((length, channels), BF16),
+        scratch_shapes=[
+            pltpu.VMEM((length, channels), BF16),
+            pltpu.SemaphoreType.DMA((channels // width,)),
+        ],
+        compiler_params=pltpu.CompilerParams(vmem_limit_bytes=8 * MIB),
+        cost_estimate=pl.CostEstimate(
+            flops=2 * length * depth * channels, bytes_accessed=6 * length * channels, transcendentals=0
+        ),
     )(turned, weight, back, tail, *pieces)
 
 
@@ -382,12 +400,15 @@
     rows_fwd = {m: wire.exchange(mid[m], m) for m in others} | {0: mid[0]}
     spread_cot[0] = after(spread_cot[0], mid[0])
     kernel_grad, mid = middle_call(place_ref, factors, kernel, [spread_cot[m] for m in range(peers)], spread)
-    rows_bwd = {m: wire.exchange(mid[m], m) for m in others} | {0: mid[0]}
-
+    rows_bwd = {0: mid[0]}
+    for m in others[:-1]:
+        rows_bwd[m] = wire.exchange(mid[m], m)
+    rows_fwd[0] = after(rows_fwd[0], rows_bwd[others[0]])
     mixer_out, back, head = forward_call(
         turned, short_weight, flat, preceding, cot, [rows_fwd[m] for m in arrival]
     )
     following = shifted(head, -1)
+    rows_bwd[others[-1]] = wire.exchange(after(mid[others[-1]], head), others[-1])
     late = max(1, peers // 4)
     back = partial_call(turned, back, [rows_bwd[m] for m in arrival[:-late]])
     token_grad = backward_call(turned, short_weight, back, following, [rows_bwd[m] for m in arrival[-late:]])

time: 221 us -> 217 us (0.982)
  starting transfers between devices: 68.5 us -> 82.9 us
  waiting for transfers between devices: 85.3 us -> 72.3 us
  Pallas kernels: 58 us -> 51 us
    ppermute x35, waiting for transfers between devices: 84.8 us -> 69.9 us  [exchange(): lax.ppermute(block, 'seq', [(i, i ^ mask) for i in range(lax.axis_size('s...]
    ppermute x35, starting transfers between devices: 60.2 us -> 70 us  [exchange(): lax.ppermute(block, 'seq', [(i, i ^ mask) for i in range(lax.axis_size('s...]
    pallas_call x2, Pallas kernels: 10.6 us -> 3.65 us  [the longest x1 1.84 us: backward_call(): pl.pallas_call(functools.partial(backward_body, peers, width), name='back...]
    ppermute x2, starting transfers between devices: 7.32 us -> 12 us  [shifted(): lax.ppermute(block, 'seq', [(i - distance, i) for i in devices if i - dis...]
  transfers between devices with their start and end apart: 44 -> 44, of which waited for: 15 -> 15; matrix products, arithmetic and copies ran while one was open for 2% -> 2% of each run, Pallas kernels for 24% -> 23%
where the time goes in v2:
time: 217 us; the launch traced here: 216 us
  starting transfers between devices  82.9 us (38%)
  waiting for transfers between devices  72.3 us (33%)
  Pallas kernels  51 us (24%)
  local copies, waits for them, and re-layouts  6.25 us (3%)
    ppermute x35, starting transfers between devices, exchange(): lax.ppermute(block, 'seq', [(i, i ^ mask) for i in range(lax.axis_size('s...  70 us
    ppermute x35, waiting for transfers between devices, exchange(): lax.ppermute(block, 'seq', [(i, i ^ mask) for i in range(lax.axis_size('s...  69.9 us
    pallas_call x2, Pallas kernels, middle_call(): call(functools.partial(middle_body, peers, side // peers, with_grad), 'mi...  16.3 us
    ppermute x2, starting transfers between devices, shifted(): lax.ppermute(block, 'seq', [(i - distance, i) for i in devices if i - dis...  12 us
    pallas_call x1, Pallas kernels, forward_call(): call(functools.partial(forward_body, peers), 'forward_rows', (channels //...  11 us
    pallas_call x1, Pallas kernels, spread_gated_call(): call(functools.partial(spread_gated_body, peers), 'spread_gated', (channe...  9.42 us
    pallas_call x7, Pallas kernels, spread_peer_call(): call(spread_peer_body, 'spread_peer', (channels // width,), [whole((half,...  8.7 us
  transfers between devices with their start and end apart: 44, of which 15 were waited for; matrix products, arithmetic and copies ran while one was open for 2% of the time, Pallas kernels for 23%

profile of v2, /device:TPU:14, one launch (start us, length us, event | category | flops | bytes accessed | tf_op | source)
XLA Modules:
  0.0 216.0 jit_solution(15384162887325834325)
XLA Ops:
  10.6 2.9 %collective-permute-done.mine = bf16[64,1024]{1,0:T(8,128)(2,1)S(1)} collective-permute-done((bf16[64,1024]{1,0:T(8,128)(2,1)S(1)}, bf16[64,1024]{1,0:T(8,128)(2,1)S(1)}, u32[]{:S(2)}, u32[]{:S(2)}) %collective-permute-start) | collective-permute-done | bytes 131104 | tf_op jit(solution)/shard_map/ppermute | solution.py:16
  13.5 3.0 %collective-permute-start.12 = (bf16[64,1024]{1,0:T(8,128)(2,1)S(1)}, bf16[64,1024]{1,0:T(8,128)(2,1)S(1)}, u32[]{:S(2)}, u32[]{:S(2)}) collective-permute-start(bf16[64,1024]{1,0:T(8,128)(2,1)S(1)} %collective-permute-done.mine), channel_id=1, source_target_pairs={{0,6},{2,4},{4,2},{6,0},{8,14},{10,12},{12,10},{14,8},{1,7},{3,5},... | collective-permute-start | bytes 393224 | tf_op jit(solution)/shard_map/ppermute | solution.py:16
  36.3 4.2 %collective-permute-start.14 = (bf16[2,1024]{1,0:T(2,128)(2,1)S(1)}, bf16[2,1024]{1,0:T(2,128)(2,1)S(1)}, u32[]{:S(2)}, u32[]{:S(2)}) collective-permute-start(bf16[2,1024]{1,0:T(2,128)(2,1)S(1)} %slice_bitcast_fusion), channel_id=1, source_target_pairs={{0,2},{2,4},{4,6},{6,8},{8,10},{10,12},{12,14},{1,3},{3,5},{5,7},{... | collective-permute-start | bytes 12296 | tf_op jit(solution)/shard_map/ppermute | solution.py:21
  44.1 2.9 %collective-permute-start.20 = (bf16[128,1024]{1,0:T(8,128)(2,1)S(1)}, bf16[128,1024]{1,0:T(8,128)(2,1)S(1)}, u32[]{:S(2)}, u32[]{:S(2)}) collective-permute-start(bf16[128,1024]{1,0:T(8,128)(2,1)S(1)} %get-tuple-element.101), channel_id=1, source_target_pairs={{0,12},{2,14},{4,8},{6,10},{8,4},{10,6},{12,0},{14,2},{1,13},{3,15... | collective-permute-start | bytes 786440 | tf_op jit(solution)/shard_map/ppermute | solution.py:16
  46.9 9.4 %spread_gated.1 = (bf16[128,1024]{1,0:T(8,128)(2,1)S(1)}, bf16[128,1024]{1,0:T(8,128)(2,1)S(1)}, bf16[128,1024]{1,0:T(8,128)(2,1)S(1)}, bf16[128,1024]{1,0:T(8,1...) custom-call(bf16[1024,1024]{1,0:T(8,128)(2,1)} %bitcast.17, ...), custom_call_target="tpu_custom_call" | custom-call | flops 2147483648 | bytes 8388608 | tf_op jit(solution)/shard_map/spread_gated/pallas_call | solution.py:131
  56.5 4.3 %collective-permute-start.18 = (bf16[128,1024]{1,0:T(8,128)(2,1)S(1)}, bf16[128,1024]{1,0:T(8,128)(2,1)S(1)}, u32[]{:S(2)}, u32[]{:S(2)}) collective-permute-start(bf16[128,1024]{1,0:T(8,128)(2,1)S(1)} %get-tuple-element.97), channel_id=1, source_target_pairs={{0,6},{2,4},{4,2},{6,0},{8,14},{10,12},{12,10},{14,8},{1,7},{3,5},... | collective-permute-start | bytes 786440 | tf_op jit(solution)/shard_map/ppermute | solution.py:16
  63.2 9.2 %collective-permute-done.20.refs_6_.refs_14_ = bf16[128,1024]{1,0:T(8,128)(2,1)S(1)} collective-permute-done((bf16[128,1024]{1,0:T(8,128)(2,1)S(1)}, bf16[128,1024]{1,0:T(8,128)(2,1)S(1)}, u32[]{:S(2)}, u32[]{:S(2)}) %collective-permute-start.20) | collective-permute-done | bytes 262176 | tf_op jit(solution)/shard_map/ppermute | solution.py:16
  72.4 4.0 %collective-permute-start.24 = (bf16[128,1024]{1,0:T(8,128)(2,1)S(1)}, bf16[128,1024]{1,0:T(8,128)(2,1)S(1)}, u32[]{:S(2)}, u32[]{:S(2)}) collective-permute-start(bf16[128,1024]{1,0:T(8,128)(2,1)S(1)} %get-tuple-element.112), channel_id=1, source_target_pairs={{0,8},{2,10},{4,12},{6,14},{8,0},{10,2},{12,4},{14,6},{1,9},{3,11}... | collective-permute-start | bytes 786440 | tf_op jit(solution)/shard_map/ppermute | solution.py:16
  77.2 18.7 %collective-permute-done.21.refs_7_.refs_15_ = bf16[128,1024]{1,0:T(8,128)(2,1)S(1)} collective-permute-done((bf16[128,1024]{1,0:T(8,128)(2,1)S(1)}, bf16[128,1024]{1,0:T(8,128)(2,1)S(1)}, u32[]{:S(2)}, u32[]{:S(2)}) %collective-permute-start.21) | collective-permute-done | bytes 262176 | tf_op jit(solution)/shard_map/ppermute | solution.py:16
  97.8 7.5 %middle.1 = (bf16[128,1024]{1,0:T(8,128)(2,1)S(1)}, bf16[128,1024]{1,0:T(8,128)(2,1)S(1)}, bf16[128,1024]{1,0:T(8,128)(2,1)S(1)}, bf16[128,1024]{1,0:T(8,128)(2,...) custom-call(s32[1]{0:T(128)} %bitcast.4.place, ...), custom_call_target="tpu_custom_call" | custom-call | flops 2684354560 | bytes 8388608 | tf_op jit(solution)/shard_map/middle/pallas_call | solution.py:202
  105.4 5.1 %collective-permute-done.24.refs_4_ = bf16[128,1024]{1,0:T(8,128)(2,1)S(1)} collective-permute-done((bf16[128,1024]{1,0:T(8,128)(2,1)S(1)}, bf16[128,1024]{1,0:T(8,128)(2,1)S(1)}, u32[]{:S(2)}, u32[]{:S(2)}) %collective-permute-start.24) | collective-permute-done | bytes 262176 | tf_op jit(solution)/shard_map/ppermute | solution.py:16
  110.5 3.8 %collective-permute-start.25 = (bf16[128,1024]{1,0:T(8,128)(2,1)S(1)}, bf16[128,1024]{1,0:T(8,128)(2,1)S(1)}, u32[]{:S(2)}, u32[]{:S(2)}) collective-permute-start(bf16[128,1024]{1,0:T(8,128)(2,1)S(1)} %get-tuple-element.113), channel_id=1, source_target_pairs={{0,6},{2,4},{4,2},{6,0},{8,14},{10,12},{12,10},{14,8},{1,7},{3,5},... | collective-permute-start | bytes 786440 | tf_op jit(solution)/shard_map/ppermute | solution.py:16
  114.3 3.1 %collective-permute-done.27.refs_6_ = bf16[128,1024]{1,0:T(8,128)(2,1)S(1)} collective-permute-done((bf16[128,1024]{1,0:T(8,128)(2,1)S(1)}, bf16[128,1024]{1,0:T(8,128)(2,1)S(1)}, u32[]{:S(2)}, u32[]{:S(2)}) %collective-permute-start.27) | collective-permute-done | bytes 262176 | tf_op jit(solution)/shard_map/ppermute | solution.py:16
  117.4 18.3 %collective-permute-done.28.refs_7_ = bf16[128,1024]{1,0:T(8,128)(2,1)S(1)} collective-permute-done((bf16[128,1024]{1,0:T(8,128)(2,1)S(1)}, bf16[128,1024]{1,0:T(8,128)(2,1)S(1)}, u32[]{:S(2)}, u32[]{:S(2)}) %collective-permute-start.28) | collective-permute-done | bytes 262176 | tf_op jit(solution)/shard_map/ppermute | solution.py:16
  137.0 3.7 %collective-permute-start.33 = (bf16[128,1024]{1,0:T(8,128)(2,1)S(1)}, bf16[128,1024]{1,0:T(8,128)(2,1)S(1)}, u32[]{:S(2)}, u32[]{:S(2)}) collective-permute-start(bf16[128,1024]{1,0:T(8,128)(2,1)S(1)} %get-tuple-element.130), channel_id=1, source_target_pairs={{0,4},{2,6},{4,0},{6,2},{8,12},{10,14},{12,8},{14,10},{1,5},{3,7},... | collective-permute-start | bytes 786440 | tf_op jit(solution)/shard_map/ppermute | solution.py:16
  141.3 5.9 %collective-permute-start.35 = (bf16[128,1024]{1,0:T(8,128)(2,1)S(1)}, bf16[128,1024]{1,0:T(8,128)(2,1)S(1)}, u32[]{:S(2)}, u32[]{:S(2)}) collective-permute-start(bf16[128,1024]{1,0:T(8,128)(2,1)S(1)} %get-tuple-element.134), channel_id=1, source_target_pairs={{0,6},{2,4},{4,2},{6,0},{8,14},{10,12},{12,10},{14,8},{1,7},{3,5},... | collective-permute-start | bytes 786440 | tf_op jit(solution)/shard_map/ppermute | solution.py:16
  147.3 8.8 %middle_grad.1 = (bf16[8,128,1024]{2,1,0:T(8,128)(2,1)}, bf16[128,1024]{1,0:T(8,128)(2,1)S(1)}, bf16[128,1024]{1,0:T(8,128)(2,1)S(1)}, bf16[128,1024]{1,0:T(8,12...) custom-call(s32[1]{0:T(128)} %bitcast.4.place, ...), custom_call_target="tpu_custom_call" | custom-call | flops 3758096384 | bytes 12582912 | tf_op jit(solution)/shard_map/middle_grad/pallas_call | solution.py:202
  158.6 10.1 %collective-permute-start.37 = (bf16[128,1024]{1,0:T(8,128)(2,1)S(1)}, bf16[128,1024]{1,0:T(8,128)(2,1)S(1)}, u32[]{:S(2)}, u32[]{:S(2)}) collective-permute-start(bf16[128,1024]{1,0:T(8,128)(2,1)S(1)} %get-tuple-element.141), channel_id=1, source_target_pairs={{0,2},{2,0},{4,6},{6,4},{8,10},{10,8},{12,14},{14,12},{1,3},{3,1},... | collective-permute-start | bytes 786440 | tf_op jit(solution)/shard_map/ppermute | solution.py:16
  170.0 5.2 %collective-permute-start.39 = (bf16[128,1024]{1,0:T(8,128)(2,1)S(1)}, bf16[128,1024]{1,0:T(8,128)(2,1)S(1)}, u32[]{:S(2)}, u32[]{:S(2)}) collective-permute-start(bf16[128,1024]{1,0:T(8,128)(2,1)S(1)} %get-tuple-element.145), channel_id=1, source_target_pairs={{0,4},{2,6},{4,0},{6,2},{8,12},{10,14},{12,8},{14,10},{1,5},{3,7},... | collective-permute-start | bytes 786440 | tf_op jit(solution)/shard_map/ppermute | solution.py:16
  175.3 4.1 %collective-permute-start.40 = (bf16[128,1024]{1,0:T(8,128)(2,1)S(1)}, bf16[128,1024]{1,0:T(8,128)(2,1)S(1)}, u32[]{:S(2)}, u32[]{:S(2)}) collective-permute-start(bf16[128,1024]{1,0:T(8,128)(2,1)S(1)} %get-tuple-element.147), channel_id=1, source_target_pairs={{0,12},{2,14},{4,8},{6,10},{8,4},{10,6},{12,0},{14,2},{1,13},{3,15... | collective-permute-start | bytes 786440 | tf_op jit(solution)/shard_map/ppermute | solution.py:16
  179.4 4.2 %collective-permute-done.30.refs_1_ = bf16[128,1024]{1,0:T(8,128)(2,1)S(1)} collective-permute-done((bf16[128,1024]{1,0:T(8,128)(2,1)S(1)}, bf16[128,1024]{1,0:T(8,128)(2,1)S(1)}, u32[]{:S(2)}, u32[]{:S(2)}) %collective-permute-start.30) | collective-permute-done | bytes 262176 | tf_op jit(solution)/shard_map/ppermute | solution.py:16
  183.6 4.7 %collective-permute-start.42 = (bf16[128,1024]{1,0:T(8,128)(2,1)S(1)}, bf16[128,1024]{1,0:T(8,128)(2,1)S(1)}, u32[]{:S(2)}, u32[]{:S(2)}) collective-permute-start(bf16[128,1024]{1,0:T(8,128)(2,1)S(1)} %get-tuple-element.150), channel_id=1, source_target_pairs={{0,6},{2,4},{4,2},{6,0},{8,14},{10,12},{12,10},{14,8},{1,7},{3,5},... | collective-permute-start | bytes 786440 | tf_op jit(solution)/shard_map/ppermute | solution.py:16
  188.3 11.0 %forward_rows.1 = (bf16[1024,1024]{1,0:T(8,128)(2,1)}, f32[1024,1024]{1,0:T(8,128)}, f32[2,1024]{1,0:T(2,128)S(1)}) custom-call(bf16[1024,1024]{1,0:T(8,128)(2,1)S(1)} %turn.1.turned, f32[3,1024]{1,0:T(4,128)S(1)} %copy-done.9, bf16[1024,1024]{1,0:T(8,128)(2,1)} %bitcast.18, bf16[2,1024]{1,0:T(2,128)(2,1)S(1)} %collective-permute-done.14.halo, ...), custom_call_target="tpu_custom_call" | custom-call | flops 2147483648 | bytes 14680064 | tf_op jit(solution)/shard_map/forward_rows/pallas_call | solution.py:259
  199.4 7.8 %collective-permute-start.41 = (f32[2,1024]{1,0:T(2,128)S(1)}, f32[2,1024]{1,0:T(2,128)S(1)}, u32[]{:S(2)}, u32[]{:S(2)}) collective-permute-start(f32[2,1024]{1,0:T(2,128)S(1)} %get-tuple-element.148), channel_id=1, source_target_pairs={{2,0},{4,2},{6,4},{8,6},{10,8},{12,10},{14,12},{3,1},{5,3},{7,5},{... | collective-permute-start | bytes 24584 | tf_op jit(solution)/shard_map/ppermute | solution.py:21
  (116 shorter events, 53.0 us)
Async XLA Ops:
  29.3 27.1 %collective-permute-start.17 = (bf16[128,1024]{1,0:T(8,128)(2,1)S(1)}, bf16[128,1024]{1,0:T(8,128)(2,1)S(1)}, u32[]{:S(2)}, u32[]{:S(2)}) collective-permute-start(bf16[128,1024]{1,0:T(8,128)(2,1)S(1)} %get-tuple-element.96), channel_id=1, source_target_pairs={{0,8},{2,10},{4,12},{6,14},{8,0},{10,2},{12,4},{14,6},{1,9},{3,11}... | collective-permute-start | bytes 786440 | tf_op jit(solution)/shard_map/ppermute | solution.py:16
  32.3 24.1 %collective-permute-start.15 = (bf16[128,1024]{1,0:T(8,128)(2,1)S(1)}, bf16[128,1024]{1,0:T(8,128)(2,1)S(1)}, u32[]{:S(2)}, u32[]{:S(2)}) collective-permute-start(bf16[128,1024]{1,0:T(8,128)(2,1)S(1)} %get-tuple-element.91), channel_id=1, source_target_pairs={{0,2},{2,0},{4,6},{6,4},{8,10},{10,8},{12,14},{14,12},{1,3},{3,1},... | collective-permute-start | bytes 786440 | tf_op jit(solution)/shard_map/ppermute | solution.py:16
  34.8 26.0 %collective-permute-start.16 = (bf16[128,1024]{1,0:T(8,128)(2,1)S(1)}, bf16[128,1024]{1,0:T(8,128)(2,1)S(1)}, u32[]{:S(2)}, u32[]{:S(2)}) collective-permute-start(bf16[128,1024]{1,0:T(8,128)(2,1)S(1)} %get-tuple-element.93), channel_id=1, source_target_pairs={{0,4},{2,6},{4,0},{6,2},{8,12},{10,14},{12,8},{14,10},{1,5},{3,7},... | collective-permute-start | bytes 786440 | tf_op jit(solution)/shard_map/ppermute | solution.py:16
  41.8 21.4 %collective-permute-start.19 = (bf16[128,1024]{1,0:T(8,128)(2,1)S(1)}, bf16[128,1024]{1,0:T(8,128)(2,1)S(1)}, u32[]{:S(2)}, u32[]{:S(2)}) collective-permute-start(bf16[128,1024]{1,0:T(8,128)(2,1)S(1)} %get-tuple-element.99), channel_id=1, source_target_pairs={{0,10},{2,8},{4,14},{6,12},{8,2},{10,0},{12,6},{14,4},{1,11},{3,9}... | collective-permute-start | bytes 786440 | tf_op jit(solution)/shard_map/ppermute | solution.py:16
  44.1 28.3 %collective-permute-start.20 = (bf16[128,1024]{1,0:T(8,128)(2,1)S(1)}, bf16[128,1024]{1,0:T(8,128)(2,1)S(1)}, u32[]{:S(2)}, u32[]{:S(2)}) collective-permute-start(bf16[128,1024]{1,0:T(8,128)(2,1)S(1)} %get-tuple-element.101), channel_id=1, source_target_pairs={{0,12},{2,14},{4,8},{6,10},{8,4},{10,6},{12,0},{14,2},{1,13},{3,15... | collective-permute-start | bytes 786440 | tf_op jit(solution)/shard_map/ppermute | solution.py:16
  56.4 39.5 %collective-permute-start.21 = (bf16[128,1024]{1,0:T(8,128)(2,1)S(1)}, bf16[128,1024]{1,0:T(8,128)(2,1)S(1)}, u32[]{:S(2)}, u32[]{:S(2)}) collective-permute-start(bf16[128,1024]{1,0:T(8,128)(2,1)S(1)} %get-tuple-element.102), channel_id=1, source_target_pairs={{0,14},{2,12},{4,10},{6,8},{8,6},{10,4},{12,2},{14,0},{1,15},{3,13... | collective-permute-start | bytes 786440 | tf_op jit(solution)/shard_map/ppermute | solution.py:16
  56.5 20.8 %collective-permute-start.18 = (bf16[128,1024]{1,0:T(8,128)(2,1)S(1)}, bf16[128,1024]{1,0:T(8,128)(2,1)S(1)}, u32[]{:S(2)}, u32[]{:S(2)}) collective-permute-start(bf16[128,1024]{1,0:T(8,128)(2,1)S(1)} %get-tuple-element.97), channel_id=1, source_target_pairs={{0,6},{2,4},{4,2},{6,0},{8,14},{10,12},{12,10},{14,8},{1,7},{3,5},... | collective-permute-start | bytes 786440 | tf_op jit(solution)/shard_map/ppermute | solution.py:16
  60.8 35.1 %collective-permute-start.22 = (bf16[128,1024]{1,0:T(8,128)(2,1)S(1)}, bf16[128,1024]{1,0:T(8,128)(2,1)S(1)}, u32[]{:S(2)}, u32[]{:S(2)}) collective-permute-start(bf16[128,1024]{1,0:T(8,128)(2,1)S(1)} %get-tuple-element.107), channel_id=1, source_target_pairs={{0,2},{2,0},{4,6},{6,4},{8,10},{10,8},{12,14},{14,12},{1,3},{3,1},... | collective-permute-start | bytes 786440 | tf_op jit(solution)/shard_map/ppermute | solution.py:16
  72.4 41.9 %collective-permute-start.26 = (bf16[128,1024]{1,0:T(8,128)(2,1)S(1)}, bf16[128,1024]{1,0:T(8,128)(2,1)S(1)}, u32[]{:S(2)}, u32[]{:S(2)}) collective-permute-start(bf16[128,1024]{1,0:T(8,128)(2,1)S(1)} %get-tuple-element.115), channel_id=1, source_target_pairs={{0,10},{2,8},{4,14},{6,12},{8,2},{10,0},{12,6},{14,4},{1,11},{3,9}... | collective-permute-start | bytes 786440 | tf_op jit(solution)/shard_map/ppermute | solution.py:16
  72.4 38.1 %collective-permute-start.24 = (bf16[128,1024]{1,0:T(8,128)(2,1)S(1)}, bf16[128,1024]{1,0:T(8,128)(2,1)S(1)}, u32[]{:S(2)}, u32[]{:S(2)}) collective-permute-start(bf16[128,1024]{1,0:T(8,128)(2,1)S(1)} %get-tuple-element.112), channel_id=1, source_target_pairs={{0,8},{2,10},{4,12},{6,14},{8,0},{10,2},{12,4},{14,6},{1,9},{3,11}... | collective-permute-start | bytes 786440 | tf_op jit(solution)/shard_map/ppermute | solution.py:16
  95.9 21.5 %collective-permute-start.27 = (bf16[128,1024]{1,0:T(8,128)(2,1)S(1)}, bf16[128,1024]{1,0:T(8,128)(2,1)S(1)}, u32[]{:S(2)}, u32[]{:S(2)}) collective-permute-start(bf16[128,1024]{1,0:T(8,128)(2,1)S(1)} %get-tuple-element.117), channel_id=1, source_target_pairs={{0,12},{2,14},{4,8},{6,10},{8,4},{10,6},{12,0},{14,2},{1,13},{3,15... | collective-permute-start | bytes 786440 | tf_op jit(solution)/shard_map/ppermute | solution.py:16
  95.9 21.5 %collective-permute-start.23 = (bf16[128,1024]{1,0:T(8,128)(2,1)S(1)}, bf16[128,1024]{1,0:T(8,128)(2,1)S(1)}, u32[]{:S(2)}, u32[]{:S(2)}) collective-permute-start(bf16[128,1024]{1,0:T(8,128)(2,1)S(1)} %get-tuple-element.109), channel_id=1, source_target_pairs={{0,4},{2,6},{4,0},{6,2},{8,12},{10,14},{12,8},{14,10},{1,5},{3,7},... | collective-permute-start | bytes 786440 | tf_op jit(solution)/shard_map/ppermute | solution.py:16
  95.9 39.8 %collective-permute-start.28 = (bf16[128,1024]{1,0:T(8,128)(2,1)S(1)}, bf16[128,1024]{1,0:T(8,128)(2,1)S(1)}, u32[]{:S(2)}, u32[]{:S(2)}) collective-permute-start(bf16[128,1024]{1,0:T(8,128)(2,1)S(1)} %get-tuple-element.119), channel_id=1, source_target_pairs={{0,14},{2,12},{4,10},{6,8},{8,6},{10,4},{12,2},{14,0},{1,15},{3,13... | collective-permute-start | bytes 786440 | tf_op jit(solution)/shard_map/ppermute | solution.py:16
  110.5 26.5 %collective-permute-start.25 = (bf16[128,1024]{1,0:T(8,128)(2,1)S(1)}, bf16[128,1024]{1,0:T(8,128)(2,1)S(1)}, u32[]{:S(2)}, u32[]{:S(2)}) collective-permute-start(bf16[128,1024]{1,0:T(8,128)(2,1)S(1)} %get-tuple-element.113), channel_id=1, source_target_pairs={{0,6},{2,4},{4,2},{6,0},{8,14},{10,12},{12,10},{14,8},{1,7},{3,5},... | collective-permute-start | bytes 786440 | tf_op jit(solution)/shard_map/ppermute | solution.py:16
  114.3 27.1 %collective-permute-start.31 = (bf16[128,1024]{1,0:T(8,128)(2,1)S(1)}, bf16[128,1024]{1,0:T(8,128)(2,1)S(1)}, u32[]{:S(2)}, u32[]{:S(2)}) collective-permute-start(bf16[128,1024]{1,0:T(8,128)(2,1)S(1)} %get-tuple-element.126), channel_id=1, source_target_pairs={{0,8},{2,10},{4,12},{6,14},{8,0},{10,2},{12,4},{14,6},{1,9},{3,11}... | collective-permute-start | bytes 786440 | tf_op jit(solution)/shard_map/ppermute | solution.py:16
  135.7 34.3 %collective-permute-start.34 = (bf16[128,1024]{1,0:T(8,128)(2,1)S(1)}, bf16[128,1024]{1,0:T(8,128)(2,1)S(1)}, u32[]{:S(2)}, u32[]{:S(2)}) collective-permute-start(bf16[128,1024]{1,0:T(8,128)(2,1)S(1)} %get-tuple-element.132), channel_id=1, source_target_pairs={{0,12},{2,14},{4,8},{6,10},{8,4},{10,6},{12,0},{14,2},{1,13},{3,15... | collective-permute-start | bytes 786440 | tf_op jit(solution)/shard_map/ppermute | solution.py:16
  137.0 21.6 %collective-permute-start.33 = (bf16[128,1024]{1,0:T(8,128)(2,1)S(1)}, bf16[128,1024]{1,0:T(8,128)(2,1)S(1)}, u32[]{:S(2)}, u32[]{:S(2)}) collective-permute-start(bf16[128,1024]{1,0:T(8,128)(2,1)S(1)} %get-tuple-element.130), channel_id=1, source_target_pairs={{0,4},{2,6},{4,0},{6,2},{8,12},{10,14},{12,8},{14,10},{1,5},{3,7},... | collective-permute-start | bytes 786440 | tf_op jit(solution)/shard_map/ppermute | solution.py:16
  141.3 28.7 %collective-permute-start.35 = (bf16[128,1024]{1,0:T(8,128)(2,1)S(1)}, bf16[128,1024]{1,0:T(8,128)(2,1)S(1)}, u32[]{:S(2)}, u32[]{:S(2)}) collective-permute-start(bf16[128,1024]{1,0:T(8,128)(2,1)S(1)} %get-tuple-element.134), channel_id=1, source_target_pairs={{0,6},{2,4},{4,2},{6,0},{8,14},{10,12},{12,10},{14,8},{1,7},{3,5},... | collective-permute-start | bytes 786440 | tf_op jit(solution)/shard_map/ppermute | solution.py:16
  156.2 27.4 %collective-permute-start.30 = (bf16[128,1024]{1,0:T(8,128)(2,1)S(1)}, bf16[128,1024]{1,0:T(8,128)(2,1)S(1)}, u32[]{:S(2)}, u32[]{:S(2)}) collective-permute-start(bf16[128,1024]{1,0:T(8,128)(2,1)S(1)} %get-tuple-element.123), channel_id=1, source_target_pairs={{0,8},{2,10},{4,12},{6,14},{8,0},{10,2},{12,4},{14,6},{1,9},{3,11}... | collective-permute-start | bytes 786440 | tf_op jit(solution)/shard_map/ppermute | solution.py:16
  158.6 40.6 %collective-permute-start.37 = (bf16[128,1024]{1,0:T(8,128)(2,1)S(1)}, bf16[128,1024]{1,0:T(8,128)(2,1)S(1)}, u32[]{:S(2)}, u32[]{:S(2)}) collective-permute-start(bf16[128,1024]{1,0:T(8,128)(2,1)S(1)} %get-tuple-element.141), channel_id=1, source_target_pairs={{0,2},{2,0},{4,6},{6,4},{8,10},{10,8},{12,14},{14,12},{1,3},{3,1},... | collective-permute-start | bytes 786440 | tf_op jit(solution)/shard_map/ppermute | solution.py:16
  170.0 29.4 %collective-permute-start.38 = (bf16[128,1024]{1,0:T(8,128)(2,1)S(1)}, bf16[128,1024]{1,0:T(8,128)(2,1)S(1)}, u32[]{:S(2)}, u32[]{:S(2)}) collective-permute-start(bf16[128,1024]{1,0:T(8,128)(2,1)S(1)} %get-tuple-element.143), channel_id=1, source_target_pairs={{0,10},{2,8},{4,14},{6,12},{8,2},{10,0},{12,6},{14,4},{1,11},{3,9}... | collective-permute-start | bytes 786440 | tf_op jit(solution)/shard_map/ppermute | solution.py:16
  170.0 37.1 %collective-permute-start.39 = (bf16[128,1024]{1,0:T(8,128)(2,1)S(1)}, bf16[128,1024]{1,0:T(8,128)(2,1)S(1)}, u32[]{:S(2)}, u32[]{:S(2)}) collective-permute-start(bf16[128,1024]{1,0:T(8,128)(2,1)S(1)} %get-tuple-element.145), channel_id=1, source_target_pairs={{0,4},{2,6},{4,0},{6,2},{8,12},{10,14},{12,8},{14,10},{1,5},{3,7},... | collective-permute-start | bytes 786440 | tf_op jit(solution)/shard_map/ppermute | solution.py:16
  175.3 32.7 %collective-permute-start.40 = (bf16[128,1024]{1,0:T(8,128)(2,1)S(1)}, bf16[128,1024]{1,0:T(8,128)(2,1)S(1)}, u32[]{:S(2)}, u32[]{:S(2)}) collective-permute-start(bf16[128,1024]{1,0:T(8,128)(2,1)S(1)} %get-tuple-element.147), channel_id=1, source_target_pairs={{0,12},{2,14},{4,8},{6,10},{8,4},{10,6},{12,0},{14,2},{1,13},{3,15... | collective-permute-start | bytes 786440 | tf_op jit(solution)/shard_map/ppermute | solution.py:16
  183.6 30.4 %collective-permute-start.42 = (bf16[128,1024]{1,0:T(8,128)(2,1)S(1)}, bf16[128,1024]{1,0:T(8,128)(2,1)S(1)}, u32[]{:S(2)}, u32[]{:S(2)}) collective-permute-start(bf16[128,1024]{1,0:T(8,128)(2,1)S(1)} %get-tuple-element.150), channel_id=1, source_target_pairs={{0,6},{2,4},{4,2},{6,0},{8,14},{10,12},{12,10},{14,8},{1,7},{3,5},... | collective-permute-start | bytes 786440 | tf_op jit(solution)/shard_map/ppermute | solution.py:16
  (31 other events, 429.1 us)

commit v3 on v2

--- a/solution.py
+++ b/solution.py
@@ -48,6 +48,10 @@
 
 def struct(shape, dtype):
     return jax.ShapeDtypeStruct(shape, dtype)
+
+
+def in_hbm(shape, dtype):
+    return pltpu.HBM(shape, dtype)
 
 
 def matmul(left, right):
@@ -135,7 +139,7 @@
         [tile(block, width), tile(2, width), tile(3, width), tile(block, width)]
         + [whole((share, block))] * peers,
         [tile(share, width)] * peers,
-        [struct((share, channels), BF16)] * peers,
+        [in_hbm((share, channels), BF16)] * peers,
         2 * peers * share * block * channels,
         4 * block * channels + 2 * peers * share * (block + channels),
         transcendentals=2 * block * channels,
@@ -205,7 +209,7 @@
         (channels // width,),
         [whole((groups, side, side))] * 4 + [cube] + [tile(columns, width)] * n_in,
         ([cube] if with_grad else []) + [tile(columns, width)] * peers,
-        ([struct(kern.shape, BF16)] if with_grad else []) + [struct((columns, channels), BF16)] * peers,
+        ([struct(kern.shape, BF16)] if with_grad else []) + [in_hbm((columns, channels), BF16)] * peers,
         (14 if with_grad else 10) * groups * side * side * channels,
         (10 if with_grad else 6) * peers * columns * channels + 8 * groups * side * side,
         scalars=1,
@@ -213,23 +217,51 @@
     return (out[0], list(out[1:])) if with_grad else list(out)
 
 
+def exact(left, right):
+    return jnp.dot(left, right, precision=lax.Precision.HIGHEST, preferred_element_type=F32)
+
+
+def factors_body(span, place, outer, twiddle, high, low, high_t, low_t):
+    peers, columns = twiddle.shape
+    side = peers * span
+
+    def spots(shape, axis):
+        return lax.broadcasted_iota(jnp.int32, shape, axis)
+
+    pick = jnp.where(lax.bitwise_xor(spots((peers, peers), 0), place[0]) == spots((peers, peers), 1), 1.0, 0.0)
+    spread_rows = jnp.where(lax.div(spots((side, peers), 0), span) == spots((side, peers), 1), 1.0, 0.0)
+    owner = lax.div(spots((peers, side), 1), span) == spots((peers, side), 0)
+    spread_columns = jnp.where(owner, 1.0, 0.0)
+    outer_here = exact(pick, exact(outer[...], pick))
+    twiddle_here = exact(pick, twiddle[...])
+    wide = exact(exact(spread_rows, outer_here), spread_columns)
+    same = lax.rem(spots((side, side), 0), span) == lax.rem(spots((side, side), 1), span)
+    wide = jnp.where(same, wide, 0.0)
+    for g in range(columns // span):
+        at = lax.rem(spots((columns, side), 1), span) + g * span == spots((columns, side), 0)
+        scale = exact(twiddle_here, jnp.where(at, 1.0, 0.0))
+        scale = jnp.sum(jnp.where(owner, scale, 0.0), axis=0, keepdims=True)
+        factor = wide * scale
+        high[g], low[g] = two_part(factor)
+        high_t[g], low_t[g] = two_part(factor.T)
+
+
 def middle_factors(outer, twiddle, place):
     peers, columns = twiddle.shape
     span = min(columns, max(16, 256 // peers))
     groups, side = columns // span, peers * span
-    order = lax.bitwise_xor(jnp.arange(peers), place)
-    pick = (order[:, None] == jnp.arange(peers)[None, :]).astype(F32)
-    exact = functools.partial(jnp.dot, precision=lax.Precision.HIGHEST, preferred_element_type=F32)
-    outer_here, twiddle_here = exact(exact(pick, outer), pick.T), exact(pick, twiddle)
-    wide = jnp.repeat(jnp.repeat(outer_here, span, axis=0), span, axis=1)
-    spot = jnp.arange(side) % span
-    wide = jnp.where(spot[:, None] == spot[None, :], wide, 0.0)
-    scale = twiddle_here.reshape(peers, groups, span).transpose(1, 0, 2).reshape(groups, 1, side)
-    factor = wide[None] * scale
-    high = lax.reduce_precision(factor, 8, 7)
-    low = factor - high
-    high, low = high.astype(BF16), low.astype(BF16)
-    return high, low, high.transpose(0, 2, 1), low.transpose(0, 2, 1)
+    shape = (groups, side, side)
+    return call(
+        functools.partial(factors_body, span),
+        "factors",
+        (1,),
+        [whole(outer.shape), whole(twiddle.shape)],
+        [whole(shape)] * 4,
+        [struct(shape, BF16)] * 4,
+        16 * groups * side * side,
+        8 * groups * side * side,
+        scalars=1,
+    )(place, outer, twiddle)
 
 
 def join_rows(pieces):
@@ -389,9 +421,9 @@
     held = after(flat, pieces[-1])
     spread[0] = spread_own_call(inner_factor, held)
 
-    factors = middle_factors(outer_factor, twiddle, place)
     in_order = [rows[m] for m in range(peers)]
     spread_cot = spread_gated_call(held, preceding, short_weight, cot, in_order)
+    factors = middle_factors(after(outer_factor, spread_cot[0]), twiddle, place_ref)
     spread_cot = {m: wire.exchange(spread_cot[m], m) for m in others} | {0: spread_cot[0]}
     turned = turn_call([rows[m] for m in arrival])
 
@@ -401,14 +433,14 @@
     spread_cot[0] = after(spread_cot[0], mid[0])
     kernel_grad, mid = middle_call(place_ref, factors, kernel, [spread_cot[m] for m in range(peers)], spread)
     rows_bwd = {0: mid[0]}
-    for m in others[:-1]:
+    for m in others[:-2]:
         rows_bwd[m] = wire.exchange(mid[m], m)
-    rows_fwd[0] = after(rows_fwd[0], rows_bwd[others[0]])
     mixer_out, back, head = forward_call(
         turned, short_weight, flat, preceding, cot, [rows_fwd[m] for m in arrival]
     )
     following = shifted(head, -1)
-    rows_bwd[others[-1]] = wire.exchange(after(mid[others[-1]], head), others[-1])
+    for m in others[-2:]:
+        rows_bwd[m] = wire.exchange(after(mid[m], head), m)
     late = max(1, peers // 4)
     back = partial_call(turned, back, [rows_bwd[m] for m in arrival[:-late]])
     token_grad = backward_call(turned, short_weight, back, following, [rows_bwd[m] for m in arrival[-late:]])

time: 217 us -> 212 us (0.977)
  starting transfers between devices: 82.9 us -> 65.9 us
  waiting for transfers between devices: 72.3 us -> 82.7 us
  Pallas kernels: 51 us -> 55.6 us
    ppermute x35, starting transfers between devices: 70 us -> 55.7 us  [exchange(): lax.ppermute(block, 'seq', [(i, i ^ mask) for i in range(lax.axis_size('s...]
    ppermute x35, waiting for transfers between devices: 69.9 us -> 80.1 us  [exchange(): lax.ppermute(block, 'seq', [(i, i ^ mask) for i in range(lax.axis_size('s...]
    ppermute x2, starting transfers between devices: 12 us -> 9 us  [shifted(): lax.ppermute(block, 'seq', [(i - distance, i) for i in devices if i - dis...]
    pallas_call x7, Pallas kernels: 8.7 us -> 11.2 us  [spread_peer_call(): call(spread_peer_body, 'spread_peer', (channels // width,), [whole((half,...]
    unnamed x22 -> x62, local copies, waits for them, and re-layouts: 4.16 us -> 5.27 us
  transfers between devices with their start and end apart: 44 -> 44, of which waited for: 15 -> 15; matrix products, arithmetic and copies ran while one was open for 2% -> 0% of each run, Pallas kernels for 23% -> 25%
where the time goes in v3:
time: 212 us
  waiting for transfers between devices  82.7 us (39%)
  starting transfers between devices  65.9 us (31%)
  Pallas kernels  55.6 us (26%)
  local copies, waits for them, and re-layouts  6.19 us (3%)
    ppermute x35, waiting for transfers between devices, exchange(): lax.ppermute(block, 'seq', [(i, i ^ mask) for i in range(lax.axis_size('s...  80.1 us
    ppermute x35, starting transfers between devices, exchange(): lax.ppermute(block, 'seq', [(i, i ^ mask) for i in range(lax.axis_size('s...  55.7 us
    pallas_call x2, Pallas kernels, middle_call(): call(functools.partial(middle_body, peers, side // peers, with_grad), 'mi...  16.3 us
    pallas_call x7, Pallas kernels, spread_peer_call(): call(spread_peer_body, 'spread_peer', (channels // width,), [whole((half,...  11.2 us
    pallas_call x1, Pallas kernels, forward_call(): call(functools.partial(forward_body, peers), 'forward_rows', (channels //...  11.1 us
    pallas_call x1, Pallas kernels, spread_gated_call(): call(functools.partial(spread_gated_body, peers), 'spread_gated', (channe...  9.98 us
    ppermute x2, starting transfers between devices, shifted(): lax.ppermute(block, 'seq', [(i - distance, i) for i in devices if i - dis...  9 us
    unnamed x62, local copies, waits for them, and re-layouts  5.27 us
  transfers between devices with their start and end apart: 44, of which 15 were waited for; matrix products, arithmetic and copies ran while one was open for 0% of the time, Pallas kernels for 25%

profile of v3, /device:TPU:14, one launch (start us, length us, event | category | flops | bytes accessed | tf_op | source)
XLA Modules:
  0.0 211.6 jit_solution(5903688830118334847)
XLA Ops:
  1.6 2.7 %collective-permute-start = (bf16[64,1024]{1,0:T(8,128)(2,1)S(1)}, bf16[64,1024]{1,0:T(8,128)(2,1)S(1)}, u32[]{:S(2)}, u32[]{:S(2)}) collective-permute-start(bf16[64,1024]{1,0:T(8,128)(2,1)S(1)} %constant_dynamic-slice_fusion), channel_id=1, source_target_pairs={{0,8},{2,10},{4,12},{6,14},{8,0},{10,2},{12,4},{14,6},{1,9},{3,11}... | collective-permute-start | bytes 393224 | tf_op jit(solution)/shard_map/ppermute | solution.py:16
  30.8 4.9 %collective-permute-start.14 = (bf16[2,1024]{1,0:T(2,128)(2,1)S(1)}, bf16[2,1024]{1,0:T(2,128)(2,1)S(1)}, u32[]{:S(2)}, u32[]{:S(2)}) collective-permute-start(bf16[2,1024]{1,0:T(2,128)(2,1)S(1)} %slice_bitcast_fusion), channel_id=1, source_target_pairs={{0,2},{2,4},{4,6},{6,8},{8,10},{10,12},{12,14},{1,3},{3,5},{5,7},{... | collective-permute-start | bytes 12296 | tf_op jit(solution)/shard_map/ppermute | solution.py:21
  41.2 3.7 %collective-permute-start.18 = (bf16[128,1024]{1,0:T(8,128)(2,1)}, bf16[128,1024]{1,0:T(8,128)(2,1)}, u32[]{:S(2)}, u32[]{:S(2)}) collective-permute-start(bf16[128,1024]{1,0:T(8,128)(2,1)} %get-tuple-element.108), channel_id=1, source_target_pairs={{0,6},{2,4},{4,2},{6,0},{8,14},{10,12},{12,10},{14,8},{1,7},{3,5},... | collective-permute-start | bytes 786440 | tf_op jit(solution)/shard_map/ppermute | solution.py:16
  44.8 10.0 %spread_gated.1 = (bf16[128,1024]{1,0:T(8,128)(2,1)}, bf16[128,1024]{1,0:T(8,128)(2,1)}, bf16[128,1024]{1,0:T(8,128)(2,1)}, bf16[128,1024]{1,0:T(8,128)(2,1)}, b...) custom-call(bf16[1024,1024]{1,0:T(8,128)(2,1)S(1)} %bitcast.16, ...), custom_call_target="tpu_custom_call" | custom-call | flops 2147483648 | bytes 8388608 | tf_op jit(solution)/shard_map/spread_gated/pallas_call | solution.py:135
  58.2 9.8 %collective-permute-done.20.refs_6_.refs_14_ = bf16[128,1024]{1,0:T(8,128)(2,1)} collective-permute-done((bf16[128,1024]{1,0:T(8,128)(2,1)}, bf16[128,1024]{1,0:T(8,128)(2,1)}, u32[]{:S(2)}, u32[]{:S(2)}) %collective-permute-start.20) | collective-permute-done | bytes 262176 | tf_op jit(solution)/shard_map/ppermute | solution.py:16
  68.0 5.0 %collective-permute-start.22 = (bf16[128,1024]{1,0:T(8,128)(2,1)}, bf16[128,1024]{1,0:T(8,128)(2,1)S(1)}, u32[]{:S(2)}, u32[]{:S(2)}) collective-permute-start(bf16[128,1024]{1,0:T(8,128)(2,1)} %get-tuple-element.117), channel_id=1, source_target_pairs={{0,10},{2,8},{4,14},{6,12},{8,2},{10,0},{12,6},{14,4},{1,11},{3,9}... | collective-permute-start | bytes 786440 | tf_op jit(solution)/shard_map/ppermute | solution.py:16
  75.3 14.2 %collective-permute-done.21.refs_7_.refs_15_ = bf16[128,1024]{1,0:T(8,128)(2,1)} collective-permute-done((bf16[128,1024]{1,0:T(8,128)(2,1)}, bf16[128,1024]{1,0:T(8,128)(2,1)}, u32[]{:S(2)}, u32[]{:S(2)}) %collective-permute-start.21) | collective-permute-done | bytes 262176 | tf_op jit(solution)/shard_map/ppermute | solution.py:16
  89.7 7.8 %middle.1 = (bf16[128,1024]{1,0:T(8,128)(2,1)}, bf16[128,1024]{1,0:T(8,128)(2,1)}, bf16[128,1024]{1,0:T(8,128)(2,1)}, bf16[128,1024]{1,0:T(8,128)(2,1)}, bf16[12...) custom-call(s32[1]{0:T(128)} %bitcast.4.place, ...), custom_call_target="tpu_custom_call" | custom-call | flops 2684354560 | bytes 8388608 | tf_op jit(solution)/shard_map/middle/pallas_call | solution.py:206
  97.5 3.6 %collective-permute-done.28.refs_4_ = bf16[128,1024]{1,0:T(8,128)(2,1)S(1)} collective-permute-done((bf16[128,1024]{1,0:T(8,128)(2,1)}, bf16[128,1024]{1,0:T(8,128)(2,1)S(1)}, u32[]{:S(2)}, u32[]{:S(2)}) %collective-permute-start.28) | collective-permute-done | bytes 262176 | tf_op jit(solution)/shard_map/ppermute | solution.py:16
  101.1 4.1 %collective-permute-start.29 = (bf16[128,1024]{1,0:T(8,128)(2,1)S(1)}, bf16[128,1024]{1,0:T(8,128)(2,1)S(1)}, u32[]{:S(2)}, u32[]{:S(2)}) collective-permute-start(bf16[128,1024]{1,0:T(8,128)(2,1)S(1)} %copy-done.25), channel_id=1, source_target_pairs={{0,6},{2,4},{4,2},{6,0},{8,14},{10,12},{12,10},{14,8},{1,7},{3,5},... | collective-permute-start | bytes 786440 | tf_op jit(solution)/shard_map/ppermute | solution.py:16
  108.9 2.6 %collective-permute-start.25 = (bf16[128,1024]{1,0:T(8,128)(2,1)}, bf16[128,1024]{1,0:T(8,128)(2,1)S(1)}, u32[]{:S(2)}, u32[]{:S(2)}) collective-permute-start(bf16[128,1024]{1,0:T(8,128)(2,1)} %get-tuple-element.122), channel_id=1, source_target_pairs={{0,2},{2,0},{4,6},{6,4},{8,10},{10,8},{12,14},{14,12},{1,3},{3,1},... | collective-permute-start | bytes 786440 | tf_op jit(solution)/shard_map/ppermute | solution.py:16
  111.5 18.3 %collective-permute-done.26.refs_6_ = bf16[128,1024]{1,0:T(8,128)(2,1)S(1)} collective-permute-done((bf16[128,1024]{1,0:T(8,128)(2,1)S(1)}, bf16[128,1024]{1,0:T(8,128)(2,1)S(1)}, u32[]{:S(2)}, u32[]{:S(2)}) %collective-permute-start.26) | collective-permute-done | bytes 262176 | tf_op jit(solution)/shard_map/ppermute | solution.py:16
  132.2 3.3 %collective-permute-start.30 = (bf16[128,1024]{1,0:T(8,128)(2,1)}, bf16[128,1024]{1,0:T(8,128)(2,1)S(1)}, u32[]{:S(2)}, u32[]{:S(2)}) collective-permute-start(bf16[128,1024]{1,0:T(8,128)(2,1)} %get-tuple-element.132), channel_id=1, source_target_pairs={{0,4},{2,6},{4,0},{6,2},{8,12},{10,14},{12,8},{14,10},{1,5},{3,7},... | collective-permute-start | bytes 786440 | tf_op jit(solution)/shard_map/ppermute | solution.py:16
  135.6 4.0 %collective-permute-done.23.refs_1_ = bf16[128,1024]{1,0:T(8,128)(2,1)S(1)} collective-permute-done((bf16[128,1024]{1,0:T(8,128)(2,1)}, bf16[128,1024]{1,0:T(8,128)(2,1)S(1)}, u32[]{:S(2)}, u32[]{:S(2)}) %collective-permute-start.23) | collective-permute-done | bytes 262176 | tf_op jit(solution)/shard_map/ppermute | solution.py:16
  139.6 5.0 %collective-permute-start.34 = (bf16[128,1024]{1,0:T(8,128)(2,1)}, bf16[128,1024]{1,0:T(8,128)(2,1)S(1)}, u32[]{:S(2)}, u32[]{:S(2)}) collective-permute-start(bf16[128,1024]{1,0:T(8,128)(2,1)} %get-tuple-element.140), channel_id=1, source_target_pairs={{0,6},{2,4},{4,2},{6,0},{8,14},{10,12},{12,10},{14,8},{1,7},{3,5},... | collective-permute-start | bytes 786440 | tf_op jit(solution)/shard_map/ppermute | solution.py:16
  145.8 8.4 %middle_grad.1 = (bf16[8,128,1024]{2,1,0:T(8,128)(2,1)}, bf16[128,1024]{1,0:T(8,128)(2,1)}, bf16[128,1024]{1,0:T(8,128)(2,1)}, bf16[128,1024]{1,0:T(8,128)(2,1)}...) custom-call(s32[1]{0:T(128)} %bitcast.4.place, ...), custom_call_target="tpu_custom_call" | custom-call | flops 3758096384 | bytes 12582912 | tf_op jit(solution)/shard_map/middle_grad/pallas_call | solution.py:206
  154.2 3.7 %collective-permute-done.27.refs_3_ = bf16[128,1024]{1,0:T(8,128)(2,1)S(1)} collective-permute-done((bf16[128,1024]{1,0:T(8,128)(2,1)}, bf16[128,1024]{1,0:T(8,128)(2,1)S(1)}, u32[]{:S(2)}, u32[]{:S(2)}) %collective-permute-start.27) | collective-permute-done | bytes 262176 | tf_op jit(solution)/shard_map/ppermute | solution.py:16
  157.9 3.4 %collective-permute-start.36 = (bf16[128,1024]{1,0:T(8,128)(2,1)}, bf16[128,1024]{1,0:T(8,128)(2,1)S(1)}, u32[]{:S(2)}, u32[]{:S(2)}) collective-permute-start(bf16[128,1024]{1,0:T(8,128)(2,1)} %get-tuple-element.148), channel_id=1, source_target_pairs={{0,8},{2,10},{4,12},{6,14},{8,0},{10,2},{12,4},{14,6},{1,9},{3,11}... | collective-permute-start | bytes 786440 | tf_op jit(solution)/shard_map/ppermute | solution.py:16
  164.2 3.2 %collective-permute-start.39 = (bf16[128,1024]{1,0:T(8,128)(2,1)S(1)}, bf16[128,1024]{1,0:T(8,128)(2,1)S(1)}, u32[]{:S(2)}, u32[]{:S(2)}) collective-permute-start(bf16[128,1024]{1,0:T(8,128)(2,1)S(1)} %copy-done.27), channel_id=1, source_target_pairs={{0,4},{2,6},{4,0},{6,2},{8,12},{10,14},{12,8},{14,10},{1,5},{3,7},... | collective-permute-start | bytes 786440 | tf_op jit(solution)/shard_map/ppermute | solution.py:16
  167.4 11.6 %collective-permute-done.35.refs_7_ = bf16[128,1024]{1,0:T(8,128)(2,1)S(1)} collective-permute-done((bf16[128,1024]{1,0:T(8,128)(2,1)}, bf16[128,1024]{1,0:T(8,128)(2,1)S(1)}, u32[]{:S(2)}, u32[]{:S(2)}) %collective-permute-start.35) | collective-permute-done | bytes 262176 | tf_op jit(solution)/shard_map/ppermute | solution.py:16
  179.1 11.1 %forward_rows.1 = (bf16[1024,1024]{1,0:T(8,128)(2,1)}, f32[1024,1024]{1,0:T(8,128)}, f32[2,1024]{1,0:T(2,128)S(1)}) custom-call(bf16[1024,1024]{1,0:T(8,128)(2,1)S(1)} %turn.1.turned, f32[3,1024]{1,0:T(4,128)S(1)} %copy-done.12, bf16[1024,1024]{1,0:T(8,128)(2,1)} %bitcast.8, bf16[2,1024]{1,0:T(2,128)(2,1)S(1)} %collective-permute-done.14.halo, ...), custom_call_target="tpu_custom_call" | custom-call | flops 2147483648 | bytes 14680064 | tf_op jit(solution)/shard_map/forward_rows/pallas_call | solution.py:291
  191.6 4.1 %collective-permute-start.41 = (f32[2,1024]{1,0:T(2,128)S(1)}, f32[2,1024]{1,0:T(2,128)S(1)}, u32[]{:S(2)}, u32[]{:S(2)}) collective-permute-start(f32[2,1024]{1,0:T(2,128)S(1)} %get-tuple-element.157), channel_id=1, source_target_pairs={{2,0},{4,2},{6,4},{8,6},{10,8},{12,10},{14,12},{3,1},{5,3},{7,5},{... | collective-permute-start | bytes 24584 | tf_op jit(solution)/shard_map/ppermute | solution.py:21
  195.6 7.3 %collective-permute-done.40.refs_5_ = bf16[128,1024]{1,0:T(8,128)(2,1)S(1)} collective-permute-done((bf16[128,1024]{1,0:T(8,128)(2,1)S(1)}, bf16[128,1024]{1,0:T(8,128)(2,1)S(1)}, u32[]{:S(2)}, u32[]{:S(2)}) %collective-permute-start.40) | collective-permute-done | bytes 262176 | tf_op jit(solution)/shard_map/ppermute | solution.py:16
  207.0 2.6 %collective-permute-done.41.tail = f32[2,1024]{1,0:T(2,128)S(1)} collective-permute-done((f32[2,1024]{1,0:T(2,128)S(1)}, f32[2,1024]{1,0:T(2,128)S(1)}, u32[]{:S(2)}, u32[]{:S(2)}) %collective-permute-start.41) | collective-permute-done | bytes 8224 | tf_op jit(solution)/shard_map/ppermute | solution.py:21
  (144 shorter events, 55.9 us)
Async XLA Ops:
  24.8 30.1 %collective-permute-start.15 = (bf16[128,1024]{1,0:T(8,128)(2,1)S(1)}, bf16[128,1024]{1,0:T(8,128)(2,1)S(1)}, u32[]{:S(2)}, u32[]{:S(2)}) collective-permute-start(bf16[128,1024]{1,0:T(8,128)(2,1)S(1)} %get-tuple-element.102), channel_id=1, source_target_pairs={{0,2},{2,0},{4,6},{6,4},{8,10},{10,8},{12,14},{14,12},{1,3},{3,1},... | collective-permute-start | bytes 786440 | tf_op jit(solution)/shard_map/ppermute | solution.py:16
  28.3 27.9 %collective-permute-start.16 = (bf16[128,1024]{1,0:T(8,128)(2,1)S(1)}, bf16[128,1024]{1,0:T(8,128)(2,1)S(1)}, u32[]{:S(2)}, u32[]{:S(2)}) collective-permute-start(bf16[128,1024]{1,0:T(8,128)(2,1)S(1)} %get-tuple-element.104), channel_id=1, source_target_pairs={{0,4},{2,6},{4,0},{6,2},{8,12},{10,14},{12,8},{14,10},{1,5},{3,7},... | collective-permute-start | bytes 786440 | tf_op jit(solution)/shard_map/ppermute | solution.py:16
  37.6 30.4 %collective-permute-start.19 = (bf16[128,1024]{1,0:T(8,128)(2,1)}, bf16[128,1024]{1,0:T(8,128)(2,1)}, u32[]{:S(2)}, u32[]{:S(2)}) collective-permute-start(bf16[128,1024]{1,0:T(8,128)(2,1)} %get-tuple-element.110), channel_id=1, source_target_pairs={{0,10},{2,8},{4,14},{6,12},{8,2},{10,0},{12,6},{14,4},{1,11},{3,9}... | collective-permute-start | bytes 786440 | tf_op jit(solution)/shard_map/ppermute | solution.py:16
  39.8 28.2 %collective-permute-start.20 = (bf16[128,1024]{1,0:T(8,128)(2,1)}, bf16[128,1024]{1,0:T(8,128)(2,1)}, u32[]{:S(2)}, u32[]{:S(2)}) collective-permute-start(bf16[128,1024]{1,0:T(8,128)(2,1)} %get-tuple-element.112), channel_id=1, source_target_pairs={{0,12},{2,14},{4,8},{6,10},{8,4},{10,6},{12,0},{14,2},{1,13},{3,15... | collective-permute-start | bytes 786440 | tf_op jit(solution)/shard_map/ppermute | solution.py:16
  41.2 31.9 %collective-permute-start.18 = (bf16[128,1024]{1,0:T(8,128)(2,1)}, bf16[128,1024]{1,0:T(8,128)(2,1)}, u32[]{:S(2)}, u32[]{:S(2)}) collective-permute-start(bf16[128,1024]{1,0:T(8,128)(2,1)} %get-tuple-element.108), channel_id=1, source_target_pairs={{0,6},{2,4},{4,2},{6,0},{8,14},{10,12},{12,10},{14,8},{1,7},{3,5},... | collective-permute-start | bytes 786440 | tf_op jit(solution)/shard_map/ppermute | solution.py:16
  55.6 33.9 %collective-permute-start.21 = (bf16[128,1024]{1,0:T(8,128)(2,1)}, bf16[128,1024]{1,0:T(8,128)(2,1)}, u32[]{:S(2)}, u32[]{:S(2)}) collective-permute-start(bf16[128,1024]{1,0:T(8,128)(2,1)} %get-tuple-element.113), channel_id=1, source_target_pairs={{0,14},{2,12},{4,10},{6,8},{8,6},{10,4},{12,2},{14,0},{1,15},{3,13... | collective-permute-start | bytes 786440 | tf_op jit(solution)/shard_map/ppermute | solution.py:16
  56.9 32.6 %collective-permute-start.31 = (bf16[128,1024]{1,0:T(8,128)(2,1)}, bf16[128,1024]{1,0:T(8,128)(2,1)}, u32[]{:S(2)}, u32[]{:S(2)}) collective-permute-start(bf16[128,1024]{1,0:T(8,128)(2,1)} %get-tuple-element.136), channel_id=1, source_target_pairs={{0,2},{2,0},{4,6},{6,4},{8,10},{10,8},{12,14},{14,12},{1,3},{3,1},... | collective-permute-start | bytes 786440 | tf_op jit(solution)/shard_map/ppermute | solution.py:16
  68.0 33.1 %collective-permute-start.28 = (bf16[128,1024]{1,0:T(8,128)(2,1)}, bf16[128,1024]{1,0:T(8,128)(2,1)S(1)}, u32[]{:S(2)}, u32[]{:S(2)}) collective-permute-start(bf16[128,1024]{1,0:T(8,128)(2,1)} %get-tuple-element.130), channel_id=1, source_target_pairs={{0,8},{2,10},{4,12},{6,14},{8,0},{10,2},{12,4},{14,6},{1,9},{3,11}... | collective-permute-start | bytes 786440 | tf_op jit(solution)/shard_map/ppermute | solution.py:16
  68.0 38.7 %collective-permute-start.22 = (bf16[128,1024]{1,0:T(8,128)(2,1)}, bf16[128,1024]{1,0:T(8,128)(2,1)S(1)}, u32[]{:S(2)}, u32[]{:S(2)}) collective-permute-start(bf16[128,1024]{1,0:T(8,128)(2,1)} %get-tuple-element.117), channel_id=1, source_target_pairs={{0,10},{2,8},{4,14},{6,12},{8,2},{10,0},{12,6},{14,4},{1,11},{3,9}... | collective-permute-start | bytes 786440 | tf_op jit(solution)/shard_map/ppermute | solution.py:16
  73.0 35.9 %collective-permute-start.24 = (bf16[128,1024]{1,0:T(8,128)(2,1)}, bf16[128,1024]{1,0:T(8,128)(2,1)S(1)}, u32[]{:S(2)}, u32[]{:S(2)}) collective-permute-start(bf16[128,1024]{1,0:T(8,128)(2,1)} %get-tuple-element.121), channel_id=1, source_target_pairs={{0,4},{2,6},{4,0},{6,2},{8,12},{10,14},{12,8},{14,10},{1,5},{3,7},... | collective-permute-start | bytes 786440 | tf_op jit(solution)/shard_map/ppermute | solution.py:16
  89.5 40.3 %collective-permute-start.32 = (bf16[128,1024]{1,0:T(8,128)(2,1)S(1)}, bf16[128,1024]{1,0:T(8,128)(2,1)S(1)}, u32[]{:S(2)}, u32[]{:S(2)}) collective-permute-start(bf16[128,1024]{1,0:T(8,128)(2,1)S(1)} %copy-done.28), channel_id=1, source_target_pairs={{0,14},{2,12},{4,10},{6,8},{8,6},{10,4},{12,2},{14,0},{1,15},{3,13... | collective-permute-start | bytes 786440 | tf_op jit(solution)/shard_map/ppermute | solution.py:16
  89.5 40.3 %collective-permute-start.26 = (bf16[128,1024]{1,0:T(8,128)(2,1)S(1)}, bf16[128,1024]{1,0:T(8,128)(2,1)S(1)}, u32[]{:S(2)}, u32[]{:S(2)}) collective-permute-start(bf16[128,1024]{1,0:T(8,128)(2,1)S(1)} %copy-done.29), channel_id=1, source_target_pairs={{0,12},{2,14},{4,8},{6,10},{8,4},{10,6},{12,0},{14,2},{1,13},{3,15... | collective-permute-start | bytes 786440 | tf_op jit(solution)/shard_map/ppermute | solution.py:16
  101.1 31.1 %collective-permute-start.29 = (bf16[128,1024]{1,0:T(8,128)(2,1)S(1)}, bf16[128,1024]{1,0:T(8,128)(2,1)S(1)}, u32[]{:S(2)}, u32[]{:S(2)}) collective-permute-start(bf16[128,1024]{1,0:T(8,128)(2,1)S(1)} %copy-done.25), channel_id=1, source_target_pairs={{0,6},{2,4},{4,2},{6,0},{8,14},{10,12},{12,10},{14,8},{1,7},{3,5},... | collective-permute-start | bytes 786440 | tf_op jit(solution)/shard_map/ppermute | solution.py:16
  106.8 32.8 %collective-permute-start.23 = (bf16[128,1024]{1,0:T(8,128)(2,1)}, bf16[128,1024]{1,0:T(8,128)(2,1)S(1)}, u32[]{:S(2)}, u32[]{:S(2)}) collective-permute-start(bf16[128,1024]{1,0:T(8,128)(2,1)} %get-tuple-element.118), channel_id=1, source_target_pairs={{0,8},{2,10},{4,12},{6,14},{8,0},{10,2},{12,4},{14,6},{1,9},{3,11}... | collective-permute-start | bytes 786440 | tf_op jit(solution)/shard_map/ppermute | solution.py:16
  108.9 35.7 %collective-permute-start.25 = (bf16[128,1024]{1,0:T(8,128)(2,1)}, bf16[128,1024]{1,0:T(8,128)(2,1)S(1)}, u32[]{:S(2)}, u32[]{:S(2)}) collective-permute-start(bf16[128,1024]{1,0:T(8,128)(2,1)} %get-tuple-element.122), channel_id=1, source_target_pairs={{0,2},{2,0},{4,6},{6,4},{8,10},{10,8},{12,14},{14,12},{1,3},{3,1},... | collective-permute-start | bytes 786440 | tf_op jit(solution)/shard_map/ppermute | solution.py:16
  129.8 34.2 %collective-permute-start.33 = (bf16[128,1024]{1,0:T(8,128)(2,1)}, bf16[128,1024]{1,0:T(8,128)(2,1)S(1)}, u32[]{:S(2)}, u32[]{:S(2)}) collective-permute-start(bf16[128,1024]{1,0:T(8,128)(2,1)} %get-tuple-element.138), channel_id=1, source_target_pairs={{0,12},{2,14},{4,8},{6,10},{8,4},{10,6},{12,0},{14,2},{1,13},{3,15... | collective-permute-start | bytes 786440 | tf_op jit(solution)/shard_map/ppermute | solution.py:16
  132.2 25.7 %collective-permute-start.27 = (bf16[128,1024]{1,0:T(8,128)(2,1)}, bf16[128,1024]{1,0:T(8,128)(2,1)S(1)}, u32[]{:S(2)}, u32[]{:S(2)}) collective-permute-start(bf16[128,1024]{1,0:T(8,128)(2,1)} %get-tuple-element.126), channel_id=1, source_target_pairs={{0,10},{2,8},{4,14},{6,12},{8,2},{10,0},{12,6},{14,4},{1,11},{3,9}... | collective-permute-start | bytes 786440 | tf_op jit(solution)/shard_map/ppermute | solution.py:16
  132.2 29.1 %collective-permute-start.30 = (bf16[128,1024]{1,0:T(8,128)(2,1)}, bf16[128,1024]{1,0:T(8,128)(2,1)S(1)}, u32[]{:S(2)}, u32[]{:S(2)}) collective-permute-start(bf16[128,1024]{1,0:T(8,128)(2,1)} %get-tuple-element.132), channel_id=1, source_target_pairs={{0,4},{2,6},{4,0},{6,2},{8,12},{10,14},{12,8},{14,10},{1,5},{3,7},... | collective-permute-start | bytes 786440 | tf_op jit(solution)/shard_map/ppermute | solution.py:16
  139.6 24.6 %collective-permute-start.34 = (bf16[128,1024]{1,0:T(8,128)(2,1)}, bf16[128,1024]{1,0:T(8,128)(2,1)S(1)}, u32[]{:S(2)}, u32[]{:S(2)}) collective-permute-start(bf16[128,1024]{1,0:T(8,128)(2,1)} %get-tuple-element.140), channel_id=1, source_target_pairs={{0,6},{2,4},{4,2},{6,0},{8,14},{10,12},{12,10},{14,8},{1,7},{3,5},... | collective-permute-start | bytes 786440 | tf_op jit(solution)/shard_map/ppermute | solution.py:16
  144.6 34.4 %collective-permute-start.35 = (bf16[128,1024]{1,0:T(8,128)(2,1)}, bf16[128,1024]{1,0:T(8,128)(2,1)S(1)}, u32[]{:S(2)}, u32[]{:S(2)}) collective-permute-start(bf16[128,1024]{1,0:T(8,128)(2,1)} %get-tuple-element.142), channel_id=1, source_target_pairs={{0,14},{2,12},{4,10},{6,8},{8,6},{10,4},{12,2},{14,0},{1,15},{3,13... | collective-permute-start | bytes 786440 | tf_op jit(solution)/shard_map/ppermute | solution.py:16
  157.9 32.3 %collective-permute-start.36 = (bf16[128,1024]{1,0:T(8,128)(2,1)}, bf16[128,1024]{1,0:T(8,128)(2,1)S(1)}, u32[]{:S(2)}, u32[]{:S(2)}) collective-permute-start(bf16[128,1024]{1,0:T(8,128)(2,1)} %get-tuple-element.148), channel_id=1, source_target_pairs={{0,8},{2,10},{4,12},{6,14},{8,0},{10,2},{12,4},{14,6},{1,9},{3,11}... | collective-permute-start | bytes 786440 | tf_op jit(solution)/shard_map/ppermute | solution.py:16
  161.4 28.9 %collective-permute-start.37 = (bf16[128,1024]{1,0:T(8,128)(2,1)}, bf16[128,1024]{1,0:T(8,128)(2,1)S(1)}, u32[]{:S(2)}, u32[]{:S(2)}) collective-permute-start(bf16[128,1024]{1,0:T(8,128)(2,1)} %get-tuple-element.150), channel_id=1, source_target_pairs={{0,2},{2,0},{4,6},{6,4},{8,10},{10,8},{12,14},{14,12},{1,3},{3,1},... | collective-permute-start | bytes 786440 | tf_op jit(solution)/shard_map/ppermute | solution.py:16
  164.0 27.6 %collective-permute-start.38 = (bf16[128,1024]{1,0:T(8,128)(2,1)S(1)}, bf16[128,1024]{1,0:T(8,128)(2,1)S(1)}, u32[]{:S(2)}, u32[]{:S(2)}) collective-permute-start(bf16[128,1024]{1,0:T(8,128)(2,1)S(1)} %copy-done.30), channel_id=1, source_target_pairs={{0,10},{2,8},{4,14},{6,12},{8,2},{10,0},{12,6},{14,4},{1,11},{3,9}... | collective-permute-start | bytes 786440 | tf_op jit(solution)/shard_map/ppermute | solution.py:16
  164.2 31.4 %collective-permute-start.39 = (bf16[128,1024]{1,0:T(8,128)(2,1)S(1)}, bf16[128,1024]{1,0:T(8,128)(2,1)S(1)}, u32[]{:S(2)}, u32[]{:S(2)}) collective-permute-start(bf16[128,1024]{1,0:T(8,128)(2,1)S(1)} %copy-done.27), channel_id=1, source_target_pairs={{0,4},{2,6},{4,0},{6,2},{8,12},{10,14},{12,8},{14,10},{1,5},{3,7},... | collective-permute-start | bytes 786440 | tf_op jit(solution)/shard_map/ppermute | solution.py:16
  (51 other events, 747.5 us)

commit v4 on v3

--- a/solution.py
+++ b/solution.py
@@ -86,7 +86,7 @@
 def spread_peer_call(core, mine, other, values):
     half, block = mine.shape
     channels = values.shape[1]
-    width = min(channels, 512)
+    width = channels
     return call(
         spread_peer_body,
         "spread_peer",

time: 212 us -> 210 us (level)
  transfers between devices with their start and end apart: 44 -> 44, of which waited for: 15 -> 16; matrix products, arithmetic and copies ran while one was open for 0% -> 0% of each run, Pallas kernels for 25% -> 25%
where the time goes in v4:
time: 210 us
  waiting for transfers between devices  83.6 us (40%)
  starting transfers between devices  65.3 us (31%)
  Pallas kernels  53.6 us (26%)
  local copies, waits for them, and re-layouts  6.19 us (3%)
    ppermute x35, waiting for transfers between devices, exchange(): lax.ppermute(block, 'seq', [(i, i ^ mask) for i in range(lax.axis_size('s...  80.9 us
    ppermute x35, starting transfers between devices, exchange(): lax.ppermute(block, 'seq', [(i, i ^ mask) for i in range(lax.axis_size('s...  55.6 us
    pallas_call x2, Pallas kernels, middle_call(): call(functools.partial(middle_body, peers, side // peers, with_grad), 'mi...  16.3 us
    pallas_call x1, Pallas kernels, forward_call(): call(functools.partial(forward_body, peers), 'forward_rows', (channels //...  11.1 us
    pallas_call x1, Pallas kernels, spread_gated_call(): call(functools.partial(spread_gated_body, peers), 'spread_gated', (channe...  10 us
    pallas_call x7, Pallas kernels, spread_peer_call(): call(spread_peer_body, 'spread_peer', (channels // width,), [whole((half,...  9.18 us
    ppermute x2, starting transfers between devices, shifted(): lax.ppermute(block, 'seq', [(i - distance, i) for i in devices if i - dis...  8.67 us
    unnamed x62, local copies, waits for them, and re-layouts  5.27 us
  transfers between devices with their start and end apart: 44, of which 16 were waited for; matrix products, arithmetic and copies ran while one was open for 0% of the time, Pallas kernels for 25%

profile of v4, /device:TPU:14, one launch (start us, length us, event | category | flops | bytes accessed | tf_op | source)
XLA Modules:
  0.0 209.9 jit_solution(551738343323492452)
XLA Ops:
  1.6 2.7 %collective-permute-start = (bf16[64,1024]{1,0:T(8,128)(2,1)S(1)}, bf16[64,1024]{1,0:T(8,128)(2,1)S(1)}, u32[]{:S(2)}, u32[]{:S(2)}) collective-permute-start(bf16[64,1024]{1,0:T(8,128)(2,1)S(1)} %constant_dynamic-slice_fusion), channel_id=1, source_target_pairs={{0,8},{2,10},{4,12},{6,14},{8,0},{10,2},{12,4},{14,6},{1,9},{3,11}... | collective-permute-start | bytes 393224 | tf_op jit(solution)/shard_map/ppermute | solution.py:16
  29.5 4.8 %collective-permute-start.14 = (bf16[2,1024]{1,0:T(2,128)(2,1)S(1)}, bf16[2,1024]{1,0:T(2,128)(2,1)S(1)}, u32[]{:S(2)}, u32[]{:S(2)}) collective-permute-start(bf16[2,1024]{1,0:T(2,128)(2,1)S(1)} %slice_bitcast_fusion), channel_id=1, source_target_pairs={{0,2},{2,4},{4,6},{6,8},{8,10},{10,12},{12,14},{1,3},{3,5},{5,7},{... | collective-permute-start | bytes 12296 | tf_op jit(solution)/shard_map/ppermute | solution.py:21
  39.2 3.7 %collective-permute-start.18 = (bf16[128,1024]{1,0:T(8,128)(2,1)}, bf16[128,1024]{1,0:T(8,128)(2,1)}, u32[]{:S(2)}, u32[]{:S(2)}) collective-permute-start(bf16[128,1024]{1,0:T(8,128)(2,1)} %get-tuple-element.108), channel_id=1, source_target_pairs={{0,6},{2,4},{4,2},{6,0},{8,14},{10,12},{12,10},{14,8},{1,7},{3,5},... | collective-permute-start | bytes 786440 | tf_op jit(solution)/shard_map/ppermute | solution.py:16
  42.9 10.0 %spread_gated.1 = (bf16[128,1024]{1,0:T(8,128)(2,1)}, bf16[128,1024]{1,0:T(8,128)(2,1)}, bf16[128,1024]{1,0:T(8,128)(2,1)}, bf16[128,1024]{1,0:T(8,128)(2,1)}, b...) custom-call(bf16[1024,1024]{1,0:T(8,128)(2,1)S(1)} %bitcast.16, ...), custom_call_target="tpu_custom_call" | custom-call | flops 2147483648 | bytes 8388608 | tf_op jit(solution)/shard_map/spread_gated/pallas_call | solution.py:135
  57.1 9.2 %collective-permute-done.20.refs_6_.refs_14_ = bf16[128,1024]{1,0:T(8,128)(2,1)} collective-permute-done((bf16[128,1024]{1,0:T(8,128)(2,1)}, bf16[128,1024]{1,0:T(8,128)(2,1)}, u32[]{:S(2)}, u32[]{:S(2)}) %collective-permute-start.20) | collective-permute-done | bytes 262176 | tf_op jit(solution)/shard_map/ppermute | solution.py:16
  66.3 5.0 %collective-permute-start.22 = (bf16[128,1024]{1,0:T(8,128)(2,1)}, bf16[128,1024]{1,0:T(8,128)(2,1)S(1)}, u32[]{:S(2)}, u32[]{:S(2)}) collective-permute-start(bf16[128,1024]{1,0:T(8,128)(2,1)} %get-tuple-element.117), channel_id=1, source_target_pairs={{0,10},{2,8},{4,14},{6,12},{8,2},{10,0},{12,6},{14,4},{1,11},{3,9}... | collective-permute-start | bytes 786440 | tf_op jit(solution)/shard_map/ppermute | solution.py:16
  73.5 13.8 %collective-permute-done.21.refs_7_.refs_15_ = bf16[128,1024]{1,0:T(8,128)(2,1)} collective-permute-done((bf16[128,1024]{1,0:T(8,128)(2,1)}, bf16[128,1024]{1,0:T(8,128)(2,1)}, u32[]{:S(2)}, u32[]{:S(2)}) %collective-permute-start.21) | collective-permute-done | bytes 262176 | tf_op jit(solution)/shard_map/ppermute | solution.py:16
  87.5 7.8 %middle.1 = (bf16[128,1024]{1,0:T(8,128)(2,1)}, bf16[128,1024]{1,0:T(8,128)(2,1)}, bf16[128,1024]{1,0:T(8,128)(2,1)}, bf16[128,1024]{1,0:T(8,128)(2,1)}, bf16[12...) custom-call(s32[1]{0:T(128)} %bitcast.4.place, ...), custom_call_target="tpu_custom_call" | custom-call | flops 2684354560 | bytes 8388608 | tf_op jit(solution)/shard_map/middle/pallas_call | solution.py:206
  95.4 3.9 %collective-permute-done.28.refs_4_ = bf16[128,1024]{1,0:T(8,128)(2,1)S(1)} collective-permute-done((bf16[128,1024]{1,0:T(8,128)(2,1)}, bf16[128,1024]{1,0:T(8,128)(2,1)S(1)}, u32[]{:S(2)}, u32[]{:S(2)}) %collective-permute-start.28) | collective-permute-done | bytes 262176 | tf_op jit(solution)/shard_map/ppermute | solution.py:16
  99.3 4.1 %collective-permute-start.29 = (bf16[128,1024]{1,0:T(8,128)(2,1)S(1)}, bf16[128,1024]{1,0:T(8,128)(2,1)S(1)}, u32[]{:S(2)}, u32[]{:S(2)}) collective-permute-start(bf16[128,1024]{1,0:T(8,128)(2,1)S(1)} %copy-done.25), channel_id=1, source_target_pairs={{0,6},{2,4},{4,2},{6,0},{8,14},{10,12},{12,10},{14,8},{1,7},{3,5},... | collective-permute-start | bytes 786440 | tf_op jit(solution)/shard_map/ppermute | solution.py:16
  107.1 2.6 %collective-permute-start.25 = (bf16[128,1024]{1,0:T(8,128)(2,1)}, bf16[128,1024]{1,0:T(8,128)(2,1)S(1)}, u32[]{:S(2)}, u32[]{:S(2)}) collective-permute-start(bf16[128,1024]{1,0:T(8,128)(2,1)} %get-tuple-element.122), channel_id=1, source_target_pairs={{0,2},{2,0},{4,6},{6,4},{8,10},{10,8},{12,14},{14,12},{1,3},{3,1},... | collective-permute-start | bytes 786440 | tf_op jit(solution)/shard_map/ppermute | solution.py:16
  109.7 18.3 %collective-permute-done.26.refs_6_ = bf16[128,1024]{1,0:T(8,128)(2,1)S(1)} collective-permute-done((bf16[128,1024]{1,0:T(8,128)(2,1)S(1)}, bf16[128,1024]{1,0:T(8,128)(2,1)S(1)}, u32[]{:S(2)}, u32[]{:S(2)}) %collective-permute-start.26) | collective-permute-done | bytes 262176 | tf_op jit(solution)/shard_map/ppermute | solution.py:16
  130.5 3.3 %collective-permute-start.30 = (bf16[128,1024]{1,0:T(8,128)(2,1)}, bf16[128,1024]{1,0:T(8,128)(2,1)S(1)}, u32[]{:S(2)}, u32[]{:S(2)}) collective-permute-start(bf16[128,1024]{1,0:T(8,128)(2,1)} %get-tuple-element.132), channel_id=1, source_target_pairs={{0,4},{2,6},{4,0},{6,2},{8,12},{10,14},{12,8},{14,10},{1,5},{3,7},... | collective-permute-start | bytes 786440 | tf_op jit(solution)/shard_map/ppermute | solution.py:16
  133.8 4.1 %collective-permute-done.23.refs_1_ = bf16[128,1024]{1,0:T(8,128)(2,1)S(1)} collective-permute-done((bf16[128,1024]{1,0:T(8,128)(2,1)}, bf16[128,1024]{1,0:T(8,128)(2,1)S(1)}, u32[]{:S(2)}, u32[]{:S(2)}) %collective-permute-start.23) | collective-permute-done | bytes 262176 | tf_op jit(solution)/shard_map/ppermute | solution.py:16
  137.9 4.8 %collective-permute-start.34 = (bf16[128,1024]{1,0:T(8,128)(2,1)}, bf16[128,1024]{1,0:T(8,128)(2,1)S(1)}, u32[]{:S(2)}, u32[]{:S(2)}) collective-permute-start(bf16[128,1024]{1,0:T(8,128)(2,1)} %get-tuple-element.140), channel_id=1, source_target_pairs={{0,6},{2,4},{4,2},{6,0},{8,14},{10,12},{12,10},{14,8},{1,7},{3,5},... | collective-permute-start | bytes 786440 | tf_op jit(solution)/shard_map/ppermute | solution.py:16
  143.2 8.4 %middle_grad.1 = (bf16[8,128,1024]{2,1,0:T(8,128)(2,1)}, bf16[128,1024]{1,0:T(8,128)(2,1)}, bf16[128,1024]{1,0:T(8,128)(2,1)}, bf16[128,1024]{1,0:T(8,128)(2,1)}...) custom-call(s32[1]{0:T(128)} %bitcast.4.place, ...), custom_call_target="tpu_custom_call" | custom-call | flops 3758096384 | bytes 12582912 | tf_op jit(solution)/shard_map/middle_grad/pallas_call | solution.py:206
  151.7 4.6 %collective-permute-done.27.refs_3_ = bf16[128,1024]{1,0:T(8,128)(2,1)S(1)} collective-permute-done((bf16[128,1024]{1,0:T(8,128)(2,1)}, bf16[128,1024]{1,0:T(8,128)(2,1)S(1)}, u32[]{:S(2)}, u32[]{:S(2)}) %collective-permute-start.27) | collective-permute-done | bytes 262176 | tf_op jit(solution)/shard_map/ppermute | solution.py:16
  156.2 3.3 %collective-permute-start.36 = (bf16[128,1024]{1,0:T(8,128)(2,1)}, bf16[128,1024]{1,0:T(8,128)(2,1)S(1)}, u32[]{:S(2)}, u32[]{:S(2)}) collective-permute-start(bf16[128,1024]{1,0:T(8,128)(2,1)} %get-tuple-element.148), channel_id=1, source_target_pairs={{0,8},{2,10},{4,12},{6,14},{8,0},{10,2},{12,4},{14,6},{1,9},{3,11}... | collective-permute-start | bytes 786440 | tf_op jit(solution)/shard_map/ppermute | solution.py:16
  162.4 3.2 %collective-permute-start.39 = (bf16[128,1024]{1,0:T(8,128)(2,1)S(1)}, bf16[128,1024]{1,0:T(8,128)(2,1)S(1)}, u32[]{:S(2)}, u32[]{:S(2)}) collective-permute-start(bf16[128,1024]{1,0:T(8,128)(2,1)S(1)} %copy-done.27), channel_id=1, source_target_pairs={{0,4},{2,6},{4,0},{6,2},{8,12},{10,14},{12,8},{14,10},{1,5},{3,7},... | collective-permute-start | bytes 786440 | tf_op jit(solution)/shard_map/ppermute | solution.py:16
  165.6 11.6 %collective-permute-done.35.refs_7_ = bf16[128,1024]{1,0:T(8,128)(2,1)S(1)} collective-permute-done((bf16[128,1024]{1,0:T(8,128)(2,1)}, bf16[128,1024]{1,0:T(8,128)(2,1)S(1)}, u32[]{:S(2)}, u32[]{:S(2)}) %collective-permute-start.35) | collective-permute-done | bytes 262176 | tf_op jit(solution)/shard_map/ppermute | solution.py:16
  177.3 11.1 %forward_rows.1 = (bf16[1024,1024]{1,0:T(8,128)(2,1)}, f32[1024,1024]{1,0:T(8,128)}, f32[2,1024]{1,0:T(2,128)S(1)}) custom-call(bf16[1024,1024]{1,0:T(8,128)(2,1)S(1)} %turn.1.turned, f32[3,1024]{1,0:T(4,128)S(1)} %copy-done.12, bf16[1024,1024]{1,0:T(8,128)(2,1)} %bitcast.8, bf16[2,1024]{1,0:T(2,128)(2,1)S(1)} %collective-permute-done.14.halo, ...), custom_call_target="tpu_custom_call" | custom-call | flops 2147483648 | bytes 14680064 | tf_op jit(solution)/shard_map/forward_rows/pallas_call | solution.py:291
  189.8 3.9 %collective-permute-start.41 = (f32[2,1024]{1,0:T(2,128)S(1)}, f32[2,1024]{1,0:T(2,128)S(1)}, u32[]{:S(2)}, u32[]{:S(2)}) collective-permute-start(f32[2,1024]{1,0:T(2,128)S(1)} %get-tuple-element.157), channel_id=1, source_target_pairs={{2,0},{4,2},{6,4},{8,6},{10,8},{12,10},{14,12},{3,1},{5,3},{7,5},{... | collective-permute-start | bytes 24584 | tf_op jit(solution)/shard_map/ppermute | solution.py:21
  193.8 7.4 %collective-permute-done.40.refs_5_ = bf16[128,1024]{1,0:T(8,128)(2,1)S(1)} collective-permute-done((bf16[128,1024]{1,0:T(8,128)(2,1)S(1)}, bf16[128,1024]{1,0:T(8,128)(2,1)S(1)}, u32[]{:S(2)}, u32[]{:S(2)}) %collective-permute-start.40) | collective-permute-done | bytes 262176 | tf_op jit(solution)/shard_map/ppermute | solution.py:16
  205.2 2.7 %collective-permute-done.41.tail = f32[2,1024]{1,0:T(2,128)S(1)} collective-permute-done((f32[2,1024]{1,0:T(2,128)S(1)}, f32[2,1024]{1,0:T(2,128)S(1)}, u32[]{:S(2)}, u32[]{:S(2)}) %collective-permute-start.41) | collective-permute-done | bytes 8224 | tf_op jit(solution)/shard_map/ppermute | solution.py:21
  (144 shorter events, 54.5 us)
Async XLA Ops:
  24.1 28.9 %collective-permute-start.15 = (bf16[128,1024]{1,0:T(8,128)(2,1)S(1)}, bf16[128,1024]{1,0:T(8,128)(2,1)S(1)}, u32[]{:S(2)}, u32[]{:S(2)}) collective-permute-start(bf16[128,1024]{1,0:T(8,128)(2,1)S(1)} %get-tuple-element.102), channel_id=1, source_target_pairs={{0,2},{2,0},{4,6},{6,4},{8,10},{10,8},{12,14},{14,12},{1,3},{3,1},... | collective-permute-start | bytes 786440 | tf_op jit(solution)/shard_map/ppermute | solution.py:16
  27.3 26.9 %collective-permute-start.16 = (bf16[128,1024]{1,0:T(8,128)(2,1)S(1)}, bf16[128,1024]{1,0:T(8,128)(2,1)S(1)}, u32[]{:S(2)}, u32[]{:S(2)}) collective-permute-start(bf16[128,1024]{1,0:T(8,128)(2,1)S(1)} %get-tuple-element.104), channel_id=1, source_target_pairs={{0,4},{2,6},{4,0},{6,2},{8,12},{10,14},{12,8},{14,10},{1,5},{3,7},... | collective-permute-start | bytes 786440 | tf_op jit(solution)/shard_map/ppermute | solution.py:16
  35.8 30.4 %collective-permute-start.19 = (bf16[128,1024]{1,0:T(8,128)(2,1)}, bf16[128,1024]{1,0:T(8,128)(2,1)}, u32[]{:S(2)}, u32[]{:S(2)}) collective-permute-start(bf16[128,1024]{1,0:T(8,128)(2,1)} %get-tuple-element.110), channel_id=1, source_target_pairs={{0,10},{2,8},{4,14},{6,12},{8,2},{10,0},{12,6},{14,4},{1,11},{3,9}... | collective-permute-start | bytes 786440 | tf_op jit(solution)/shard_map/ppermute | solution.py:16
  38.0 28.3 %collective-permute-start.20 = (bf16[128,1024]{1,0:T(8,128)(2,1)}, bf16[128,1024]{1,0:T(8,128)(2,1)}, u32[]{:S(2)}, u32[]{:S(2)}) collective-permute-start(bf16[128,1024]{1,0:T(8,128)(2,1)} %get-tuple-element.112), channel_id=1, source_target_pairs={{0,12},{2,14},{4,8},{6,10},{8,4},{10,6},{12,0},{14,2},{1,13},{3,15... | collective-permute-start | bytes 786440 | tf_op jit(solution)/shard_map/ppermute | solution.py:16
  39.2 32.0 %collective-permute-start.18 = (bf16[128,1024]{1,0:T(8,128)(2,1)}, bf16[128,1024]{1,0:T(8,128)(2,1)}, u32[]{:S(2)}, u32[]{:S(2)}) collective-permute-start(bf16[128,1024]{1,0:T(8,128)(2,1)} %get-tuple-element.108), channel_id=1, source_target_pairs={{0,6},{2,4},{4,2},{6,0},{8,14},{10,12},{12,10},{14,8},{1,7},{3,5},... | collective-permute-start | bytes 786440 | tf_op jit(solution)/shard_map/ppermute | solution.py:16
  53.7 33.7 %collective-permute-start.21 = (bf16[128,1024]{1,0:T(8,128)(2,1)}, bf16[128,1024]{1,0:T(8,128)(2,1)}, u32[]{:S(2)}, u32[]{:S(2)}) collective-permute-start(bf16[128,1024]{1,0:T(8,128)(2,1)} %get-tuple-element.113), channel_id=1, source_target_pairs={{0,14},{2,12},{4,10},{6,8},{8,6},{10,4},{12,2},{14,0},{1,15},{3,13... | collective-permute-start | bytes 786440 | tf_op jit(solution)/shard_map/ppermute | solution.py:16
  54.9 32.4 %collective-permute-start.31 = (bf16[128,1024]{1,0:T(8,128)(2,1)}, bf16[128,1024]{1,0:T(8,128)(2,1)}, u32[]{:S(2)}, u32[]{:S(2)}) collective-permute-start(bf16[128,1024]{1,0:T(8,128)(2,1)} %get-tuple-element.136), channel_id=1, source_target_pairs={{0,2},{2,0},{4,6},{6,4},{8,10},{10,8},{12,14},{14,12},{1,3},{3,1},... | collective-permute-start | bytes 786440 | tf_op jit(solution)/shard_map/ppermute | solution.py:16
  66.3 33.1 %collective-permute-start.28 = (bf16[128,1024]{1,0:T(8,128)(2,1)}, bf16[128,1024]{1,0:T(8,128)(2,1)S(1)}, u32[]{:S(2)}, u32[]{:S(2)}) collective-permute-start(bf16[128,1024]{1,0:T(8,128)(2,1)} %get-tuple-element.130), channel_id=1, source_target_pairs={{0,8},{2,10},{4,12},{6,14},{8,0},{10,2},{12,4},{14,6},{1,9},{3,11}... | collective-permute-start | bytes 786440 | tf_op jit(solution)/shard_map/ppermute | solution.py:16
  66.3 38.7 %collective-permute-start.22 = (bf16[128,1024]{1,0:T(8,128)(2,1)}, bf16[128,1024]{1,0:T(8,128)(2,1)S(1)}, u32[]{:S(2)}, u32[]{:S(2)}) collective-permute-start(bf16[128,1024]{1,0:T(8,128)(2,1)} %get-tuple-element.117), channel_id=1, source_target_pairs={{0,10},{2,8},{4,14},{6,12},{8,2},{10,0},{12,6},{14,4},{1,11},{3,9}... | collective-permute-start | bytes 786440 | tf_op jit(solution)/shard_map/ppermute | solution.py:16
  71.2 35.9 %collective-permute-start.24 = (bf16[128,1024]{1,0:T(8,128)(2,1)}, bf16[128,1024]{1,0:T(8,128)(2,1)S(1)}, u32[]{:S(2)}, u32[]{:S(2)}) collective-permute-start(bf16[128,1024]{1,0:T(8,128)(2,1)} %get-tuple-element.121), channel_id=1, source_target_pairs={{0,4},{2,6},{4,0},{6,2},{8,12},{10,14},{12,8},{14,10},{1,5},{3,7},... | collective-permute-start | bytes 786440 | tf_op jit(solution)/shard_map/ppermute | solution.py:16
  87.3 40.7 %collective-permute-start.32 = (bf16[128,1024]{1,0:T(8,128)(2,1)S(1)}, bf16[128,1024]{1,0:T(8,128)(2,1)S(1)}, u32[]{:S(2)}, u32[]{:S(2)}) collective-permute-start(bf16[128,1024]{1,0:T(8,128)(2,1)S(1)} %copy-done.28), channel_id=1, source_target_pairs={{0,14},{2,12},{4,10},{6,8},{8,6},{10,4},{12,2},{14,0},{1,15},{3,13... | collective-permute-start | bytes 786440 | tf_op jit(solution)/shard_map/ppermute | solution.py:16
  87.5 40.6 %collective-permute-start.26 = (bf16[128,1024]{1,0:T(8,128)(2,1)S(1)}, bf16[128,1024]{1,0:T(8,128)(2,1)S(1)}, u32[]{:S(2)}, u32[]{:S(2)}) collective-permute-start(bf16[128,1024]{1,0:T(8,128)(2,1)S(1)} %copy-done.29), channel_id=1, source_target_pairs={{0,12},{2,14},{4,8},{6,10},{8,4},{10,6},{12,0},{14,2},{1,13},{3,15... | collective-permute-start | bytes 786440 | tf_op jit(solution)/shard_map/ppermute | solution.py:16
  99.3 31.2 %collective-permute-start.29 = (bf16[128,1024]{1,0:T(8,128)(2,1)S(1)}, bf16[128,1024]{1,0:T(8,128)(2,1)S(1)}, u32[]{:S(2)}, u32[]{:S(2)}) collective-permute-start(bf16[128,1024]{1,0:T(8,128)(2,1)S(1)} %copy-done.25), channel_id=1, source_target_pairs={{0,6},{2,4},{4,2},{6,0},{8,14},{10,12},{12,10},{14,8},{1,7},{3,5},... | collective-permute-start | bytes 786440 | tf_op jit(solution)/shard_map/ppermute | solution.py:16
  105.0 33.0 %collective-permute-start.23 = (bf16[128,1024]{1,0:T(8,128)(2,1)}, bf16[128,1024]{1,0:T(8,128)(2,1)S(1)}, u32[]{:S(2)}, u32[]{:S(2)}) collective-permute-start(bf16[128,1024]{1,0:T(8,128)(2,1)} %get-tuple-element.118), channel_id=1, source_target_pairs={{0,8},{2,10},{4,12},{6,14},{8,0},{10,2},{12,4},{14,6},{1,9},{3,11}... | collective-permute-start | bytes 786440 | tf_op jit(solution)/shard_map/ppermute | solution.py:16
  107.1 35.6 %collective-permute-start.25 = (bf16[128,1024]{1,0:T(8,128)(2,1)}, bf16[128,1024]{1,0:T(8,128)(2,1)S(1)}, u32[]{:S(2)}, u32[]{:S(2)}) collective-permute-start(bf16[128,1024]{1,0:T(8,128)(2,1)} %get-tuple-element.122), channel_id=1, source_target_pairs={{0,2},{2,0},{4,6},{6,4},{8,10},{10,8},{12,14},{14,12},{1,3},{3,1},... | collective-permute-start | bytes 786440 | tf_op jit(solution)/shard_map/ppermute | solution.py:16
  128.0 34.2 %collective-permute-start.33 = (bf16[128,1024]{1,0:T(8,128)(2,1)}, bf16[128,1024]{1,0:T(8,128)(2,1)S(1)}, u32[]{:S(2)}, u32[]{:S(2)}) collective-permute-start(bf16[128,1024]{1,0:T(8,128)(2,1)} %get-tuple-element.138), channel_id=1, source_target_pairs={{0,12},{2,14},{4,8},{6,10},{8,4},{10,6},{12,0},{14,2},{1,13},{3,15... | collective-permute-start | bytes 786440 | tf_op jit(solution)/shard_map/ppermute | solution.py:16
  130.5 25.7 %collective-permute-start.27 = (bf16[128,1024]{1,0:T(8,128)(2,1)}, bf16[128,1024]{1,0:T(8,128)(2,1)S(1)}, u32[]{:S(2)}, u32[]{:S(2)}) collective-permute-start(bf16[128,1024]{1,0:T(8,128)(2,1)} %get-tuple-element.126), channel_id=1, source_target_pairs={{0,10},{2,8},{4,14},{6,12},{8,2},{10,0},{12,6},{14,4},{1,11},{3,9}... | collective-permute-start | bytes 786440 | tf_op jit(solution)/shard_map/ppermute | solution.py:16
  130.5 29.0 %collective-permute-start.30 = (bf16[128,1024]{1,0:T(8,128)(2,1)}, bf16[128,1024]{1,0:T(8,128)(2,1)S(1)}, u32[]{:S(2)}, u32[]{:S(2)}) collective-permute-start(bf16[128,1024]{1,0:T(8,128)(2,1)} %get-tuple-element.132), channel_id=1, source_target_pairs={{0,4},{2,6},{4,0},{6,2},{8,12},{10,14},{12,8},{14,10},{1,5},{3,7},... | collective-permute-start | bytes 786440 | tf_op jit(solution)/shard_map/ppermute | solution.py:16
  137.9 24.4 %collective-permute-start.34 = (bf16[128,1024]{1,0:T(8,128)(2,1)}, bf16[128,1024]{1,0:T(8,128)(2,1)S(1)}, u32[]{:S(2)}, u32[]{:S(2)}) collective-permute-start(bf16[128,1024]{1,0:T(8,128)(2,1)} %get-tuple-element.140), channel_id=1, source_target_pairs={{0,6},{2,4},{4,2},{6,0},{8,14},{10,12},{12,10},{14,8},{1,7},{3,5},... | collective-permute-start | bytes 786440 | tf_op jit(solution)/shard_map/ppermute | solution.py:16
  142.8 34.4 %collective-permute-start.35 = (bf16[128,1024]{1,0:T(8,128)(2,1)}, bf16[128,1024]{1,0:T(8,128)(2,1)S(1)}, u32[]{:S(2)}, u32[]{:S(2)}) collective-permute-start(bf16[128,1024]{1,0:T(8,128)(2,1)} %get-tuple-element.142), channel_id=1, source_target_pairs={{0,14},{2,12},{4,10},{6,8},{8,6},{10,4},{12,2},{14,0},{1,15},{3,13... | collective-permute-start | bytes 786440 | tf_op jit(solution)/shard_map/ppermute | solution.py:16
  156.2 32.1 %collective-permute-start.36 = (bf16[128,1024]{1,0:T(8,128)(2,1)}, bf16[128,1024]{1,0:T(8,128)(2,1)S(1)}, u32[]{:S(2)}, u32[]{:S(2)}) collective-permute-start(bf16[128,1024]{1,0:T(8,128)(2,1)} %get-tuple-element.148), channel_id=1, source_target_pairs={{0,8},{2,10},{4,12},{6,14},{8,0},{10,2},{12,4},{14,6},{1,9},{3,11}... | collective-permute-start | bytes 786440 | tf_op jit(solution)/shard_map/ppermute | solution.py:16
  159.6 28.9 %collective-permute-start.37 = (bf16[128,1024]{1,0:T(8,128)(2,1)}, bf16[128,1024]{1,0:T(8,128)(2,1)S(1)}, u32[]{:S(2)}, u32[]{:S(2)}) collective-permute-start(bf16[128,1024]{1,0:T(8,128)(2,1)} %get-tuple-element.150), channel_id=1, source_target_pairs={{0,2},{2,0},{4,6},{6,4},{8,10},{10,8},{12,14},{14,12},{1,3},{3,1},... | collective-permute-start | bytes 786440 | tf_op jit(solution)/shard_map/ppermute | solution.py:16
  162.3 27.6 %collective-permute-start.38 = (bf16[128,1024]{1,0:T(8,128)(2,1)S(1)}, bf16[128,1024]{1,0:T(8,128)(2,1)S(1)}, u32[]{:S(2)}, u32[]{:S(2)}) collective-permute-start(bf16[128,1024]{1,0:T(8,128)(2,1)S(1)} %copy-done.30), channel_id=1, source_target_pairs={{0,10},{2,8},{4,14},{6,12},{8,2},{10,0},{12,6},{14,4},{1,11},{3,9}... | collective-permute-start | bytes 786440 | tf_op jit(solution)/shard_map/ppermute | solution.py:16
  162.4 31.4 %collective-permute-start.39 = (bf16[128,1024]{1,0:T(8,128)(2,1)S(1)}, bf16[128,1024]{1,0:T(8,128)(2,1)S(1)}, u32[]{:S(2)}, u32[]{:S(2)}) collective-permute-start(bf16[128,1024]{1,0:T(8,128)(2,1)S(1)} %copy-done.27), channel_id=1, source_target_pairs={{0,4},{2,6},{4,0},{6,2},{8,12},{10,14},{12,8},{14,10},{1,5},{3,7},... | collective-permute-start | bytes 786440 | tf_op jit(solution)/shard_map/ppermute | solution.py:16
  (51 other events, 733.8 us)

commit v5 on v4

--- a/solution.py
+++ b/solution.py
@@ -107,7 +107,7 @@
 def spread_own_call(row, values):
     share, block = row.shape
     channels = values.shape[1]
-    width = min(channels, 512)
+    width = channels
     return call(
         spread_own_body,
         "spread_own",
@@ -287,7 +287,7 @@
 def forward_call(turned, weight, tokens, halo, cot, pieces):
     length, channels = tokens.shape
     peers, share = len(pieces), pieces[0].shape[0]
-    width = min(channels, 128)
+    width = min(channels, 256)
     return call(
         functools.partial(forward_body, peers),
         "forward_rows",

time: 210 us -> 210 us (level)
  Pallas kernels: 53.6 us -> 51.3 us
  transfers between devices with their start and end apart: 44 -> 44, of which waited for: 16 -> 16; matrix products, arithmetic and copies ran while one was open for 0% -> 0% of each run, Pallas kernels for 25% -> 24%
where the time goes in v5:
time: 210 us
  waiting for transfers between devices  84.8 us (40%)
  starting transfers between devices  66.5 us (32%)
  Pallas kernels  51.3 us (24%)
  local copies, waits for them, and re-layouts  6.19 us (3%)
    ppermute x35, waiting for transfers between devices, exchange(): lax.ppermute(block, 'seq', [(i, i ^ mask) for i in range(lax.axis_size('s...  82.1 us
    ppermute x35, starting transfers between devices, exchange(): lax.ppermute(block, 'seq', [(i, i ^ mask) for i in range(lax.axis_size('s...  57.6 us
    pallas_call x2, Pallas kernels, middle_call(): call(functools.partial(middle_body, peers, side // peers, with_grad), 'mi...  16.3 us
    pallas_call x1, Pallas kernels, spread_gated_call(): call(functools.partial(spread_gated_body, peers), 'spread_gated', (channe...  10 us
    pallas_call x7, Pallas kernels, spread_peer_call(): call(spread_peer_body, 'spread_peer', (channels // width,), [whole((half,...  9.18 us
    pallas_call x1, Pallas kernels, forward_call(): call(functools.partial(forward_body, peers), 'forward_rows', (channels //...  9.15 us
    ppermute x2, starting transfers between devices, shifted(): lax.ppermute(block, 'seq', [(i - distance, i) for i in devices if i - dis...  7.86 us
    unnamed x62, local copies, waits for them, and re-layouts  5.27 us
  transfers between devices with their start and end apart: 44, of which 16 were waited for; matrix products, arithmetic and copies ran while one was open for 0% of the time, Pallas kernels for 24%

profile of v5, /device:TPU:14, one launch (start us, length us, event | category | flops | bytes accessed | tf_op | source)
XLA Modules:
  0.0 209.9 jit_solution(14308204851149981328)
XLA Ops:
  1.6 2.7 %collective-permute-start = (bf16[64,1024]{1,0:T(8,128)(2,1)S(1)}, bf16[64,1024]{1,0:T(8,128)(2,1)S(1)}, u32[]{:S(2)}, u32[]{:S(2)}) collective-permute-start(bf16[64,1024]{1,0:T(8,128)(2,1)S(1)} %constant_dynamic-slice_fusion), channel_id=1, source_target_pairs={{0,8},{2,10},{4,12},{6,14},{8,0},{10,2},{12,4},{14,6},{1,9},{3,11}... | collective-permute-start | bytes 393224 | tf_op jit(solution)/shard_map/ppermute | solution.py:16
  29.5 4.8 %collective-permute-start.14 = (bf16[2,1024]{1,0:T(2,128)(2,1)S(1)}, bf16[2,1024]{1,0:T(2,128)(2,1)S(1)}, u32[]{:S(2)}, u32[]{:S(2)}) collective-permute-start(bf16[2,1024]{1,0:T(2,128)(2,1)S(1)} %slice_bitcast_fusion), channel_id=1, source_target_pairs={{0,2},{2,4},{4,6},{6,8},{8,10},{10,12},{12,14},{1,3},{3,5},{5,7},{... | collective-permute-start | bytes 12296 | tf_op jit(solution)/shard_map/ppermute | solution.py:21
  39.2 3.7 %collective-permute-start.18 = (bf16[128,1024]{1,0:T(8,128)(2,1)}, bf16[128,1024]{1,0:T(8,128)(2,1)}, u32[]{:S(2)}, u32[]{:S(2)}) collective-permute-start(bf16[128,1024]{1,0:T(8,128)(2,1)} %get-tuple-element.108), channel_id=1, source_target_pairs={{0,6},{2,4},{4,2},{6,0},{8,14},{10,12},{12,10},{14,8},{1,7},{3,5},... | collective-permute-start | bytes 786440 | tf_op jit(solution)/shard_map/ppermute | solution.py:16
  42.9 10.0 %spread_gated.1 = (bf16[128,1024]{1,0:T(8,128)(2,1)}, bf16[128,1024]{1,0:T(8,128)(2,1)}, bf16[128,1024]{1,0:T(8,128)(2,1)}, bf16[128,1024]{1,0:T(8,128)(2,1)}, b...) custom-call(bf16[1024,1024]{1,0:T(8,128)(2,1)S(1)} %bitcast.16, ...), custom_call_target="tpu_custom_call" | custom-call | flops 2147483648 | bytes 8388608 | tf_op jit(solution)/shard_map/spread_gated/pallas_call | solution.py:135
  57.1 9.2 %collective-permute-done.20.refs_6_.refs_14_ = bf16[128,1024]{1,0:T(8,128)(2,1)} collective-permute-done((bf16[128,1024]{1,0:T(8,128)(2,1)}, bf16[128,1024]{1,0:T(8,128)(2,1)}, u32[]{:S(2)}, u32[]{:S(2)}) %collective-permute-start.20) | collective-permute-done | bytes 262176 | tf_op jit(solution)/shard_map/ppermute | solution.py:16
  66.3 5.0 %collective-permute-start.22 = (bf16[128,1024]{1,0:T(8,128)(2,1)}, bf16[128,1024]{1,0:T(8,128)(2,1)S(1)}, u32[]{:S(2)}, u32[]{:S(2)}) collective-permute-start(bf16[128,1024]{1,0:T(8,128)(2,1)} %get-tuple-element.117), channel_id=1, source_target_pairs={{0,10},{2,8},{4,14},{6,12},{8,2},{10,0},{12,6},{14,4},{1,11},{3,9}... | collective-permute-start | bytes 786440 | tf_op jit(solution)/shard_map/ppermute | solution.py:16
  73.2 14.2 %collective-permute-done.21.refs_7_.refs_15_ = bf16[128,1024]{1,0:T(8,128)(2,1)} collective-permute-done((bf16[128,1024]{1,0:T(8,128)(2,1)}, bf16[128,1024]{1,0:T(8,128)(2,1)}, u32[]{:S(2)}, u32[]{:S(2)}) %collective-permute-start.21) | collective-permute-done | bytes 262176 | tf_op jit(solution)/shard_map/ppermute | solution.py:16
  87.5 7.8 %middle.1 = (bf16[128,1024]{1,0:T(8,128)(2,1)}, bf16[128,1024]{1,0:T(8,128)(2,1)}, bf16[128,1024]{1,0:T(8,128)(2,1)}, bf16[128,1024]{1,0:T(8,128)(2,1)}, bf16[12...) custom-call(s32[1]{0:T(128)} %bitcast.4.place, ...), custom_call_target="tpu_custom_call" | custom-call | flops 2684354560 | bytes 8388608 | tf_op jit(solution)/shard_map/middle/pallas_call | solution.py:206
  95.4 3.9 %collective-permute-done.28.refs_4_ = bf16[128,1024]{1,0:T(8,128)(2,1)S(1)} collective-permute-done((bf16[128,1024]{1,0:T(8,128)(2,1)}, bf16[128,1024]{1,0:T(8,128)(2,1)S(1)}, u32[]{:S(2)}, u32[]{:S(2)}) %collective-permute-start.28) | collective-permute-done | bytes 262176 | tf_op jit(solution)/shard_map/ppermute | solution.py:16
  99.3 4.1 %collective-permute-start.29 = (bf16[128,1024]{1,0:T(8,128)(2,1)S(1)}, bf16[128,1024]{1,0:T(8,128)(2,1)S(1)}, u32[]{:S(2)}, u32[]{:S(2)}) collective-permute-start(bf16[128,1024]{1,0:T(8,128)(2,1)S(1)} %copy-done.25), channel_id=1, source_target_pairs={{0,6},{2,4},{4,2},{6,0},{8,14},{10,12},{12,10},{14,8},{1,7},{3,5},... | collective-permute-start | bytes 786440 | tf_op jit(solution)/shard_map/ppermute | solution.py:16
  109.7 18.3 %collective-permute-done.26.refs_6_ = bf16[128,1024]{1,0:T(8,128)(2,1)S(1)} collective-permute-done((bf16[128,1024]{1,0:T(8,128)(2,1)S(1)}, bf16[128,1024]{1,0:T(8,128)(2,1)S(1)}, u32[]{:S(2)}, u32[]{:S(2)}) %collective-permute-start.26) | collective-permute-done | bytes 262176 | tf_op jit(solution)/shard_map/ppermute | solution.py:16
  130.5 3.3 %collective-permute-start.30 = (bf16[128,1024]{1,0:T(8,128)(2,1)}, bf16[128,1024]{1,0:T(8,128)(2,1)S(1)}, u32[]{:S(2)}, u32[]{:S(2)}) collective-permute-start(bf16[128,1024]{1,0:T(8,128)(2,1)} %get-tuple-element.132), channel_id=1, source_target_pairs={{0,4},{2,6},{4,0},{6,2},{8,12},{10,14},{12,8},{14,10},{1,5},{3,7},... | collective-permute-start | bytes 786440 | tf_op jit(solution)/shard_map/ppermute | solution.py:16
  133.8 4.1 %collective-permute-done.23.refs_1_ = bf16[128,1024]{1,0:T(8,128)(2,1)S(1)} collective-permute-done((bf16[128,1024]{1,0:T(8,128)(2,1)}, bf16[128,1024]{1,0:T(8,128)(2,1)S(1)}, u32[]{:S(2)}, u32[]{:S(2)}) %collective-permute-start.23) | collective-permute-done | bytes 262176 | tf_op jit(solution)/shard_map/ppermute | solution.py:16
  137.9 4.8 %collective-permute-start.34 = (bf16[128,1024]{1,0:T(8,128)(2,1)}, bf16[128,1024]{1,0:T(8,128)(2,1)S(1)}, u32[]{:S(2)}, u32[]{:S(2)}) collective-permute-start(bf16[128,1024]{1,0:T(8,128)(2,1)} %get-tuple-element.140), channel_id=1, source_target_pairs={{0,6},{2,4},{4,2},{6,0},{8,14},{10,12},{12,10},{14,8},{1,7},{3,5},... | collective-permute-start | bytes 786440 | tf_op jit(solution)/shard_map/ppermute | solution.py:16
  143.2 8.4 %middle_grad.1 = (bf16[8,128,1024]{2,1,0:T(8,128)(2,1)}, bf16[128,1024]{1,0:T(8,128)(2,1)}, bf16[128,1024]{1,0:T(8,128)(2,1)}, bf16[128,1024]{1,0:T(8,128)(2,1)}...) custom-call(s32[1]{0:T(128)} %bitcast.4.place, ...), custom_call_target="tpu_custom_call" | custom-call | flops 3758096384 | bytes 12582912 | tf_op jit(solution)/shard_map/middle_grad/pallas_call | solution.py:206
  151.7 4.6 %collective-permute-done.27.refs_3_ = bf16[128,1024]{1,0:T(8,128)(2,1)S(1)} collective-permute-done((bf16[128,1024]{1,0:T(8,128)(2,1)}, bf16[128,1024]{1,0:T(8,128)(2,1)S(1)}, u32[]{:S(2)}, u32[]{:S(2)}) %collective-permute-start.27) | collective-permute-done | bytes 262176 | tf_op jit(solution)/shard_map/ppermute | solution.py:16
  156.2 3.3 %collective-permute-start.36 = (bf16[128,1024]{1,0:T(8,128)(2,1)}, bf16[128,1024]{1,0:T(8,128)(2,1)S(1)}, u32[]{:S(2)}, u32[]{:S(2)}) collective-permute-start(bf16[128,1024]{1,0:T(8,128)(2,1)} %get-tuple-element.148), channel_id=1, source_target_pairs={{0,8},{2,10},{4,12},{6,14},{8,0},{10,2},{12,4},{14,6},{1,9},{3,11}... | collective-permute-start | bytes 786440 | tf_op jit(solution)/shard_map/ppermute | solution.py:16
  162.4 3.2 %collective-permute-start.39 = (bf16[128,1024]{1,0:T(8,128)(2,1)S(1)}, bf16[128,1024]{1,0:T(8,128)(2,1)S(1)}, u32[]{:S(2)}, u32[]{:S(2)}) collective-permute-start(bf16[128,1024]{1,0:T(8,128)(2,1)S(1)} %copy-done.27), channel_id=1, source_target_pairs={{0,4},{2,6},{4,0},{6,2},{8,12},{10,14},{12,8},{14,10},{1,5},{3,7},... | collective-permute-start | bytes 786440 | tf_op jit(solution)/shard_map/ppermute | solution.py:16
  165.6 11.6 %collective-permute-done.35.refs_7_ = bf16[128,1024]{1,0:T(8,128)(2,1)S(1)} collective-permute-done((bf16[128,1024]{1,0:T(8,128)(2,1)}, bf16[128,1024]{1,0:T(8,128)(2,1)S(1)}, u32[]{:S(2)}, u32[]{:S(2)}) %collective-permute-start.35) | collective-permute-done | bytes 262176 | tf_op jit(solution)/shard_map/ppermute | solution.py:16
  177.3 9.1 %forward_rows.1 = (bf16[1024,1024]{1,0:T(8,128)(2,1)}, f32[1024,1024]{1,0:T(8,128)}, f32[2,1024]{1,0:T(2,128)S(1)}) custom-call(bf16[1024,1024]{1,0:T(8,128)(2,1)S(1)} %turn.1.turned, f32[3,1024]{1,0:T(4,128)S(1)} %copy-done.12, bf16[1024,1024]{1,0:T(8,128)(2,1)} %bitcast.8, bf16[2,1024]{1,0:T(2,128)(2,1)S(1)} %collective-permute-done.14.halo, ...), custom_call_target="tpu_custom_call" | custom-call | flops 2147483648 | bytes 14680064 | tf_op jit(solution)/shard_map/forward_rows/pallas_call | solution.py:291
  189.1 3.0 %collective-permute-done.38.refs_3_ = bf16[128,1024]{1,0:T(8,128)(2,1)S(1)} collective-permute-done((bf16[128,1024]{1,0:T(8,128)(2,1)S(1)}, bf16[128,1024]{1,0:T(8,128)(2,1)S(1)}, u32[]{:S(2)}, u32[]{:S(2)}) %collective-permute-start.38) | collective-permute-done | bytes 262176 | tf_op jit(solution)/shard_map/ppermute | solution.py:16
  192.1 3.1 %collective-permute-start.41 = (f32[2,1024]{1,0:T(2,128)S(1)}, f32[2,1024]{1,0:T(2,128)S(1)}, u32[]{:S(2)}, u32[]{:S(2)}) collective-permute-start(f32[2,1024]{1,0:T(2,128)S(1)} %get-tuple-element.157), channel_id=1, source_target_pairs={{2,0},{4,2},{6,4},{8,6},{10,8},{12,10},{14,12},{3,1},{5,3},{7,5},{... | collective-permute-start | bytes 24584 | tf_op jit(solution)/shard_map/ppermute | solution.py:21
  195.2 6.0 %collective-permute-done.40.refs_5_ = bf16[128,1024]{1,0:T(8,128)(2,1)S(1)} collective-permute-done((bf16[128,1024]{1,0:T(8,128)(2,1)S(1)}, bf16[128,1024]{1,0:T(8,128)(2,1)S(1)}, u32[]{:S(2)}, u32[]{:S(2)}) %collective-permute-start.40) | collective-permute-done | bytes 262176 | tf_op jit(solution)/shard_map/ppermute | solution.py:16
  205.2 2.7 %collective-permute-done.41.tail = f32[2,1024]{1,0:T(2,128)S(1)} collective-permute-done((f32[2,1024]{1,0:T(2,128)S(1)}, f32[2,1024]{1,0:T(2,128)S(1)}, u32[]{:S(2)}, u32[]{:S(2)}) %collective-permute-start.41) | collective-permute-done | bytes 8224 | tf_op jit(solution)/shard_map/ppermute | solution.py:21
  (144 shorter events, 58.0 us)
Async XLA Ops:
  24.1 28.9 %collective-permute-start.15 = (bf16[128,1024]{1,0:T(8,128)(2,1)S(1)}, bf16[128,1024]{1,0:T(8,128)(2,1)S(1)}, u32[]{:S(2)}, u32[]{:S(2)}) collective-permute-start(bf16[128,1024]{1,0:T(8,128)(2,1)S(1)} %get-tuple-element.102), channel_id=1, source_target_pairs={{0,2},{2,0},{4,6},{6,4},{8,10},{10,8},{12,14},{14,12},{1,3},{3,1},... | collective-permute-start | bytes 786440 | tf_op jit(solution)/shard_map/ppermute | solution.py:16
  27.3 26.9 %collective-permute-start.16 = (bf16[128,1024]{1,0:T(8,128)(2,1)S(1)}, bf16[128,1024]{1,0:T(8,128)(2,1)S(1)}, u32[]{:S(2)}, u32[]{:S(2)}) collective-permute-start(bf16[128,1024]{1,0:T(8,128)(2,1)S(1)} %get-tuple-element.104), channel_id=1, source_target_pairs={{0,4},{2,6},{4,0},{6,2},{8,12},{10,14},{12,8},{14,10},{1,5},{3,7},... | collective-permute-start | bytes 786440 | tf_op jit(solution)/shard_map/ppermute | solution.py:16
  35.8 30.4 %collective-permute-start.19 = (bf16[128,1024]{1,0:T(8,128)(2,1)}, bf16[128,1024]{1,0:T(8,128)(2,1)}, u32[]{:S(2)}, u32[]{:S(2)}) collective-permute-start(bf16[128,1024]{1,0:T(8,128)(2,1)} %get-tuple-element.110), channel_id=1, source_target_pairs={{0,10},{2,8},{4,14},{6,12},{8,2},{10,0},{12,6},{14,4},{1,11},{3,9}... | collective-permute-start | bytes 786440 | tf_op jit(solution)/shard_map/ppermute | solution.py:16
  38.0 28.3 %collective-permute-start.20 = (bf16[128,1024]{1,0:T(8,128)(2,1)}, bf16[128,1024]{1,0:T(8,128)(2,1)}, u32[]{:S(2)}, u32[]{:S(2)}) collective-permute-start(bf16[128,1024]{1,0:T(8,128)(2,1)} %get-tuple-element.112), channel_id=1, source_target_pairs={{0,12},{2,14},{4,8},{6,10},{8,4},{10,6},{12,0},{14,2},{1,13},{3,15... | collective-permute-start | bytes 786440 | tf_op jit(solution)/shard_map/ppermute | solution.py:16
  39.2 32.0 %collective-permute-start.18 = (bf16[128,1024]{1,0:T(8,128)(2,1)}, bf16[128,1024]{1,0:T(8,128)(2,1)}, u32[]{:S(2)}, u32[]{:S(2)}) collective-permute-start(bf16[128,1024]{1,0:T(8,128)(2,1)} %get-tuple-element.108), channel_id=1, source_target_pairs={{0,6},{2,4},{4,2},{6,0},{8,14},{10,12},{12,10},{14,8},{1,7},{3,5},... | collective-permute-start | bytes 786440 | tf_op jit(solution)/shard_map/ppermute | solution.py:16
  53.7 33.7 %collective-permute-start.21 = (bf16[128,1024]{1,0:T(8,128)(2,1)}, bf16[128,1024]{1,0:T(8,128)(2,1)}, u32[]{:S(2)}, u32[]{:S(2)}) collective-permute-start(bf16[128,1024]{1,0:T(8,128)(2,1)} %get-tuple-element.113), channel_id=1, source_target_pairs={{0,14},{2,12},{4,10},{6,8},{8,6},{10,4},{12,2},{14,0},{1,15},{3,13... | collective-permute-start | bytes 786440 | tf_op jit(solution)/shard_map/ppermute | solution.py:16
  54.9 32.4 %collective-permute-start.31 = (bf16[128,1024]{1,0:T(8,128)(2,1)}, bf16[128,1024]{1,0:T(8,128)(2,1)}, u32[]{:S(2)}, u32[]{:S(2)}) collective-permute-start(bf16[128,1024]{1,0:T(8,128)(2,1)} %get-tuple-element.136), channel_id=1, source_target_pairs={{0,2},{2,0},{4,6},{6,4},{8,10},{10,8},{12,14},{14,12},{1,3},{3,1},... | collective-permute-start | bytes 786440 | tf_op jit(solution)/shard_map/ppermute | solution.py:16
  66.3 33.1 %collective-permute-start.28 = (bf16[128,1024]{1,0:T(8,128)(2,1)}, bf16[128,1024]{1,0:T(8,128)(2,1)S(1)}, u32[]{:S(2)}, u32[]{:S(2)}) collective-permute-start(bf16[128,1024]{1,0:T(8,128)(2,1)} %get-tuple-element.130), channel_id=1, source_target_pairs={{0,8},{2,10},{4,12},{6,14},{8,0},{10,2},{12,4},{14,6},{1,9},{3,11}... | collective-permute-start | bytes 786440 | tf_op jit(solution)/shard_map/ppermute | solution.py:16
  66.3 38.7 %collective-permute-start.22 = (bf16[128,1024]{1,0:T(8,128)(2,1)}, bf16[128,1024]{1,0:T(8,128)(2,1)S(1)}, u32[]{:S(2)}, u32[]{:S(2)}) collective-permute-start(bf16[128,1024]{1,0:T(8,128)(2,1)} %get-tuple-element.117), channel_id=1, source_target_pairs={{0,10},{2,8},{4,14},{6,12},{8,2},{10,0},{12,6},{14,4},{1,11},{3,9}... | collective-permute-start | bytes 786440 | tf_op jit(solution)/shard_map/ppermute | solution.py:16
  71.2 35.9 %collective-permute-start.24 = (bf16[128,1024]{1,0:T(8,128)(2,1)}, bf16[128,1024]{1,0:T(8,128)(2,1)S(1)}, u32[]{:S(2)}, u32[]{:S(2)}) collective-permute-start(bf16[128,1024]{1,0:T(8,128)(2,1)} %get-tuple-element.121), channel_id=1, source_target_pairs={{0,4},{2,6},{4,0},{6,2},{8,12},{10,14},{12,8},{14,10},{1,5},{3,7},... | collective-permute-start | bytes 786440 | tf_op jit(solution)/shard_map/ppermute | solution.py:16
  87.3 40.7 %collective-permute-start.32 = (bf16[128,1024]{1,0:T(8,128)(2,1)S(1)}, bf16[128,1024]{1,0:T(8,128)(2,1)S(1)}, u32[]{:S(2)}, u32[]{:S(2)}) collective-permute-start(bf16[128,1024]{1,0:T(8,128)(2,1)S(1)} %copy-done.28), channel_id=1, source_target_pairs={{0,14},{2,12},{4,10},{6,8},{8,6},{10,4},{12,2},{14,0},{1,15},{3,13... | collective-permute-start | bytes 786440 | tf_op jit(solution)/shard_map/ppermute | solution.py:16
  87.5 40.6 %collective-permute-start.26 = (bf16[128,1024]{1,0:T(8,128)(2,1)S(1)}, bf16[128,1024]{1,0:T(8,128)(2,1)S(1)}, u32[]{:S(2)}, u32[]{:S(2)}) collective-permute-start(bf16[128,1024]{1,0:T(8,128)(2,1)S(1)} %copy-done.29), channel_id=1, source_target_pairs={{0,12},{2,14},{4,8},{6,10},{8,4},{10,6},{12,0},{14,2},{1,13},{3,15... | collective-permute-start | bytes 786440 | tf_op jit(solution)/shard_map/ppermute | solution.py:16
  99.3 31.2 %collective-permute-start.29 = (bf16[128,1024]{1,0:T(8,128)(2,1)S(1)}, bf16[128,1024]{1,0:T(8,128)(2,1)S(1)}, u32[]{:S(2)}, u32[]{:S(2)}) collective-permute-start(bf16[128,1024]{1,0:T(8,128)(2,1)S(1)} %copy-done.25), channel_id=1, source_target_pairs={{0,6},{2,4},{4,2},{6,0},{8,14},{10,12},{12,10},{14,8},{1,7},{3,5},... | collective-permute-start | bytes 786440 | tf_op jit(solution)/shard_map/ppermute | solution.py:16
  105.0 33.0 %collective-permute-start.23 = (bf16[128,1024]{1,0:T(8,128)(2,1)}, bf16[128,1024]{1,0:T(8,128)(2,1)S(1)}, u32[]{:S(2)}, u32[]{:S(2)}) collective-permute-start(bf16[128,1024]{1,0:T(8,128)(2,1)} %get-tuple-element.118), channel_id=1, source_target_pairs={{0,8},{2,10},{4,12},{6,14},{8,0},{10,2},{12,4},{14,6},{1,9},{3,11}... | collective-permute-start | bytes 786440 | tf_op jit(solution)/shard_map/ppermute | solution.py:16
  107.1 35.6 %collective-permute-start.25 = (bf16[128,1024]{1,0:T(8,128)(2,1)}, bf16[128,1024]{1,0:T(8,128)(2,1)S(1)}, u32[]{:S(2)}, u32[]{:S(2)}) collective-permute-start(bf16[128,1024]{1,0:T(8,128)(2,1)} %get-tuple-element.122), channel_id=1, source_target_pairs={{0,2},{2,0},{4,6},{6,4},{8,10},{10,8},{12,14},{14,12},{1,3},{3,1},... | collective-permute-start | bytes 786440 | tf_op jit(solution)/shard_map/ppermute | solution.py:16
  128.0 34.2 %collective-permute-start.33 = (bf16[128,1024]{1,0:T(8,128)(2,1)}, bf16[128,1024]{1,0:T(8,128)(2,1)S(1)}, u32[]{:S(2)}, u32[]{:S(2)}) collective-permute-start(bf16[128,1024]{1,0:T(8,128)(2,1)} %get-tuple-element.138), channel_id=1, source_target_pairs={{0,12},{2,14},{4,8},{6,10},{8,4},{10,6},{12,0},{14,2},{1,13},{3,15... | collective-permute-start | bytes 786440 | tf_op jit(solution)/shard_map/ppermute | solution.py:16
  130.5 25.7 %collective-permute-start.27 = (bf16[128,1024]{1,0:T(8,128)(2,1)}, bf16[128,1024]{1,0:T(8,128)(2,1)S(1)}, u32[]{:S(2)}, u32[]{:S(2)}) collective-permute-start(bf16[128,1024]{1,0:T(8,128)(2,1)} %get-tuple-element.126), channel_id=1, source_target_pairs={{0,10},{2,8},{4,14},{6,12},{8,2},{10,0},{12,6},{14,4},{1,11},{3,9}... | collective-permute-start | bytes 786440 | tf_op jit(solution)/shard_map/ppermute | solution.py:16
  130.5 29.0 %collective-permute-start.30 = (bf16[128,1024]{1,0:T(8,128)(2,1)}, bf16[128,1024]{1,0:T(8,128)(2,1)S(1)}, u32[]{:S(2)}, u32[]{:S(2)}) collective-permute-start(bf16[128,1024]{1,0:T(8,128)(2,1)} %get-tuple-element.132), channel_id=1, source_target_pairs={{0,4},{2,6},{4,0},{6,2},{8,12},{10,14},{12,8},{14,10},{1,5},{3,7},... | collective-permute-start | bytes 786440 | tf_op jit(solution)/shard_map/ppermute | solution.py:16
  137.9 24.4 %collective-permute-start.34 = (bf16[128,1024]{1,0:T(8,128)(2,1)}, bf16[128,1024]{1,0:T(8,128)(2,1)S(1)}, u32[]{:S(2)}, u32[]{:S(2)}) collective-permute-start(bf16[128,1024]{1,0:T(8,128)(2,1)} %get-tuple-element.140), channel_id=1, source_target_pairs={{0,6},{2,4},{4,2},{6,0},{8,14},{10,12},{12,10},{14,8},{1,7},{3,5},... | collective-permute-start | bytes 786440 | tf_op jit(solution)/shard_map/ppermute | solution.py:16
  142.8 34.4 %collective-permute-start.35 = (bf16[128,1024]{1,0:T(8,128)(2,1)}, bf16[128,1024]{1,0:T(8,128)(2,1)S(1)}, u32[]{:S(2)}, u32[]{:S(2)}) collective-permute-start(bf16[128,1024]{1,0:T(8,128)(2,1)} %get-tuple-element.142), channel_id=1, source_target_pairs={{0,14},{2,12},{4,10},{6,8},{8,6},{10,4},{12,2},{14,0},{1,15},{3,13... | collective-permute-start | bytes 786440 | tf_op jit(solution)/shard_map/ppermute | solution.py:16
  156.2 30.2 %collective-permute-start.36 = (bf16[128,1024]{1,0:T(8,128)(2,1)}, bf16[128,1024]{1,0:T(8,128)(2,1)S(1)}, u32[]{:S(2)}, u32[]{:S(2)}) collective-permute-start(bf16[128,1024]{1,0:T(8,128)(2,1)} %get-tuple-element.148), channel_id=1, source_target_pairs={{0,8},{2,10},{4,12},{6,14},{8,0},{10,2},{12,4},{14,6},{1,9},{3,11}... | collective-permute-start | bytes 786440 | tf_op jit(solution)/shard_map/ppermute | solution.py:16
  159.6 28.4 %collective-permute-start.37 = (bf16[128,1024]{1,0:T(8,128)(2,1)}, bf16[128,1024]{1,0:T(8,128)(2,1)S(1)}, u32[]{:S(2)}, u32[]{:S(2)}) collective-permute-start(bf16[128,1024]{1,0:T(8,128)(2,1)} %get-tuple-element.150), channel_id=1, source_target_pairs={{0,2},{2,0},{4,6},{6,4},{8,10},{10,8},{12,14},{14,12},{1,3},{3,1},... | collective-permute-start | bytes 786440 | tf_op jit(solution)/shard_map/ppermute | solution.py:16
  162.3 29.8 %collective-permute-start.38 = (bf16[128,1024]{1,0:T(8,128)(2,1)S(1)}, bf16[128,1024]{1,0:T(8,128)(2,1)S(1)}, u32[]{:S(2)}, u32[]{:S(2)}) collective-permute-start(bf16[128,1024]{1,0:T(8,128)(2,1)S(1)} %copy-done.30), channel_id=1, source_target_pairs={{0,10},{2,8},{4,14},{6,12},{8,2},{10,0},{12,6},{14,4},{1,11},{3,9}... | collective-permute-start | bytes 786440 | tf_op jit(solution)/shard_map/ppermute | solution.py:16
  162.4 32.8 %collective-permute-start.39 = (bf16[128,1024]{1,0:T(8,128)(2,1)S(1)}, bf16[128,1024]{1,0:T(8,128)(2,1)S(1)}, u32[]{:S(2)}, u32[]{:S(2)}) collective-permute-start(bf16[128,1024]{1,0:T(8,128)(2,1)S(1)} %copy-done.27), channel_id=1, source_target_pairs={{0,4},{2,6},{4,0},{6,2},{8,12},{10,14},{12,8},{14,10},{1,5},{3,7},... | collective-permute-start | bytes 786440 | tf_op jit(solution)/shard_map/ppermute | solution.py:16
  (51 other events, 731.2 us)
